TPU v7x, 128 devices: a whole 4x4x4 slice. The times are simulated.
128 devices in a mesh: img: 16 (over y, x_hi, core), cls: 8 (over z, x_lo).
Axes of the slice: x: 4 (x_hi: 2, x_lo: 2; x = x_hi * 2 + x_lo), y: 4, z: 4, core: 2. Of those that a mesh axis runs over, the one named last changes fastest.
Arguments:
- images: bfloat16 [128, 9216], P('img'), may hold values from -64 to 64
- references: bfloat16 [512, 9216], P(('img', 'cls')), may hold values from -0.2 to 0.2
- class_logprior: bfloat16 [512], P(('img', 'cls')), may hold values from -3 to 3
- ctf_table: float32 [16, 32], replicated, may hold values from -1 to 1, as said below
- noise_power: float32 [32], replicated, may hold values from 0.5 to 2
- tau_power: float32 [32], replicated, may hold values from 0.5 to 4
- defocus: int32 [128], P('img'), may hold values from 0 to 15
- offsets: int32 [128, 4, 2], P('img'), may hold values from -3 to 3
Outputs:
- new_refs: float32 [512, 9216], P(('img', 'cls'))
- new_weights: float32 [512], P(('img', 'cls'))
- loglik: float32 [128], P('img')
Inputs may be any that keep to these rules, and one draw needn't show every extreme that they name: `ctf_table`: each row is a contrast transfer curve that oscillates over the cycles.
All inputs are finite; a program needn't handle non-finite values.
Results may differ from a plain program's by a relative error of at most 0.0068.
Values may be sent and summed in bfloat16 or wider, within the bound.
No kernel may reach another device: no remote copies, remote signals or barrier semaphores. Data moves between devices by JAX's collectives and lax.ppermute only.
A program may use at most 64 MiB of HBM per device.

v0:
```python
import math

import jax
import jax.numpy as jnp
from jax import lax
from jax.sharding import PartitionSpec as P

TRANS = 4
CYCLES = 32
ANG = 144
ROT = 36
NDEF = 16


offset_sigma = 2.0
turn_group = 4


def side_by_side(arrays, axis, dim, along):
    widths = [math.prod(a.shape[along:]) for a in arrays]
    both = jnp.concatenate(
        [a.reshape(*a.shape[:along], w) for a, w in zip(arrays, widths)], axis=along
    )
    result = lax.all_gather(both, axis, axis=dim, tiled=True)
    tiles = jnp.split(result, [sum(widths[:k]) for k in range(1, len(widths))], axis=along)
    return tuple(
        (b.reshape(*result.shape[:along], *a.shape[along:]) for a, b in zip(arrays, tiles))
    )


def from_everyone(shard, axis):
    copies = jnp.broadcast_to(shard, (lax.axis_size(axis), *shard.shape))
    return lax.all_to_all(copies, axis, split_axis=0, concat_axis=0, tiled=True)


def gathered_once(shard, axis):
    leaves = jax.tree.leaves(shard)
    order = sorted(range(len(leaves)), key=lambda k: -leaves[k].size)
    width = (1, *leaves[order[0]].shape)[-1]
    lines = [
        jnp.pad(leaves[k].reshape(-1), (0, -leaves[k].size % width)).reshape(-1, width)
        for k in order
    ]
    both, at, found = (from_everyone(jnp.concatenate(lines), axis), 0, {})
    for k, line in zip(order, lines):
        share = both[:, at : at + len(line)].reshape(len(both), -1)
        found[k] = share[:, : leaves[k].size].reshape(-1, *leaves[k].shape)
        at += len(line)
    numbers = iter(range(len(leaves)))
    return jax.tree.map(lambda _: found[next(numbers)], shard)


def combined_pairwise(pieces, combine):
    while len(jax.tree.leaves(pieces)[0]) > 1:
        pieces = jax.vmap(combine)(
            *(jax.tree.map(lambda part: part[side::2], pieces) for side in (0, 1))
        )
    return jax.tree.map(lambda part: part[0], pieces)


def merged(shard, axis, combine):
    pieces = gathered_once(shard, axis)
    return combined_pairwise(pieces, combine)


def split_up(shard, dim, devices):
    dims = shard.shape
    tiles = shard.reshape(*dims[:dim], devices, dims[dim] // devices, *dims[dim + 1 :])
    return jnp.moveaxis(tiles, dim, 0)


def summed_on_arrival(shard, axis, dim):
    devices = lax.axis_size(axis)
    tiles = lax.all_to_all(split_up(shard, dim, devices), axis, 0, 0, tiled=True)
    return jnp.sum(tiles, axis=0)


def side_by_side_2(arrays, axis, dim, along):
    widths = [math.prod(a.shape[along:]) for a in arrays]
    both = jnp.concatenate(
        [a.reshape(*a.shape[:along], w) for a, w in zip(arrays, widths)], axis=along
    )
    result = summed_on_arrival(both, axis, dim)
    tiles = jnp.split(result, [sum(widths[:k]) for k in range(1, len(widths))], axis=along)
    return tuple(
        (b.reshape(*result.shape[:along], *a.shape[along:]) for a, b in zip(arrays, tiles))
    )


def phase_table(shift_x, shift_y):
    radius = jnp.arange(CYCLES, dtype=jnp.float32) + 1.0
    theta = 2.0 * math.pi * jnp.arange(ANG, dtype=jnp.float32) / ANG
    freq_x = radius[:, None] * jnp.cos(theta)[None, :]
    freq_y = radius[:, None] * jnp.sin(theta)[None, :]
    return (
        -2.0
        * math.pi
        * (shift_x[..., None, None] * freq_x + shift_y[..., None, None] * freq_y)
        / (2.0 * CYCLES)
    )


def combine_pairs(earlier, later):
    peak = jnp.maximum(earlier[0], later[0])
    return (peak, earlier[1] * jnp.exp(earlier[0] - peak) + later[1] * jnp.exp(later[0] - peak))


def turned_rows(source, group_index, stride):
    shaped = source.reshape(source.shape[0], 2, CYCLES, ANG)
    first_turn = group_index * turn_group
    turned = [
        jnp.roll(shaped, -stride * (first_turn + step), axis=-1) for step in range(turn_group)
    ]
    return jnp.stack(turned, axis=1).reshape(source.shape[0] * turn_group, source.shape[1])


def per_device(
    images, references, class_logprior, ctf_table, noise_power, tau_power, defocus, offsets
):
    img_count = images.shape[0]
    rows = img_count * TRANS
    width = images.shape[1]
    stride = ANG // ROT
    owned = references.shape[0]
    classes = owned * lax.axis_size("img")
    groups_count = ROT // turn_group
    pixels = images.astype(jnp.float32).reshape(img_count, 2, CYCLES, ANG)
    shift = offsets.astype(jnp.float32)
    angle = phase_table(shift[..., 0], shift[..., 1])
    cosine = jnp.cos(angle)
    sine = jnp.sin(angle)
    real_part = pixels[:, None, 0] * cosine - pixels[:, None, 1] * sine
    imag_part = pixels[:, None, 0] * sine + pixels[:, None, 1] * cosine
    shifted = jnp.stack([real_part, imag_part], axis=2)
    one_hot = (defocus[:, None] == jnp.arange(NDEF, dtype=jnp.int32)[None, :]).astype(jnp.float32)
    contrast = jnp.dot(one_hot, ctf_table, precision=lax.Precision.HIGHEST)
    weighted = (
        (shifted * (contrast / noise_power[None, :])[:, None, None, :, None])
        .astype(jnp.bfloat16)
        .reshape(rows, width)
    )
    inserted = (
        (shifted * contrast[:, None, None, :, None]).astype(jnp.bfloat16).reshape(rows, width)
    )
    norm_coef = jnp.repeat(contrast * contrast / (2.0 * noise_power[None, :]), TRANS, axis=0)
    squared_rows = jnp.repeat(contrast * contrast, TRANS, axis=0)
    trans_prior = -(shift[..., 0] * shift[..., 0] + shift[..., 1] * shift[..., 1]) / (
        2.0 * offset_sigma * offset_sigma
    )
    group_refs, group_prior = side_by_side((references, class_logprior), "img", 0, 1)
    power = jnp.sum(
        jnp.square(group_refs.astype(jnp.float32).reshape(classes, 2, CYCLES, ANG)), axis=(1, 3)
    )
    penalty = jnp.dot(norm_coef, power.T, precision=lax.Precision.HIGHEST)
    base_scores = (
        group_prior.astype(jnp.float32)[None, :] - penalty + trans_prior.reshape(rows)[:, None]
    )

    def score_group(group_index, current):
        rotated = turned_rows(weighted, group_index, stride)
        cross = lax.dot_general(
            rotated, group_refs, (((1,), (1,)), ((), ())), preferred_element_type=jnp.float32
        )
        values = cross.reshape(rows, turn_group, classes) + base_scores[:, None, :]
        return lax.dynamic_update_slice_in_dim(current, values, group_index * turn_group, 1)

    logp = lax.fori_loop(0, groups_count, score_group, jnp.zeros((rows, ROT, classes), jnp.float32))
    per_image = logp.reshape(img_count, TRANS * ROT * classes)
    local_peak = jnp.max(per_image, axis=1)
    local_total = jnp.sum(jnp.exp(per_image - local_peak[:, None]), axis=1)
    peak, total = merged((local_peak, local_total), "cls", combine_pairs)
    loglik = peak + jnp.log(total)
    posterior = (
        (jnp.exp(per_image - peak[:, None]) / total[:, None])
        .astype(jnp.bfloat16)
        .reshape(rows, ROT, classes)
    )

    def insert_group(group_index, numer):
        rotated = turned_rows(inserted, group_index, stride)
        section = lax.dynamic_slice_in_dim(
            posterior, group_index * turn_group, turn_group, 1
        ).reshape(rows * turn_group, classes)
        return numer + lax.dot_general(
            section, rotated, (((0,), (0,)), ((), ())), preferred_element_type=jnp.float32
        )

    numer = lax.fori_loop(0, groups_count, insert_group, jnp.zeros((classes, width), jnp.float32))
    post_sum = jnp.sum(posterior.astype(jnp.float32), axis=1)
    denom = lax.dot_general(
        post_sum, squared_rows, (((0,), (0,)), ((), ())), precision=lax.Precision.HIGHEST
    )
    weight = jnp.sum(post_sum, axis=0)
    numer_own, denom_own, weight_own = side_by_side_2((numer, denom, weight), "img", 0, 1)
    fresh = numer_own.reshape(owned, 2, CYCLES, ANG) / (
        denom_own[:, None, :, None] + 1.0 / tau_power[None, None, :, None]
    )
    return (fresh.reshape(owned, width), weight_own / (img_count * lax.axis_size("img")), loglik)


def solution(mesh):
    return jax.shard_map(
        per_device,
        mesh=mesh,
        in_specs=(
            P("img", None),
            P(("img", "cls"), None),
            P(("img", "cls")),
            P(),
            P(),
            P(),
            P("img"),
            P("img", None, None),
        ),
        out_specs=(P(("img", "cls"), None), P(("img", "cls")), P("img")),
        check_vma=False,
    )
```

profile of v0, /device:TPU:0, one launch (start us, length us, event | category | flops | bytes accessed | tf_op | source)
XLA Modules:
  0.0 539.9 jit_solution(1395684170671683542)
XLA Ops:
  13.6 4.1 multiply_subtract_fusion
  19.2 39.4 %all-gather.3.cloned.1.call-done = bf16[16,4,9217]{2,1,0:T(4,128)(2,1)} async-done(((bf16[1,4,9217]{2,1,0:T(4,128)(2,1)}), bf16[16,4,9217]{2,1,0:T(4,128)(2,1)}) %all-gather.3.cloned.1.call-update) | async-done | bytes 1179792 | tf_op jit(solution)/shard_map/all_gather | solution.py:24
  63.1 5.6 %square.7 = f32[64,2,32,144]{3,2,1,0:T(8,128)} reshape(f32[64,9216]{1,0:T(8,128)} %convert_multiply_fusion) | data formatting | bytes 4718592 | tf_op jit(solution)/shard_map/square | solution.py:152
  72.3 217.8 %while.31 = (s32[]{:T(128)}, f32[32,36,64]{2,0,1:T(8,128)}, bf16[8,4,2,32,144]{4,3,2,1,0:T(8,128)(2,1)S(1)}, bf16[64,9216]{1,0:T(8,128)(2,1)}, f32[32,64]{1,0:T(...) while((s32[]{:T(128)}, f32[32,36,64]{2,0,1:T(8,128)}, ...), condition=%wide.region_2.4_spmd, body=%wide.region_1.3_spmd.sunk | while | flops 159260720 | bytes 20718388 | solution.py:167
  73.3 10.1 %fusion.62 = (bf16[32,2,32,144]{3,2,1,0:T(8,128)(2,1)S(1)}, bf16[32,2,32,144]{3,2,1,0:T(8,128)(2,1)S(1)}, bf16[32,2,32,144]{3,2,1,0:T(8,128)(2,1)S(1)}, bf16[32,2,32,144]{3,2,1,0:T(8,128)(2,1)}) fusion(s32[]{:T(128)S(6)} %select_n.81, bf16[32,2,32,144]{3,2,1,0:T(8,128)(2,1)} %bitcast.88, s32[]{:T(128)S(6)} %select_n.83, s32[]{:T(128)S(6)} %select_n.85, ...), kind=kLoop, calls=%fused_computation.20.clone.1 | loop fusion | flops 4718592 | bytes 2949136 | tf_op jit(solution)/shard_map/while/body/eval_jaxpr/jit(_roll_dynamic)/concatenate | solution.py:112
  83.4 3.3 stack.105
  97.4 10.3 %fusion.62 = (bf16[32,2,32,144]{3,2,1,0:T(8,128)(2,1)S(1)}, bf16[32,2,32,144]{3,2,1,0:T(8,128)(2,1)S(1)}, bf16[32,2,32,144]{3,2,1,0:T(8,128)(2,1)S(1)}, bf16[32,2,32,144]{3,2,1,0:T(8,128)(2,1)}) fusion(s32[]{:T(128)S(6)} %select_n.81, bf16[32,2,32,144]{3,2,1,0:T(8,128)(2,1)} %bitcast.88, s32[]{:T(128)S(6)} %select_n.83, s32[]{:T(128)S(6)} %select_n.85, ...), kind=kLoop, calls=%fused_computation.20.clone.1 | loop fusion | flops 4718592 | bytes 2949136 | tf_op jit(solution)/shard_map/while/body/eval_jaxpr/jit(_roll_dynamic)/concatenate | solution.py:112
  121.7 10.3 %fusion.62 = (bf16[32,2,32,144]{3,2,1,0:T(8,128)(2,1)S(1)}, bf16[32,2,32,144]{3,2,1,0:T(8,128)(2,1)S(1)}, bf16[32,2,32,144]{3,2,1,0:T(8,128)(2,1)S(1)}, bf16[32,2,32,144]{3,2,1,0:T(8,128)(2,1)}) fusion(s32[]{:T(128)S(6)} %select_n.81, bf16[32,2,32,144]{3,2,1,0:T(8,128)(2,1)} %bitcast.88, s32[]{:T(128)S(6)} %select_n.83, s32[]{:T(128)S(6)} %select_n.85, ...), kind=kLoop, calls=%fused_computation.20.clone.1 | loop fusion | flops 4718592 | bytes 2949136 | tf_op jit(solution)/shard_map/while/body/eval_jaxpr/jit(_roll_dynamic)/concatenate | solution.py:112
  146.0 10.3 %fusion.62 = (bf16[32,2,32,144]{3,2,1,0:T(8,128)(2,1)S(1)}, bf16[32,2,32,144]{3,2,1,0:T(8,128)(2,1)S(1)}, bf16[32,2,32,144]{3,2,1,0:T(8,128)(2,1)S(1)}, bf16[32,2,32,144]{3,2,1,0:T(8,128)(2,1)}) fusion(s32[]{:T(128)S(6)} %select_n.81, bf16[32,2,32,144]{3,2,1,0:T(8,128)(2,1)} %bitcast.88, s32[]{:T(128)S(6)} %select_n.83, s32[]{:T(128)S(6)} %select_n.85, ...), kind=kLoop, calls=%fused_computation.20.clone.1 | loop fusion | flops 4718592 | bytes 2949136 | tf_op jit(solution)/shard_map/while/body/eval_jaxpr/jit(_roll_dynamic)/concatenate | solution.py:112
  156.3 3.3 stack.105
  170.3 10.3 %fusion.62 = (bf16[32,2,32,144]{3,2,1,0:T(8,128)(2,1)S(1)}, bf16[32,2,32,144]{3,2,1,0:T(8,128)(2,1)S(1)}, bf16[32,2,32,144]{3,2,1,0:T(8,128)(2,1)S(1)}, bf16[32,2,32,144]{3,2,1,0:T(8,128)(2,1)}) fusion(s32[]{:T(128)S(6)} %select_n.81, bf16[32,2,32,144]{3,2,1,0:T(8,128)(2,1)} %bitcast.88, s32[]{:T(128)S(6)} %select_n.83, s32[]{:T(128)S(6)} %select_n.85, ...), kind=kLoop, calls=%fused_computation.20.clone.1 | loop fusion | flops 4718592 | bytes 2949136 | tf_op jit(solution)/shard_map/while/body/eval_jaxpr/jit(_roll_dynamic)/concatenate | solution.py:112
  180.6 3.3 stack.105
  194.6 10.3 %fusion.62 = (bf16[32,2,32,144]{3,2,1,0:T(8,128)(2,1)S(1)}, bf16[32,2,32,144]{3,2,1,0:T(8,128)(2,1)S(1)}, bf16[32,2,32,144]{3,2,1,0:T(8,128)(2,1)S(1)}, bf16[32,2,32,144]{3,2,1,0:T(8,128)(2,1)}) fusion(s32[]{:T(128)S(6)} %select_n.81, bf16[32,2,32,144]{3,2,1,0:T(8,128)(2,1)} %bitcast.88, s32[]{:T(128)S(6)} %select_n.83, s32[]{:T(128)S(6)} %select_n.85, ...), kind=kLoop, calls=%fused_computation.20.clone.1 | loop fusion | flops 4718592 | bytes 2949136 | tf_op jit(solution)/shard_map/while/body/eval_jaxpr/jit(_roll_dynamic)/concatenate | solution.py:112
  218.9 10.3 %fusion.62 = (bf16[32,2,32,144]{3,2,1,0:T(8,128)(2,1)S(1)}, bf16[32,2,32,144]{3,2,1,0:T(8,128)(2,1)S(1)}, bf16[32,2,32,144]{3,2,1,0:T(8,128)(2,1)S(1)}, bf16[32,2,32,144]{3,2,1,0:T(8,128)(2,1)}) fusion(s32[]{:T(128)S(6)} %select_n.81, bf16[32,2,32,144]{3,2,1,0:T(8,128)(2,1)} %bitcast.88, s32[]{:T(128)S(6)} %select_n.83, s32[]{:T(128)S(6)} %select_n.85, ...), kind=kLoop, calls=%fused_computation.20.clone.1 | loop fusion | flops 4718592 | bytes 2949136 | tf_op jit(solution)/shard_map/while/body/eval_jaxpr/jit(_roll_dynamic)/concatenate | solution.py:112
  243.2 10.3 %fusion.62 = (bf16[32,2,32,144]{3,2,1,0:T(8,128)(2,1)S(1)}, bf16[32,2,32,144]{3,2,1,0:T(8,128)(2,1)S(1)}, bf16[32,2,32,144]{3,2,1,0:T(8,128)(2,1)S(1)}, bf16[32,2,32,144]{3,2,1,0:T(8,128)(2,1)}) fusion(s32[]{:T(128)S(6)} %select_n.81, bf16[32,2,32,144]{3,2,1,0:T(8,128)(2,1)} %bitcast.88, s32[]{:T(128)S(6)} %select_n.83, s32[]{:T(128)S(6)} %select_n.85, ...), kind=kLoop, calls=%fused_computation.20.clone.1 | loop fusion | flops 4718592 | bytes 2949136 | tf_op jit(solution)/shard_map/while/body/eval_jaxpr/jit(_roll_dynamic)/concatenate | solution.py:112
  267.5 9.6 %fusion.62 = (bf16[32,2,32,144]{3,2,1,0:T(8,128)(2,1)S(1)}, bf16[32,2,32,144]{3,2,1,0:T(8,128)(2,1)S(1)}, bf16[32,2,32,144]{3,2,1,0:T(8,128)(2,1)S(1)}, bf16[32,2,32,144]{3,2,1,0:T(8,128)(2,1)}) fusion(s32[]{:T(128)S(6)} %select_n.81, bf16[32,2,32,144]{3,2,1,0:T(8,128)(2,1)} %bitcast.88, s32[]{:T(128)S(6)} %select_n.83, s32[]{:T(128)S(6)} %select_n.85, ...), kind=kLoop, calls=%fused_computation.20.clone.1 | loop fusion | flops 4718592 | bytes 2949136 | tf_op jit(solution)/shard_map/while/body/eval_jaxpr/jit(_roll_dynamic)/concatenate | solution.py:112
  294.0 4.4 all-to-all-start
  298.4 6.2 %all-to-all-done = f32[8,2,8]{2,1,0:T(2,128)S(1)} async-done(((f32[8,2,8]{2,1,0:T(2,128)}), f32[8,2,8]{2,1,0:T(2,128)S(1)}, u32[]{:S(2)}, u32[]{:S(2)}) %all-to-all-start) | async-done | bytes 544 | tf_op jit(solution)/shard_map/all_to_all | solution.py:33
  308.1 178.9 %while.32 = (s32[]{:T(128)}, f32[64,9216]{1,0:T(8,128)}, bf16[32,36,64]{2,1,0:T(8,128)(2,1)}, bf16[8,4,2,32,144]{4,3,2,1,0:T(8,128)(2,1)S(1)}, s32[]{:T(128)}, /...) while((s32[]{:T(128)}, f32[64,9216]{1,0:T(8,128)}, ...), condition=%wide.region_8.10_spmd.clone, body=%wide.region_7.9_spmd.clone.sunk | while | flops 160432176 | bytes 19514052 | solution.py:188
  308.1 5.7 %fusion.66 = (bf16[32,1,2,32,144]{4,3,2,1,0:T(8,128)(2,1)S(1)}, bf16[32,1,2,32,144]{4,3,2,1,0:T(8,128)(2,1)S(1)}, bf16[32,1,2,32,144]{4,3,2,1,0:T(8,128)(2,1)S(1)}, bf16[32,1,2,32,144]{4,3,2,1,0:T(8,128)(2,1)S(1)}) fusion(s32[]{:T(128)S(6)} %select_n.90, bf16[32,2,32,144]{3,2,1,0:T(8,128)(2,1)S(1)} %bitcast.87, s32[]{:T(128)S(6)} %select_n.92, ...), kind=kLoop, calls=%fused_computation.37.clone.1 | loop fusion | flops 4718592 | bytes 2949136 | tf_op jit(solution)/shard_map/while/body/eval_jaxpr/stack | solution.py:114
  316.2 7.4 %reshape.270 = bf16[128,9216]{1,0:T(8,128)(2,1)S(1)} reshape(bf16[32,4,2,32,144]{4,3,2,1,0:T(8,128)(2,1)} %pad_maximum_fusion.4) | data formatting | bytes 4718592 | tf_op jit(solution)/shard_map/while/body/eval_jaxpr/reshape | solution.py:114
  326.5 5.7 %fusion.66 = (bf16[32,1,2,32,144]{4,3,2,1,0:T(8,128)(2,1)S(1)}, bf16[32,1,2,32,144]{4,3,2,1,0:T(8,128)(2,1)S(1)}, bf16[32,1,2,32,144]{4,3,2,1,0:T(8,128)(2,1)S(1)}, bf16[32,1,2,32,144]{4,3,2,1,0:T(8,128)(2,1)S(1)}) fusion(s32[]{:T(128)S(6)} %select_n.90, bf16[32,2,32,144]{3,2,1,0:T(8,128)(2,1)S(1)} %bitcast.87, s32[]{:T(128)S(6)} %select_n.92, ...), kind=kLoop, calls=%fused_computation.37.clone.1 | loop fusion | flops 4718592 | bytes 2949136 | tf_op jit(solution)/shard_map/while/body/eval_jaxpr/stack | solution.py:114
  334.6 7.4 %reshape.270 = bf16[128,9216]{1,0:T(8,128)(2,1)S(1)} reshape(bf16[32,4,2,32,144]{4,3,2,1,0:T(8,128)(2,1)} %pad_maximum_fusion.4) | data formatting | bytes 4718592 | tf_op jit(solution)/shard_map/while/body/eval_jaxpr/reshape | solution.py:114
  342.8 3.7 convolution_add_fusion.2
  346.5 5.7 %fusion.66 = (bf16[32,1,2,32,144]{4,3,2,1,0:T(8,128)(2,1)S(1)}, bf16[32,1,2,32,144]{4,3,2,1,0:T(8,128)(2,1)S(1)}, bf16[32,1,2,32,144]{4,3,2,1,0:T(8,128)(2,1)S(1)}, bf16[32,1,2,32,144]{4,3,2,1,0:T(8,128)(2,1)S(1)}) fusion(s32[]{:T(128)S(6)} %select_n.90, bf16[32,2,32,144]{3,2,1,0:T(8,128)(2,1)S(1)} %bitcast.87, s32[]{:T(128)S(6)} %select_n.92, ...), kind=kLoop, calls=%fused_computation.37.clone.1 | loop fusion | flops 4718592 | bytes 2949136 | tf_op jit(solution)/shard_map/while/body/eval_jaxpr/stack | solution.py:114
  354.6 7.4 %reshape.270 = bf16[128,9216]{1,0:T(8,128)(2,1)S(1)} reshape(bf16[32,4,2,32,144]{4,3,2,1,0:T(8,128)(2,1)} %pad_maximum_fusion.4) | data formatting | bytes 4718592 | tf_op jit(solution)/shard_map/while/body/eval_jaxpr/reshape | solution.py:114
  362.9 3.7 convolution_add_fusion.2
  366.6 5.7 %fusion.66 = (bf16[32,1,2,32,144]{4,3,2,1,0:T(8,128)(2,1)S(1)}, bf16[32,1,2,32,144]{4,3,2,1,0:T(8,128)(2,1)S(1)}, bf16[32,1,2,32,144]{4,3,2,1,0:T(8,128)(2,1)S(1)}, bf16[32,1,2,32,144]{4,3,2,1,0:T(8,128)(2,1)S(1)}) fusion(s32[]{:T(128)S(6)} %select_n.90, bf16[32,2,32,144]{3,2,1,0:T(8,128)(2,1)S(1)} %bitcast.87, s32[]{:T(128)S(6)} %select_n.92, ...), kind=kLoop, calls=%fused_computation.37.clone.1 | loop fusion | flops 4718592 | bytes 2949136 | tf_op jit(solution)/shard_map/while/body/eval_jaxpr/stack | solution.py:114
  374.7 7.4 %reshape.270 = bf16[128,9216]{1,0:T(8,128)(2,1)S(1)} reshape(bf16[32,4,2,32,144]{4,3,2,1,0:T(8,128)(2,1)} %pad_maximum_fusion.4) | data formatting | bytes 4718592 | tf_op jit(solution)/shard_map/while/body/eval_jaxpr/reshape | solution.py:114
  383.0 3.7 convolution_add_fusion.2
  386.7 5.7 %fusion.66 = (bf16[32,1,2,32,144]{4,3,2,1,0:T(8,128)(2,1)S(1)}, bf16[32,1,2,32,144]{4,3,2,1,0:T(8,128)(2,1)S(1)}, bf16[32,1,2,32,144]{4,3,2,1,0:T(8,128)(2,1)S(1)}, bf16[32,1,2,32,144]{4,3,2,1,0:T(8,128)(2,1)S(1)}) fusion(s32[]{:T(128)S(6)} %select_n.90, bf16[32,2,32,144]{3,2,1,0:T(8,128)(2,1)S(1)} %bitcast.87, s32[]{:T(128)S(6)} %select_n.92, ...), kind=kLoop, calls=%fused_computation.37.clone.1 | loop fusion | flops 4718592 | bytes 2949136 | tf_op jit(solution)/shard_map/while/body/eval_jaxpr/stack | solution.py:114
  394.8 7.4 %reshape.270 = bf16[128,9216]{1,0:T(8,128)(2,1)S(1)} reshape(bf16[32,4,2,32,144]{4,3,2,1,0:T(8,128)(2,1)} %pad_maximum_fusion.4) | data formatting | bytes 4718592 | tf_op jit(solution)/shard_map/while/body/eval_jaxpr/reshape | solution.py:114
  403.1 3.7 convolution_add_fusion.2
  406.8 5.7 %fusion.66 = (bf16[32,1,2,32,144]{4,3,2,1,0:T(8,128)(2,1)S(1)}, bf16[32,1,2,32,144]{4,3,2,1,0:T(8,128)(2,1)S(1)}, bf16[32,1,2,32,144]{4,3,2,1,0:T(8,128)(2,1)S(1)}, bf16[32,1,2,32,144]{4,3,2,1,0:T(8,128)(2,1)S(1)}) fusion(s32[]{:T(128)S(6)} %select_n.90, bf16[32,2,32,144]{3,2,1,0:T(8,128)(2,1)S(1)} %bitcast.87, s32[]{:T(128)S(6)} %select_n.92, ...), kind=kLoop, calls=%fused_computation.37.clone.1 | loop fusion | flops 4718592 | bytes 2949136 | tf_op jit(solution)/shard_map/while/body/eval_jaxpr/stack | solution.py:114
  414.9 7.4 %reshape.270 = bf16[128,9216]{1,0:T(8,128)(2,1)S(1)} reshape(bf16[32,4,2,32,144]{4,3,2,1,0:T(8,128)(2,1)} %pad_maximum_fusion.4) | data formatting | bytes 4718592 | tf_op jit(solution)/shard_map/while/body/eval_jaxpr/reshape | solution.py:114
  423.1 3.7 convolution_add_fusion.2
  426.8 5.7 %fusion.66 = (bf16[32,1,2,32,144]{4,3,2,1,0:T(8,128)(2,1)S(1)}, bf16[32,1,2,32,144]{4,3,2,1,0:T(8,128)(2,1)S(1)}, bf16[32,1,2,32,144]{4,3,2,1,0:T(8,128)(2,1)S(1)}, bf16[32,1,2,32,144]{4,3,2,1,0:T(8,128)(2,1)S(1)}) fusion(s32[]{:T(128)S(6)} %select_n.90, bf16[32,2,32,144]{3,2,1,0:T(8,128)(2,1)S(1)} %bitcast.87, s32[]{:T(128)S(6)} %select_n.92, ...), kind=kLoop, calls=%fused_computation.37.clone.1 | loop fusion | flops 4718592 | bytes 2949136 | tf_op jit(solution)/shard_map/while/body/eval_jaxpr/stack | solution.py:114
  434.9 7.4 %reshape.270 = bf16[128,9216]{1,0:T(8,128)(2,1)S(1)} reshape(bf16[32,4,2,32,144]{4,3,2,1,0:T(8,128)(2,1)} %pad_maximum_fusion.4) | data formatting | bytes 4718592 | tf_op jit(solution)/shard_map/while/body/eval_jaxpr/reshape | solution.py:114
  443.2 3.7 convolution_add_fusion.2
  446.9 5.7 %fusion.66 = (bf16[32,1,2,32,144]{4,3,2,1,0:T(8,128)(2,1)S(1)}, bf16[32,1,2,32,144]{4,3,2,1,0:T(8,128)(2,1)S(1)}, bf16[32,1,2,32,144]{4,3,2,1,0:T(8,128)(2,1)S(1)}, bf16[32,1,2,32,144]{4,3,2,1,0:T(8,128)(2,1)S(1)}) fusion(s32[]{:T(128)S(6)} %select_n.90, bf16[32,2,32,144]{3,2,1,0:T(8,128)(2,1)S(1)} %bitcast.87, s32[]{:T(128)S(6)} %select_n.92, ...), kind=kLoop, calls=%fused_computation.37.clone.1 | loop fusion | flops 4718592 | bytes 2949136 | tf_op jit(solution)/shard_map/while/body/eval_jaxpr/stack | solution.py:114
  455.0 7.4 %reshape.270 = bf16[128,9216]{1,0:T(8,128)(2,1)S(1)} reshape(bf16[32,4,2,32,144]{4,3,2,1,0:T(8,128)(2,1)} %pad_maximum_fusion.4) | data formatting | bytes 4718592 | tf_op jit(solution)/shard_map/while/body/eval_jaxpr/reshape | solution.py:114
  463.3 3.7 convolution_add_fusion.2
  467.0 5.7 %fusion.66 = (bf16[32,1,2,32,144]{4,3,2,1,0:T(8,128)(2,1)S(1)}, bf16[32,1,2,32,144]{4,3,2,1,0:T(8,128)(2,1)S(1)}, bf16[32,1,2,32,144]{4,3,2,1,0:T(8,128)(2,1)S(1)}, bf16[32,1,2,32,144]{4,3,2,1,0:T(8,128)(2,1)S(1)}) fusion(s32[]{:T(128)S(6)} %select_n.90, bf16[32,2,32,144]{3,2,1,0:T(8,128)(2,1)S(1)} %bitcast.87, s32[]{:T(128)S(6)} %select_n.92, ...), kind=kLoop, calls=%fused_computation.37.clone.1 | loop fusion | flops 4718592 | bytes 2949136 | tf_op jit(solution)/shard_map/while/body/eval_jaxpr/stack | solution.py:114
  475.1 7.4 %reshape.270 = bf16[128,9216]{1,0:T(8,128)(2,1)S(1)} reshape(bf16[32,4,2,32,144]{4,3,2,1,0:T(8,128)(2,1)} %pad_maximum_fusion.4) | data formatting | bytes 4718592 | tf_op jit(solution)/shard_map/while/body/eval_jaxpr/reshape | solution.py:114
  483.3 3.7 convolution_add_fusion.2
  489.4 3.5 concatenate.24
  492.9 5.4 %all-to-all-start.1 = ((f32[16,4,9249]{2,1,0:T(4,128)}), f32[16,4,9249]{2,1,0:T(4,128)S(1)}, u32[]{:S(2)}, u32[]{:S(2)}) async-start(f32[16,4,9249]{2,1,0:T(4,128)} %concatenate.24), calls=%async_computation.1 | async-start | bytes 4784128 | tf_op jit(solution)/shard_map/all_to_all | solution.py:74
  498.4 32.5 %all-to-all-done.1 = f32[16,4,9249]{2,1,0:T(4,128)S(1)} async-done(((f32[16,4,9249]{2,1,0:T(4,128)}), f32[16,4,9249]{2,1,0:T(4,128)S(1)}, u32[]{:S(2)}, u32[]{:S(2)}) %all-to-all-start.1) | async-done | bytes 2367776 | tf_op jit(solution)/shard_map/all_to_all | solution.py:74
  (206 shorter events, 174.9 us)
Async XLA Ops:
  7.2 5.5 %copy-start = (f32[16,32]{1,0:T(8,128)S(1)}, f32[16,32]{1,0:T(8,128)}, u32[]{:S(2)}) copy-start(f32[16,32]{1,0:T(8,128)} %param.17) | copy-start | bytes 6148
  7.2 51.4 %all-gather.3.cloned.1.call-start = ((), (), s32[]{:S(2)}) async-start(), calls=%async_computation.2 | async-start | bytes 1270784 | tf_op jit(solution)/shard_map/all_gather | solution.py:24
  72.3 1.0 copy-start.2
  89.2 4.2 copy-start.4
  89.2 4.2 copy-start.5
  93.4 3.0 copy-start.3
  96.4 1.0 copy-start.2
  113.5 4.2 copy-start.4
  113.5 4.2 copy-start.5
  117.8 3.0 copy-start.3
  120.7 1.0 copy-start.2
  137.8 4.2 copy-start.4
  137.8 4.2 copy-start.5
  142.1 3.0 copy-start.3
  145.0 1.0 copy-start.2
  162.1 4.2 copy-start.4
  162.1 4.2 copy-start.5
  166.4 3.0 copy-start.3
  169.3 1.0 copy-start.2
  186.4 4.2 copy-start.4
  186.4 4.2 copy-start.5
  190.7 3.0 copy-start.3
  193.6 1.0 copy-start.2
  210.7 4.2 copy-start.4
  210.7 4.2 copy-start.5
  215.0 3.0 copy-start.3
  217.9 1.0 copy-start.2
  235.0 4.2 copy-start.4
  235.0 4.2 copy-start.5
  239.3 3.0 copy-start.3
  242.2 1.0 copy-start.2
  259.3 4.2 copy-start.4
  259.3 4.2 copy-start.5
  263.6 3.0 copy-start.3
  266.5 1.0 copy-start.2
  282.9 4.2 copy-start.4
  282.9 4.2 copy-start.5
  287.2 3.0 copy-start.3
  290.1 17.9 %copy-start.1 = (bf16[8,4,2,32,144]{4,3,2,1,0:T(8,128)(2,1)S(1)}, bf16[8,4,2,32,144]{4,3,2,1,0:T(8,128)(2,1)}, u32[]{:S(2)}) copy-start(bf16[8,4,2,32,144]{4,3,2,1,0:T(8,128)(2,1)} %get-tuple-element.438) | copy-start | bytes 1769476
  294.0 10.6 %all-to-all-start = ((f32[8,2,8]{2,1,0:T(2,128)}), f32[8,2,8]{2,1,0:T(2,128)S(1)}, u32[]{:S(2)}, u32[]{:S(2)}) async-start(f32[8,2,8]{2,1,0:T(2,128)} %broadcast_in_dim.15), calls=%async_computation | async-start | bytes 16384 | tf_op jit(solution)/shard_map/all_to_all | solution.py:33
  492.9 5.4 %copy-start.6 = (f32[32]{0:T(128)S(1)}, f32[32]{0:T(128)}, u32[]{:S(2)}) copy-start(f32[32]{0:T(128)} %param.19) | copy-start | bytes 388
  492.9 37.9 %all-to-all-start.1 = ((f32[16,4,9249]{2,1,0:T(4,128)}), f32[16,4,9249]{2,1,0:T(4,128)S(1)}, u32[]{:S(2)}, u32[]{:S(2)}) async-start(f32[16,4,9249]{2,1,0:T(4,128)} %concatenate.24), calls=%async_computation.1 | async-start | bytes 4784128 | tf_op jit(solution)/shard_map/all_to_all | solution.py:74
Sparse Core Ops, SparseCore 0:
  11.1 47.4 all-gather.2
where the time goes:
time: 543 us; the launch traced here: 540 us
  local copies, waits for them, and re-layouts  192 us (35%)
  other arithmetic  185 us (34%)
  waiting for transfers between devices  78.1 us (14%)
  matrix products  59.5 us (11%)
  between operations  14.2 us (3%)
  starting transfers between devices  9.87 us (2%)
    concatenate x9, other arithmetic, turned_rows(): jnp.roll(shaped, -stride * (first_turn + step), axis=-1)  91.8 us
    another operation x36, local copies, waits for them, and re-layouts, turned_rows(): jnp.stack(turned, axis=1)  90.1 us
    another operation x18, other arithmetic, turned_rows(): jnp.stack(turned, axis=1)  72.7 us
    reshape x9, local copies, waits for them, and re-layouts, turned_rows(): jnp.stack(turned, axis=1)  66.4 us
    all_gather x1, waiting for transfers between devices, side_by_side(): result = lax.all_gather(both, axis, axis=dim, tiled=True)  39.4 us
    all_to_all x1, waiting for transfers between devices, summed_on_arrival(): lax.all_to_all(split_up(shard, dim, devices), axis, 0, 0, tiled=True)  32.5 us
    dot_general x9, matrix products, insert_group(): lax.dot_general(section, rotated, (((0,), (0,)), ((), ())), preferred_ele...  31.7 us
    dot_general x9, matrix products, score_group(): lax.dot_general(rotated, group_refs, (((1,), (1,)), ((), ())), preferred_...  26.6 us
  transfers between devices with their start and end apart: 3, of which 3 were waited for; matrix products, arithmetic and copies ran while one was open for 2% of the time, Pallas kernels for 0%

commit v1 on v0

v1 whole, which is shorter than its diff:
```python
import functools
import math

import jax
import jax.numpy as jnp
import ml_dtypes
import numpy as np
from jax import lax
from jax.experimental import pallas as pl
from jax.experimental.pallas import tpu as pltpu
from jax.sharding import PartitionSpec as P

TRANS = 4
CYCLES = 32
ANG = 144
ROT = 36
NDEF = 16
STEP = ANG // ROT
PAIRS = 2 * CYCLES
LANES = 2 * STEP * CYCLES
HALF = LANES // 2
OWN = 4
MINE = 8
BLOCKS = 4
KS = OWN * BLOCKS
US = MINE * BLOCKS * TRANS
ROWS = ROT * KS
REACH = 3
offset_sigma = 2.0
F32 = jnp.float32
BF16 = jnp.bfloat16
HIGHEST = lax.Precision.HIGHEST
VMEM_LIMIT = 56 * 1024 * 1024


def phase_parts():
    span = 2 * REACH + 1
    theta = 2.0 * math.pi * np.arange(ANG).reshape(ROT, STEP) / ANG
    radius = np.arange(CYCLES) + 1.0
    fx = (np.cos(theta)[:, :, None] * radius).reshape(ROT, HALF)
    fy = (np.sin(theta)[:, :, None] * radius).reshape(ROT, HALF)
    shift = np.arange(span) - REACH
    phi = (
        -2.0
        * math.pi
        * (shift[:, None, None, None] * fx + shift[None, :, None, None] * fy)
        / (2.0 * CYCLES)
    ).reshape(span * span, ROT, HALF)
    table = np.concatenate([np.cos(phi), np.sin(phi)], axis=2).transpose(1, 0, 2)
    table = np.pad(table, ((0, 0), (0, 64 - span * span), (0, 0)))
    parts = []
    rest = table
    for _ in range(3):
        part = rest.astype(np.float32).astype(ml_dtypes.bfloat16)
        parts.append(part)
        rest = rest - part.astype(np.float64)
    return np.concatenate(parts, axis=1)


def pick_turns():
    rows = np.arange(40)[:, None]
    return (np.arange(ANG)[None, :] // STEP == rows).astype(ml_dtypes.bfloat16)


def nt(a, b, **kw):
    return lax.dot_general(a, b, (((1,), (1,)), ((), ())), preferred_element_type=F32, **kw)


def arrange_kernel(img_ref, ref_ref, prior_ref, off_ref, def_ref, pick_ref, img_out, ref_out, cut, flat):
    angle = lax.broadcasted_iota(jnp.int32, (CYCLES, ANG), 1) % STEP
    pick = pick_ref[...]
    for source, count, out in ((ref_ref, OWN, ref_out), (img_ref, MINE, img_out)):
        for j in range(PAIRS):
            line = source[:, j * ANG : (j + 1) * ANG].astype(F32)
            cut[0, pl.ds(j * 8, count), :] = line[:, :HALF]
            cut[1, pl.ds(j * 8, count), : ANG - HALF] = line[:, HALF:]
        for i in range(count):
            one = jnp.concatenate(
                [cut.at[n][pl.ds(i, PAIRS, stride=8), :] for n in range(2)], axis=1
            )[:, :ANG]
            spread = jnp.concatenate(
                [
                    jnp.where(angle == c, one[p * CYCLES : (p + 1) * CYCLES], 0.0)
                    for p in range(2)
                    for c in range(STEP)
                ],
                axis=0,
            ).astype(BF16)
            turned = nt(pick, spread)
            flat[0, pl.ds(i * 40, 40), :] = turned[:, :HALF]
            flat[1, pl.ds(i * 40, 40), :] = turned[:, HALF:]
        for b in range(ROT):
            for n in range(2):
                line = flat.at[n][pl.ds(b, count, stride=40), :]
                out[b, :, n * HALF : (n + 1) * HALF] = line.astype(BF16)
    row = lax.broadcasted_iota(jnp.int32, (MINE, LANES), 0)
    lane = lax.broadcasted_iota(jnp.int32, (MINE, LANES), 1)
    extra = jnp.zeros((MINE, LANES), F32)
    for i in range(MINE):
        for t in range(TRANS):
            for d in range(2):
                value = off_ref[i, t, d].astype(F32)
                extra = jnp.where((row == i) & (lane == 2 * t + d), value, extra)
        extra = jnp.where((row == i) & (lane == 8), def_ref[i].astype(F32), extra)
    img_out[ROT] = extra.astype(BF16)
    krow = lax.broadcasted_iota(jnp.int32, (OWN, OWN), 0)
    kcol = lax.broadcasted_iota(jnp.int32, (OWN, OWN), 1)
    prior = jnp.broadcast_to(prior_ref[...].astype(F32), (OWN, OWN))
    column = jnp.sum(jnp.where(krow == kcol, prior, 0.0), axis=1, keepdims=True)
    ref_out[ROT] = jnp.broadcast_to(column, (OWN, LANES)).astype(BF16)


def arrange(images, references, prior, offsets, defocus, pick):
    vmem = pl.BlockSpec(memory_space=pltpu.VMEM)
    smem = pl.BlockSpec(memory_space=pltpu.SMEM)
    return pl.pallas_call(
        arrange_kernel,
        out_shape=(
            jax.ShapeDtypeStruct((ROT + 1, MINE, LANES), BF16),
            jax.ShapeDtypeStruct((ROT + 1, OWN, LANES), BF16),
        ),
        in_specs=[vmem, vmem, vmem, smem, smem, vmem],
        out_specs=(vmem, vmem),
        scratch_shapes=[pltpu.VMEM((2, PAIRS * 8, HALF), F32), pltpu.VMEM((2, MINE * 40, HALF), F32)],
        compiler_params=pltpu.CompilerParams(vmem_limit_bytes=VMEM_LIMIT),
        name="arrange",
    )(images, references, prior, offsets, defocus, pick)


def score_kernel(
    own_ref,
    i0, i1, i2, i3,
    r0, r1, r2, r3,
    ctf_ref, noise_ref, table_hbm,
    exp_out, stat_out, ins_out, sq_out,
    table, weighted, pictures, back, acc, sem,
):
    copy = pltpu.make_async_copy(table_hbm, table, sem)
    copy.start()
    own = own_ref[0]
    for step, source in enumerate((i0, i1, i2, i3)):
        pictures[own ^ step] = source[...]
    square = jnp.zeros((KS, LANES), F32)
    for b in range(ROT):
        block = jnp.concatenate([r[b].astype(F32) for r in (r0, r1, r2, r3)], axis=0)
        square = square + block * block
        m = (ROT - b) % ROT
        back[pl.ds(m * KS, KS), :] = block.astype(BF16)
        back[pl.ds((m + ROT) * KS, KS), :] = block.astype(BF16)
    prior = jnp.concatenate([r[ROT].astype(F32) for r in (r0, r1, r2, r3)], axis=0)[:, :HALF]

    extra = jnp.concatenate([pictures[k, ROT].astype(F32) for k in range(BLOCKS)], axis=0)
    dx = jnp.concatenate([extra[:, 2 * t : 2 * t + 1] for t in range(TRANS)], axis=0)
    dy = jnp.concatenate([extra[:, 2 * t + 1 : 2 * t + 2] for t in range(TRANS)], axis=0)
    combo = (dx + REACH) * (2 * REACH + 1) + (dy + REACH)
    slot = lax.broadcasted_iota(jnp.int32, (US, 192), 1) % 64
    hot = jnp.where(slot.astype(F32) == combo, 1.0, 0.0).astype(BF16)
    group = lax.broadcasted_iota(jnp.int32, (MINE * BLOCKS, NDEF), 1).astype(F32)
    which = jnp.where(group == extra[:, 8:9], 1.0, 0.0)
    contrast = jnp.dot(which, ctf_ref[...], precision=HIGHEST, preferred_element_type=F32)
    noise = noise_ref[...]
    whiten = contrast / noise
    squared = contrast * contrast
    coef = squared / (2.0 * noise)
    four = lambda v: jnp.concatenate([v] * TRANS, axis=0)
    sq_out[:, :HALF] = four(squared)
    sq_out[:, HALF:] = jnp.ones((US, HALF), F32)
    coef_rows = four(jnp.concatenate([coef, coef], axis=1))
    penalty = nt(square, coef_rows, precision=HIGHEST)
    near = -(dx * dx + dy * dy) / (2.0 * offset_sigma * offset_sigma)
    diag = lax.broadcasted_iota(jnp.int32, (US, US), 0) == lax.broadcasted_iota(
        jnp.int32, (US, US), 1
    )
    near_row = jnp.sum(jnp.where(diag, near, 0.0), axis=0, keepdims=True)
    base = prior - penalty + near_row

    contrast4 = four(contrast)
    whiten4 = four(whiten)
    copy.wait()

    def shift_turn(b, carry):
        turn = jnp.dot(hot, table[b], preferred_element_type=F32)
        cosine, sine = turn[:, :HALF], turn[:, HALF:]
        block = jnp.concatenate([pictures[k, b].astype(F32) for k in range(BLOCKS)], axis=0)
        real, imag = four(block[:, :HALF]), four(block[:, HALF:])
        shifted_real = real * cosine - imag * sine
        shifted_imag = real * sine + imag * cosine
        rows = pl.ds(pl.multiple_of(b * US, US), US)
        weighted[rows, :HALF] = (shifted_real * whiten4).astype(BF16)
        weighted[rows, HALF:] = (shifted_imag * whiten4).astype(BF16)
        ins_out[rows, :HALF] = (shifted_real * contrast4).astype(BF16)
        ins_out[rows, HALF:] = (shifted_imag * contrast4).astype(BF16)
        return carry

    lax.fori_loop(0, ROT, shift_turn, 0)

    acc[...] = jnp.zeros_like(acc)

    def score_turns(h, carry):
        rows = pl.ds(pl.multiple_of((ROT - 2 * h) * KS, 2 * KS), ROWS)
        cols = pl.ds(pl.multiple_of(h * 2 * US, 2 * US), 2 * US)
        acc[...] += nt(back[rows, :], weighted[cols, :])
        return carry

    lax.fori_loop(0, ROT // 2, score_turns, 0)

    peak = jnp.full((KS, US), -jnp.inf, F32)
    for r in range(ROT):
        last = (r - 1) % ROT
        logp = acc[r * KS : (r + 1) * KS, :HALF] + acc[last * KS : (last + 1) * KS, HALF:] + base
        exp_out[r * KS : (r + 1) * KS, :] = logp
        peak = jnp.maximum(peak, logp)
    peak = jnp.max(peak, axis=0, keepdims=True)
    peak = jnp.broadcast_to(peak, (8, US))
    peak = jnp.maximum(peak, pltpu.roll(peak, 32, 1))
    peak = jnp.maximum(peak, pltpu.roll(peak, 64, 1))
    wide = jnp.broadcast_to(peak[:1], (KS, US))
    total = jnp.zeros((KS, US), F32)
    for r in range(ROT):
        value = jnp.exp(exp_out[r * KS : (r + 1) * KS, :] - wide)
        exp_out[r * KS : (r + 1) * KS, :] = value
        total = total + value
    total = jnp.broadcast_to(jnp.sum(total, axis=0, keepdims=True), (8, US))
    total = total + pltpu.roll(total, 32, 1)
    total = total + pltpu.roll(total, 64, 1)
    pair = jnp.concatenate([peak[:1], total[:1]], axis=0)
    for j in range(32):
        stat_out[j] = pair


def score(own, imgs, refs, ctf4, noise4, table):
    vmem = pl.BlockSpec(memory_space=pltpu.VMEM)
    smem = pl.BlockSpec(memory_space=pltpu.SMEM)
    return pl.pallas_call(
        score_kernel,
        out_shape=(
            jax.ShapeDtypeStruct((ROWS, US), F32),
            jax.ShapeDtypeStruct((32, 2, US), F32),
            jax.ShapeDtypeStruct((ROT * US, LANES), BF16),
            jax.ShapeDtypeStruct((US, LANES), F32),
        ),
        in_specs=[smem] + [vmem] * 10 + [pl.BlockSpec(memory_space=pl.ANY)],
        out_specs=(vmem,) * 4,
        scratch_shapes=[
            pltpu.VMEM((ROT, 192, LANES), BF16),
            pltpu.VMEM((ROT * US, LANES), BF16),
            pltpu.VMEM((BLOCKS, ROT + 1, MINE, LANES), BF16),
            pltpu.VMEM((2 * ROWS, LANES), BF16),
            pltpu.VMEM((ROWS, LANES), F32),
            pltpu.SemaphoreType.DMA,
        ],
        compiler_params=pltpu.CompilerParams(vmem_limit_bytes=VMEM_LIMIT),
        name="score",
    )(own, *imgs, *refs, ctf4, noise4, table)


def insert_kernel(own_ref, exp_ref, pair_ref, all_ref, ins_ref, sq_ref, own_out, s1, s2, s3, like_out, post, acc):
    peaks = jnp.concatenate([all_ref[j, 0:1, :] for j in range(32)], axis=0)
    totals = jnp.concatenate([all_ref[j, 1:2, :] for j in range(32)], axis=0)
    peak = jnp.max(peaks, axis=0, keepdims=True)
    total = jnp.sum(totals * jnp.exp(peaks - peak), axis=0, keepdims=True)
    like = jnp.broadcast_to(peak + jnp.log(total), (8, US))
    shift = (US - own_ref[0] * MINE) % US
    like_out[...] = pltpu.roll(like, shift, 1)
    scale = jnp.broadcast_to(jnp.exp(pair_ref[0, 0:1, :] - peak) / total, (KS, US))
    count = jnp.zeros((KS, US), F32)
    for r in range(ROT):
        value = (exp_ref[r * KS : (r + 1) * KS, :] * scale).astype(BF16)
        count = count + value.astype(F32)
        for side in range(2):
            m = (side - r) % ROT
            for again in (m, m + ROT):
                post[again * KS : (again + 1) * KS, side * HALF : (side + 1) * HALF] = value

    acc[...] = jnp.zeros_like(acc)

    def insert_turns(h, carry):
        rows = pl.ds(pl.multiple_of((ROT - 2 * h) * KS, 2 * KS), ROWS)
        cols = pl.ds(pl.multiple_of(h * 2 * US, 2 * US), 2 * US)
        acc[...] += jnp.dot(post[rows, :], ins_ref[cols, :], preferred_element_type=F32)
        return carry

    lax.fori_loop(0, ROT // 2, insert_turns, 0)
    sums = jnp.dot(count, sq_ref[...], precision=HIGHEST, preferred_element_type=F32)
    high = sums.astype(BF16)
    low = (sums - high.astype(F32)).astype(BF16)
    for b in range(ROT):
        block = acc[b * KS : (b + 1) * KS, :]
        own_out[b] = block[:OWN]
        for d, out in ((1, s1), (2, s2), (3, s3)):
            out[b] = block[d * OWN : (d + 1) * OWN].astype(BF16)
    own_out[ROT] = sums[:OWN]
    own_out[ROT + 1] = jnp.zeros((OWN, LANES), F32)
    for d, out in ((1, s1), (2, s2), (3, s3)):
        part = sums[d * OWN : (d + 1) * OWN]
        high = part.astype(BF16)
        out[ROT] = high
        out[ROT + 1] = (part - high.astype(F32)).astype(BF16)


def insert(own, exps, stats, gathered, ins, sq):
    vmem = pl.BlockSpec(memory_space=pltpu.VMEM)
    smem = pl.BlockSpec(memory_space=pltpu.SMEM)
    piece = (ROT + 2, OWN, LANES)
    return pl.pallas_call(
        insert_kernel,
        out_shape=(
            jax.ShapeDtypeStruct(piece, F32),
            jax.ShapeDtypeStruct(piece, BF16),
            jax.ShapeDtypeStruct(piece, BF16),
            jax.ShapeDtypeStruct(piece, BF16),
            jax.ShapeDtypeStruct((8, US), F32),
        ),
        in_specs=[smem] + [vmem] * 5,
        out_specs=(vmem,) * 5,
        scratch_shapes=[
            pltpu.VMEM((2 * ROWS, LANES), BF16),
            pltpu.VMEM((ROWS, LANES), F32),
        ],
        compiler_params=pltpu.CompilerParams(vmem_limit_bytes=VMEM_LIMIT),
        name="insert",
    )(own, exps, stats, gathered, ins, sq)


def finish_kernel(own_ref, g1, g2, g3, tau_ref, out_ref, weight_out, fresh, turned, lines):
    parts = [own_ref, g1, g2, g3]
    sums = sum(p[ROT].astype(F32) + p[ROT + 1].astype(F32) for p in parts)
    denom = sums[:, :HALF] + 1.0 / tau_ref[...]
    denom = jnp.concatenate([denom, denom], axis=1)
    weight_out[...] = sums[:, HALF:] / (MINE * 16)
    for b in range(ROT):
        total = own_ref[b] + g1[b].astype(F32) + g2[b].astype(F32) + g3[b].astype(F32)
        total = total / denom
        fresh[0, pl.ds(b * 8, OWN), :] = total[:, :HALF]
        fresh[1, pl.ds(b * 8, OWN), :] = total[:, HALF:]
    for k in range(OWN):
        one = [fresh.at[p][pl.ds(k, ROT, stride=8), :] for p in range(2)]
        for c in range(STEP):
            pair = [one[p][:, c * CYCLES : (c + 1) * CYCLES] for p in range(2)]
            turned[pl.ds(c, ROT, stride=STEP), :] = jnp.concatenate(pair + pair, axis=1)
        first = turned[0:128, :].T
        second = turned[128:256, :].T
        lines[0, pl.ds(k * PAIRS, PAIRS), :] = first[:PAIRS]
        lines[1, pl.ds(k * PAIRS, PAIRS), :] = second[:PAIRS]
    for j in range(PAIRS):
        line = [lines.at[n][pl.ds(j, OWN, stride=PAIRS), :] for n in range(2)]
        out_ref[:, j * ANG : (j + 1) * ANG] = jnp.concatenate(line, axis=1)[:, :ANG]


def finish(own, got, tau4):
    vmem = pl.BlockSpec(memory_space=pltpu.VMEM)
    return pl.pallas_call(
        finish_kernel,
        out_shape=(
            jax.ShapeDtypeStruct((OWN, 2 * CYCLES * ANG), F32),
            jax.ShapeDtypeStruct((OWN, HALF), F32),
        ),
        in_specs=[vmem] * 5,
        out_specs=(vmem, vmem),
        scratch_shapes=[
            pltpu.VMEM((2, ROT * 8, HALF), F32),
            pltpu.VMEM((256, 128), F32),
            pltpu.VMEM((2, OWN * PAIRS, HALF), F32),
        ],
        compiler_params=pltpu.CompilerParams(vmem_limit_bytes=VMEM_LIMIT),
        name="finish",
    )(own, *got, tau4)


def along_y(value, distance):
    return lax.ppermute(
        value, "img", [(i, ((i // 4 + distance) % 4) * 4 + i % 4) for i in range(16)]
    )


def beside(value, img_flip, cls_flip):
    pairs = [
        (i * 8 + c, (i ^ img_flip) * 8 + (c ^ cls_flip)) for i in range(16) for c in range(8)
    ]
    return lax.ppermute(value, ("img", "cls"), pairs)


def per_device(
    table, pick, images, references, class_logprior, ctf_table, noise_power, tau_power, defocus, offsets
):
    own = (lax.axis_index("img") % BLOCKS).astype(jnp.int32).reshape(1)
    img, ref = arrange(images, references, class_logprior.reshape(1, OWN), offsets, defocus, pick)
    imgs = (img, beside(img, 1, 0), beside(img, 2, 1), beside(img, 3, 1))
    refs = (ref, along_y(ref, 3), along_y(ref, 2), along_y(ref, 1))
    ctf4 = jnp.tile(ctf_table, (1, STEP))
    noise4 = jnp.tile(noise_power, STEP).reshape(1, HALF)
    tau4 = jnp.tile(tau_power, STEP).reshape(1, HALF)
    exps, stats, ins, sq = score(own, imgs, refs, ctf4, noise4, table)
    same_images = [[(y * 4 + r) * 8 + c for r in range(4) for c in range(8)] for y in range(4)]
    gathered = lax.all_to_all(
        stats, ("img", "cls"), 0, 0, tiled=True, axis_index_groups=same_images
    )
    numer, s1, s2, s3, like = insert(own, exps, stats, gathered, ins, sq)
    got = (along_y(s1, 1), along_y(s2, 2), along_y(s3, 3))
    fresh, weight = finish(numer, got, tau4)
    return fresh, weight[:, 0], like[0, :MINE]


def solution(mesh):
    table = phase_parts()
    pick = pick_turns()
    body = functools.partial(per_device, jnp.asarray(table), jnp.asarray(pick))
    return jax.shard_map(
        body,
        mesh=mesh,
        in_specs=(
            P("img", None),
            P(("img", "cls"), None),
            P(("img", "cls")),
            P(),
            P(),
            P(),
            P("img"),
            P("img", None, None),
        ),
        out_specs=(P(("img", "cls"), None), P(("img", "cls")), P("img")),
        check_vma=False,
    )
```

time: 543 us -> 71.7 us (0.13)
  other arithmetic: 185 us -> 0 us
  local copies, waits for them, and re-layouts: 192 us -> 9.1 us
  waiting for transfers between devices: 78.1 us -> 13.9 us
  matrix products: 59.5 us -> 0 us
  Pallas kernels: 0 us -> 28.6 us
  between operations: 14.2 us -> 0.74 us
  starting transfers between devices: 9.87 us -> 19 us
    concatenate x10 -> x0, other arithmetic: 91.8 us -> none  [the longest x9 91.8 us: turned_rows(): jnp.roll(shaped, -stride * (first_turn + step), axis=-1)]
    another operation x36 -> x6, local copies, waits for them, and re-layouts: 90.1 us -> 3.23 us  [the longest x2 1.38 us: per_device(): ctf4 = jnp.tile(ctf_table, (1, STEP))]
    another operation x18 -> x0, other arithmetic: 72.7 us -> none  [turned_rows(): jnp.stack(turned, axis=1)]
    reshape x11 -> x0, local copies, waits for them, and re-layouts: 68.5 us -> none  [the longest x9 66.4 us: turned_rows(): jnp.stack(turned, axis=1)]
    dot_general x21 -> x0, matrix products: 59.5 us -> none  [the longest x9 31.7 us: insert_group(): lax.dot_general(section, rotated, (((0,), (0,)), ((), ())), preferred_ele...]
    all_gather x1 -> x0, waiting for transfers between devices: 39.4 us -> none  [side_by_side(): result = lax.all_gather(both, axis, axis=dim, tiled=True)]
    all_to_all x2 -> x1, waiting for transfers between devices: 38.7 us -> 6.82 us  [per_device(): lax.all_to_all(stats, ('img', 'cls'), 0, 0, tiled=True, axis_index_groups...]
    pallas_call x0 -> x4, Pallas kernels: none -> 28.6 us  [the longest x1 16.7 us: score(): pl.pallas_call(score_kernel, out_shape=(jax.ShapeDtypeStruct((ROWS, US),...]
  transfers between devices with their start and end apart: 3 -> 10, of which waited for: 3 -> 5; matrix products, arithmetic and copies ran while one was open for 2% -> 6% of each run, Pallas kernels for 0% -> 0%
where the time goes in v1:
time: 71.7 us; the launch traced here: 71.3 us
  Pallas kernels  28.6 us (40%)
  starting transfers between devices  19 us (26%)
  waiting for transfers between devices  13.9 us (19%)
  local copies, waits for them, and re-layouts  9.1 us (13%)
  between operations  0.74 us (1%)
    pallas_call x1, Pallas kernels, score(): pl.pallas_call(score_kernel, out_shape=(jax.ShapeDtypeStruct((ROWS, US),...  16.7 us
    ppermute x6, starting transfers between devices, along_y(): lax.ppermute(value, 'img', [(i, (i // 4 + distance) % 4 * 4 + i % 4) for...  8.03 us
    all_to_all x1, starting transfers between devices, per_device(): lax.all_to_all(stats, ('img', 'cls'), 0, 0, tiled=True, axis_index_groups...  7.91 us
    pallas_call x1, Pallas kernels, insert(): pl.pallas_call(insert_kernel, out_shape=(jax.ShapeDtypeStruct(piece, F32)...  7.11 us
    ppermute x6, waiting for transfers between devices, along_y(): lax.ppermute(value, 'img', [(i, (i // 4 + distance) % 4 * 4 + i % 4) for...  7.04 us
    all_to_all x1, waiting for transfers between devices, per_device(): lax.all_to_all(stats, ('img', 'cls'), 0, 0, tiled=True, axis_index_groups...  6.82 us
    unnamed x23, local copies, waits for them, and re-layouts  3.38 us
    ppermute x3, starting transfers between devices, beside(): return lax.ppermute(value, ('img', 'cls'), pairs)  3.07 us
  transfers between devices with their start and end apart: 10, of which 5 were waited for; matrix products, arithmetic and copies ran while one was open for 6% of the time, Pallas kernels for 0%

profile of v1, /device:TPU:0, one launch (start us, length us, event | category | flops | bytes accessed | tf_op | source)
XLA Modules:
  0.0 71.3 jit_solution(10555587521971138523)
XLA Ops:
  0.6 0.0 copy-start.10
  0.6 1.4 %copy.14.off_ref = s32[8,4,2]{2,1,0:T(4,128)} copy(s32[8,4,2]{0,2,1:T(2,128)} %param.17) | data formatting | bytes 512 | tf_op args[7]
  2.0 2.5 %arrange.1 = (bf16[37,8,256]{2,1,0:T(8,128)(2,1)}, bf16[37,4,256]{2,1,0:T(4,128)(2,1)}) custom-call(bf16[8,9216]{1,0:T(8,128)(2,1)} %img_ref.1, bf16[4,9216]{1,0:T(4,128)(2,1)} %ref_ref.1, bf16[1,4]{1,0:T(2,128)(2,1)} %bitcast.4, s32[8,4,2]{2,1,0:T(4,128)} %copy.14.off_ref, s32[8]{0:T(128)} %def_ref.1, bf16[40,144]{1,0:T(8,128)(2,1)} %constant.23.clone.pick_ref), custom_call_target="tpu_custom_call" | custom-call | tf_op jit(solution)/shard_map/arrange/pallas_call | solution.py:116
  4.5 3.1 %collective-permute-start.3 = (bf16[37,4,256]{2,1,0:T(4,128)(2,1)}, bf16[37,4,256]{2,1,0:T(4,128)(2,1)S(1)}, u32[]{:S(2)}, u32[]{:S(2)}) collective-permute-start(bf16[37,4,256]{2,1,0:T(4,128)(2,1)} %get-tuple-element.17.r0), channel_id=1, source_target_pairs={{0,96},{8,104},{16,112},{24,120},{32,0},{40,8},{48,16},{56,24},{64... | collective-permute-start | bytes 227336 | tf_op jit(solution)/shard_map/ppermute | solution.py:371
  7.6 0.0 collective-permute-start
  7.6 2.8 %collective-permute-start.1 = (bf16[37,8,256]{2,1,0:T(8,128)(2,1)}, bf16[37,8,256]{2,1,0:T(8,128)(2,1)S(1)}, u32[]{:S(2)}, u32[]{:S(2)}) collective-permute-start(bf16[37,8,256]{2,1,0:T(8,128)(2,1)} %get-tuple-element.16.i0), channel_id=1, source_target_pairs={{0,17},{1,16},{2,19},{3,18},{4,21},{5,20},{6,23},{7,22},{8,25},{9,... | collective-permute-start | bytes 454664 | tf_op jit(solution)/shard_map/ppermute | solution.py:380
  10.4 0.3 collective-permute-start.2
  10.7 0.6 collective-permute-start.4
  11.3 0.0 collective-permute-done.3.r1
  11.3 1.0 %collective-permute-start.5 = (bf16[37,4,256]{2,1,0:T(4,128)(2,1)}, bf16[37,4,256]{2,1,0:T(4,128)(2,1)S(1)}, u32[]{:S(2)}, u32[]{:S(2)}) collective-permute-start(bf16[37,4,256]{2,1,0:T(4,128)(2,1)} %get-tuple-element.17.r0), channel_id=1, source_target_pairs={{0,32},{8,40},{16,48},{24,56},{32,64},{40,72},{48,80},{56,88},{64,... | collective-permute-start | bytes 227336 | tf_op jit(solution)/shard_map/ppermute | solution.py:371
  12.3 0.7 tile.8
  13.0 0.7 tile.9.ctf_ref
  13.7 0.7 tile.10
  14.3 0.6 reshape_tile.6.noise_ref
  14.9 2.6 %collective-permute-done.4.r2 = bf16[37,4,256]{2,1,0:T(4,128)(2,1)S(1)} collective-permute-done((bf16[37,4,256]{2,1,0:T(4,128)(2,1)}, bf16[37,4,256]{2,1,0:T(4,128)(2,1)S(1)}, u32[]{:S(2)}, u32[]{:S(2)}) %collective-permute-start.4) | collective-permute-done | bytes 75808 | tf_op jit(solution)/shard_map/ppermute | solution.py:371
  17.6 0.0 copy-start.8
  17.6 1.0 %collective-permute-done.5.r3 = bf16[37,4,256]{2,1,0:T(4,128)(2,1)S(1)} collective-permute-done((bf16[37,4,256]{2,1,0:T(4,128)(2,1)}, bf16[37,4,256]{2,1,0:T(4,128)(2,1)S(1)}, u32[]{:S(2)}, u32[]{:S(2)}) %collective-permute-start.5) | collective-permute-done | bytes 75808 | tf_op jit(solution)/shard_map/ppermute | solution.py:371
  18.5 0.0 copy-start.9
  18.5 0.0 collective-permute-done.i1
  18.5 0.0 collective-permute-done.1.i2
  18.5 0.0 copy-start.1
  18.6 0.0 collective-permute-done.2.i3
  18.6 0.0 copy-start.2
  18.6 0.0 copy-done.7
  18.6 0.0 copy-done.8
  18.6 0.6 copy-done.9
  19.2 0.1 copy-done
  19.2 0.0 copy-done.1
  19.3 0.1 copy-done.2
  19.3 16.7 %score.1 = (f32[576,128]{1,0:T(8,128)}, f32[32,2,128]{2,1,0:T(2,128)}, bf16[4608,256]{1,0:T(8,128)(2,1)}, f32[128,256]{1,0:T(8,128)}) custom-call(s32[1]{0:T(128)} %bitcast.own_ref, bf16[37,8,256]{2,1,0:T(8,128)(2,1)} %get-tuple-element.16.i0, bf16[37,8,256]{2,1,0:T(8,128)(2,1)} %copy-done, bf16[37,8,256]{2,1,0:T(8,128)(2,1)} %copy-done.1, ...), custom_call_target="tpu_custom_call" | custom-call | tf_op jit(solution)/shard_map/score/pallas_call | solution.py:234
  36.0 7.9 %all-to-all-start = ((f32[32,2,128]{2,1,0:T(2,128)}), f32[32,2,128]{2,1,0:T(2,128)S(1)}, u32[]{:S(2)}, u32[]{:S(2)}) async-start(f32[32,2,128]{2,1,0:T(2,128)} %get-tuple-element.19.pair_ref), calls=%async_computation | async-start | bytes 65536 | tf_op jit(solution)/shard_map/all_to_all | solution.py:395
  43.9 0.0 copy-done.10
  43.9 0.6 reshape_tile.7.tau_ref
  44.5 6.8 %all-to-all-done.all_ref = f32[32,2,128]{2,1,0:T(2,128)S(1)} async-done(((f32[32,2,128]{2,1,0:T(2,128)}), f32[32,2,128]{2,1,0:T(2,128)S(1)}, u32[]{:S(2)}, u32[]{:S(2)}) %all-to-all-start) | async-done | bytes 32800 | tf_op jit(solution)/shard_map/all_to_all | solution.py:395
  51.4 0.6 copy-done.3
  52.0 7.1 %insert.1 = (f32[38,4,256]{2,1,0:T(4,128)}, bf16[38,4,256]{2,1,0:T(4,128)(2,1)}, bf16[38,4,256]{2,1,0:T(4,128)(2,1)}, bf16[38,4,256]{2,1,0:T(4,128)(2,1)}, f32[8,128]{1,0:T(8,128)}) custom-call(s32[1]{0:T(128)} %bitcast.own_ref, f32[576,128]{1,0:T(8,128)} %get-tuple-element.18.exp_ref, f32[32,2,128]{2,1,0:T(2,128)} %get-tuple-element.19.pair_ref, ...), custom_call_target="tpu_custom_call" | custom-call | tf_op jit(solution)/shard_map/insert/pallas_call | solution.py:305
  59.1 0.0 collective-permute-start.6
  59.1 2.0 %collective-permute-start.7 = (bf16[38,4,256]{2,1,0:T(4,128)(2,1)}, bf16[38,4,256]{2,1,0:T(4,128)(2,1)S(1)}, u32[]{:S(2)}, u32[]{:S(2)}) collective-permute-start(bf16[38,4,256]{2,1,0:T(4,128)(2,1)} %get-tuple-element.24), channel_id=1, source_target_pairs={{0,64},{8,72},{16,80},{24,88},{32,96},{40,104},{48,112},{56,120},{... | collective-permute-start | bytes 233480 | tf_op jit(solution)/shard_map/ppermute | solution.py:371
  61.1 1.3 %collective-permute-start.8 = (bf16[38,4,256]{2,1,0:T(4,128)(2,1)}, bf16[38,4,256]{2,1,0:T(4,128)(2,1)S(1)}, u32[]{:S(2)}, u32[]{:S(2)}) collective-permute-start(bf16[38,4,256]{2,1,0:T(4,128)(2,1)} %get-tuple-element.25), channel_id=1, source_target_pairs={{0,96},{8,104},{16,112},{24,120},{32,0},{40,8},{48,16},{56,24},{64... | collective-permute-start | bytes 233480 | tf_op jit(solution)/shard_map/ppermute | solution.py:371
  62.4 1.2 %slice_bitcast_fusion = f32[8]{0:T(128)} fusion(f32[8,128]{1,0:T(8,128)} %get-tuple-element.28), kind=kLoop, calls=%fused_computation.1 | loop fusion | bytes 64 | tf_op jit(solution)/shard_map/squeeze | solution.py:401
  63.6 2.9 %collective-permute-done.6.g1 = bf16[38,4,256]{2,1,0:T(4,128)(2,1)S(1)} collective-permute-done((bf16[38,4,256]{2,1,0:T(4,128)(2,1)}, bf16[38,4,256]{2,1,0:T(4,128)(2,1)S(1)}, u32[]{:S(2)}, u32[]{:S(2)}) %collective-permute-start.6) | collective-permute-done | bytes 77856 | tf_op jit(solution)/shard_map/ppermute | solution.py:371
  66.5 0.0 collective-permute-done.7.g2
  66.5 0.6 collective-permute-done.8.g3
  67.1 0.1 copy-done.4
  67.1 0.0 copy-done.5
  67.1 0.6 copy-done.6
  67.7 2.3 %finish.1 = (f32[4,9216]{1,0:T(4,128)}, f32[4,128]{1,0:T(4,128)}) custom-call(f32[38,4,256]{2,1,0:T(4,128)} %get-tuple-element.22.own_ref, bf16[38,4,256]{2,1,0:T(4,128)(2,1)} %copy-done.4, bf16[38,4,256]{2,1,0:T(4,128)(2,1)} %copy-done.5, bf16[38,4,256]{2,1,0:T(4,128)(2,1)} %copy-done.6, f32[1,128]{1,0:T(1,128)} %reshape_tile.7.tau_ref), custom_call_target="tpu_custom_call" | custom-call | tf_op jit(solution)/shard_map/finish/pallas_call | solution.py:352
  70.0 1.3 %slice_reduce_fusion = f32[4]{0:T(128)} fusion(f32[4,128]{1,0:T(4,128)} %get-tuple-element.27), kind=kLoop, calls=%fused_computation | loop fusion | bytes 32 | tf_op jit(solution)/shard_map/slice | solution.py:401
  (7 shorter events, 0.0 us)
Async XLA Ops:
  0.6 43.3 %copy-start.10 = (f32[32]{0:T(128)S(1)}, f32[32]{0:T(128)}, u32[]{:S(2)}) copy-start(f32[32]{0:T(128)} %param.15) | copy-start | bytes 388
  4.5 6.8 %collective-permute-start.3 = (bf16[37,4,256]{2,1,0:T(4,128)(2,1)}, bf16[37,4,256]{2,1,0:T(4,128)(2,1)S(1)}, u32[]{:S(2)}, u32[]{:S(2)}) collective-permute-start(bf16[37,4,256]{2,1,0:T(4,128)(2,1)} %get-tuple-element.17.r0), channel_id=1, source_target_pairs={{0,96},{8,104},{16,112},{24,120},{32,0},{40,8},{48,16},{56,24},{64... | collective-permute-start | bytes 227336 | tf_op jit(solution)/shard_map/ppermute | solution.py:371
  7.6 10.9 %collective-permute-start = (bf16[37,8,256]{2,1,0:T(8,128)(2,1)}, bf16[37,8,256]{2,1,0:T(8,128)(2,1)S(1)}, u32[]{:S(2)}, u32[]{:S(2)}) collective-permute-start(bf16[37,8,256]{2,1,0:T(8,128)(2,1)} %get-tuple-element.16.i0), channel_id=1, source_target_pairs={{0,8},{1,9},{2,10},{3,11},{4,12},{5,13},{6,14},{7,15},{8,0},{9,1},... | collective-permute-start | bytes 454664 | tf_op jit(solution)/shard_map/ppermute | solution.py:380
  7.6 10.9 %collective-permute-start.1 = (bf16[37,8,256]{2,1,0:T(8,128)(2,1)}, bf16[37,8,256]{2,1,0:T(8,128)(2,1)S(1)}, u32[]{:S(2)}, u32[]{:S(2)}) collective-permute-start(bf16[37,8,256]{2,1,0:T(8,128)(2,1)} %get-tuple-element.16.i0), channel_id=1, source_target_pairs={{0,17},{1,16},{2,19},{3,18},{4,21},{5,20},{6,23},{7,22},{8,25},{9,... | collective-permute-start | bytes 454664 | tf_op jit(solution)/shard_map/ppermute | solution.py:380
  10.4 8.2 %collective-permute-start.2 = (bf16[37,8,256]{2,1,0:T(8,128)(2,1)}, bf16[37,8,256]{2,1,0:T(8,128)(2,1)S(1)}, u32[]{:S(2)}, u32[]{:S(2)}) collective-permute-start(bf16[37,8,256]{2,1,0:T(8,128)(2,1)} %get-tuple-element.16.i0), channel_id=1, source_target_pairs={{0,25},{1,24},{2,27},{3,26},{4,29},{5,28},{6,31},{7,30},{8,17},{9,... | collective-permute-start | bytes 454664 | tf_op jit(solution)/shard_map/ppermute | solution.py:380
  10.7 6.9 %collective-permute-start.4 = (bf16[37,4,256]{2,1,0:T(4,128)(2,1)}, bf16[37,4,256]{2,1,0:T(4,128)(2,1)S(1)}, u32[]{:S(2)}, u32[]{:S(2)}) collective-permute-start(bf16[37,4,256]{2,1,0:T(4,128)(2,1)} %get-tuple-element.17.r0), channel_id=1, source_target_pairs={{0,64},{8,72},{16,80},{24,88},{32,96},{40,104},{48,112},{56,120},{... | collective-permute-start | bytes 227336 | tf_op jit(solution)/shard_map/ppermute | solution.py:371
  11.3 7.3 %copy-start.7 = (bf16[37,4,256]{2,1,0:T(4,128)(2,1)}, bf16[37,4,256]{2,1,0:T(4,128)(2,1)S(1)}, u32[]{:S(2)}) copy-start(bf16[37,4,256]{2,1,0:T(4,128)(2,1)S(1)} %collective-permute-done.3.r1) | copy-start | bytes 227332
  11.3 7.2 %collective-permute-start.5 = (bf16[37,4,256]{2,1,0:T(4,128)(2,1)}, bf16[37,4,256]{2,1,0:T(4,128)(2,1)S(1)}, u32[]{:S(2)}, u32[]{:S(2)}) collective-permute-start(bf16[37,4,256]{2,1,0:T(4,128)(2,1)} %get-tuple-element.17.r0), channel_id=1, source_target_pairs={{0,32},{8,40},{16,48},{24,56},{32,64},{40,72},{48,80},{56,88},{64,... | collective-permute-start | bytes 227336 | tf_op jit(solution)/shard_map/ppermute | solution.py:371
  17.6 1.0 %copy-start.8 = (bf16[37,4,256]{2,1,0:T(4,128)(2,1)}, bf16[37,4,256]{2,1,0:T(4,128)(2,1)S(1)}, u32[]{:S(2)}) copy-start(bf16[37,4,256]{2,1,0:T(4,128)(2,1)S(1)} %collective-permute-done.4.r2) | copy-start | bytes 227332
  18.5 0.6 copy-start.9
  18.5 0.7 copy-start
  18.5 0.7 %copy-start.1 = (bf16[37,8,256]{2,1,0:T(8,128)(2,1)}, bf16[37,8,256]{2,1,0:T(8,128)(2,1)S(1)}, u32[]{:S(2)}) copy-start(bf16[37,8,256]{2,1,0:T(8,128)(2,1)S(1)} %collective-permute-done.1.i2) | copy-start | bytes 454660
  18.6 0.8 %copy-start.2 = (bf16[37,8,256]{2,1,0:T(8,128)(2,1)}, bf16[37,8,256]{2,1,0:T(8,128)(2,1)S(1)}, u32[]{:S(2)}) copy-start(bf16[37,8,256]{2,1,0:T(8,128)(2,1)S(1)} %collective-permute-done.2.i3) | copy-start | bytes 454660
  36.0 15.3 %all-to-all-start = ((f32[32,2,128]{2,1,0:T(2,128)}), f32[32,2,128]{2,1,0:T(2,128)S(1)}, u32[]{:S(2)}, u32[]{:S(2)}) async-start(f32[32,2,128]{2,1,0:T(2,128)} %get-tuple-element.19.pair_ref), calls=%async_computation | async-start | bytes 65536 | tf_op jit(solution)/shard_map/all_to_all | solution.py:395
  51.4 0.6 copy-start.3
  59.1 7.4 %collective-permute-start.6 = (bf16[38,4,256]{2,1,0:T(4,128)(2,1)}, bf16[38,4,256]{2,1,0:T(4,128)(2,1)S(1)}, u32[]{:S(2)}, u32[]{:S(2)}) collective-permute-start(bf16[38,4,256]{2,1,0:T(4,128)(2,1)} %get-tuple-element.23), channel_id=1, source_target_pairs={{0,32},{8,40},{16,48},{24,56},{32,64},{40,72},{48,80},{56,88},{64,... | collective-permute-start | bytes 233480 | tf_op jit(solution)/shard_map/ppermute | solution.py:371
  59.1 7.4 %collective-permute-start.7 = (bf16[38,4,256]{2,1,0:T(4,128)(2,1)}, bf16[38,4,256]{2,1,0:T(4,128)(2,1)S(1)}, u32[]{:S(2)}, u32[]{:S(2)}) collective-permute-start(bf16[38,4,256]{2,1,0:T(4,128)(2,1)} %get-tuple-element.24), channel_id=1, source_target_pairs={{0,64},{8,72},{16,80},{24,88},{32,96},{40,104},{48,112},{56,120},{... | collective-permute-start | bytes 233480 | tf_op jit(solution)/shard_map/ppermute | solution.py:371
  61.1 5.9 %collective-permute-start.8 = (bf16[38,4,256]{2,1,0:T(4,128)(2,1)}, bf16[38,4,256]{2,1,0:T(4,128)(2,1)S(1)}, u32[]{:S(2)}, u32[]{:S(2)}) collective-permute-start(bf16[38,4,256]{2,1,0:T(4,128)(2,1)} %get-tuple-element.25), channel_id=1, source_target_pairs={{0,96},{8,104},{16,112},{24,120},{32,0},{40,8},{48,16},{56,24},{64... | collective-permute-start | bytes 233480 | tf_op jit(solution)/shard_map/ppermute | solution.py:371
  66.5 0.6 copy-start.4
  66.5 0.6 copy-start.5
  67.1 0.6 copy-start.6

commit v2 on v1

v2 whole, which is shorter than its diff:
```python
import functools
import math

import jax
import jax.numpy as jnp
import ml_dtypes
import numpy as np
from jax import lax
from jax.experimental import pallas as pl
from jax.experimental.pallas import tpu as pltpu
from jax.sharding import PartitionSpec as P

TRANS = 4
CYCLES = 32
ANG = 144
ROT = 36
NDEF = 16
STEP = ANG // ROT
PAIRS = 2 * CYCLES
LANES = 2 * STEP * CYCLES
HALF = LANES // 2
OWN = 4
MINE = 8
BLOCKS = 4
KS = OWN * BLOCKS
US = MINE * BLOCKS * TRANS
ROWS = ROT * KS
REACH = 3
offset_sigma = 2.0
F32 = jnp.float32
BF16 = jnp.bfloat16
HIGHEST = lax.Precision.HIGHEST
VMEM_LIMIT = 24 * 1024 * 1024


def phase_parts():
    span = 2 * REACH + 1
    theta = 2.0 * math.pi * np.arange(ANG).reshape(ROT, STEP) / ANG
    radius = np.arange(CYCLES) + 1.0
    fx = (np.cos(theta)[:, :, None] * radius).reshape(ROT, HALF)
    fy = (np.sin(theta)[:, :, None] * radius).reshape(ROT, HALF)
    shift = np.arange(span) - REACH
    phi = (
        -2.0
        * math.pi
        * (shift[:, None, None, None] * fx + shift[None, :, None, None] * fy)
        / (2.0 * CYCLES)
    ).reshape(span * span, ROT, HALF)
    table = np.concatenate([np.cos(phi), np.sin(phi)], axis=2).transpose(1, 0, 2)
    table = np.pad(table, ((0, 0), (0, 64 - span * span), (0, 0)))
    parts = []
    rest = table
    for _ in range(3):
        part = rest.astype(np.float32).astype(ml_dtypes.bfloat16)
        parts.append(part)
        rest = rest - part.astype(np.float64)
    return np.concatenate(parts, axis=1)


def nt(a, b, **kw):
    return lax.dot_general(a, b, (((1,), (1,)), ((), ())), preferred_element_type=F32, **kw)


def in_hbm(value):
    return pltpu.with_memory_space_constraint(value, pltpu.HBM)


def fetch(pairs, sems):
    copies = [
        pltpu.make_async_copy(src, dst, sems.at[n]) for n, (src, dst) in enumerate(pairs)
    ]
    for copy in copies:
        copy.start()
    return copies


def as_column(row, size):
    here = lax.broadcasted_iota(jnp.int32, (size, size), 0)
    there = lax.broadcasted_iota(jnp.int32, (size, size), 1)
    wide = jnp.broadcast_to(row, (size, size))
    return jnp.sum(jnp.where(here == there, wide, 0.0), axis=1, keepdims=True)


def as_row(column, size):
    here = lax.broadcasted_iota(jnp.int32, (size, size), 0)
    there = lax.broadcasted_iota(jnp.int32, (size, size), 1)
    wide = jnp.broadcast_to(column, (size, size))
    return jnp.sum(jnp.where(here == there, wide, 0.0), axis=0, keepdims=True)


def turn_major(source, count, cut, flat, out):
    angle = lax.broadcasted_iota(jnp.int32, (CYCLES, ANG), 1) % STEP
    pick_b = lax.broadcasted_iota(jnp.int32, (40, ANG), 0)
    pick_a = lax.broadcasted_iota(jnp.int32, (40, ANG), 1)
    pick = jnp.where(pick_a // STEP == pick_b, 1.0, 0.0).astype(BF16)
    for j in range(PAIRS):
        line = source[:, j * ANG : (j + 1) * ANG].astype(F32)
        cut[0, pl.ds(j * 8, count), :] = line[:, :HALF]
        cut[1, pl.ds(j * 8, count), : ANG - HALF] = line[:, HALF:]
    for i in range(count):
        one = jnp.concatenate(
            [cut.at[n][pl.ds(i, PAIRS, stride=8), :] for n in range(2)], axis=1
        )[:, :ANG]
        spread = jnp.concatenate(
            [
                jnp.where(angle == c, one[p * CYCLES : (p + 1) * CYCLES], 0.0)
                for p in range(2)
                for c in range(STEP)
            ],
            axis=0,
        ).astype(BF16)
        turned = nt(pick, spread)
        flat[0, pl.ds(i * 40, 40), :] = turned[:, :HALF]
        flat[1, pl.ds(i * 40, 40), :] = turned[:, HALF:]
    for b in range(ROT):
        for n in range(2):
            line = flat.at[n][pl.ds(b, count, stride=40), :]
            out[b, :, n * HALF : (n + 1) * HALF] = line.astype(BF16)


def arrange_kernel(
    img_hbm, ref_hbm, prior_hbm, off_hbm, def_hbm, img_out, ref_out,
    img_ref, ref_ref, prior_ref, off_ref, def_ref, cut, cut2, flat, flat2, sems,
):
    copies = fetch(
        (
            (ref_hbm, ref_ref),
            (img_hbm, img_ref),
            (prior_hbm, prior_ref),
            (off_hbm, off_ref),
            (def_hbm, def_ref),
        ),
        sems,
    )
    copies[0].wait()
    turn_major(ref_ref, OWN, cut, flat, ref_out)
    copies[1].wait()
    turn_major(img_ref, MINE, cut2, flat2, img_out)
    for copy in copies[2:]:
        copy.wait()
    lane = lax.broadcasted_iota(jnp.int32, (MINE, LANES), 1)
    extra = jnp.where(lane == 8, as_column(def_ref[...].astype(F32), MINE), 0.0)
    for t in range(TRANS):
        for d in range(2):
            column = as_column(off_ref[t, d : d + 1, :].astype(F32), MINE)
            extra = jnp.where(lane == 2 * t + d, column, extra)
    img_out[ROT] = extra.astype(BF16)
    column = as_column(prior_ref[...].astype(F32), OWN)
    ref_out[ROT] = jnp.broadcast_to(column, (OWN, LANES)).astype(BF16)


def arrange(images, references, prior, offsets, defocus):
    vmem = pl.BlockSpec(memory_space=pltpu.VMEM)
    hbm = pl.BlockSpec(memory_space=pltpu.HBM)
    wide = 2 * CYCLES * ANG
    return pl.pallas_call(
        arrange_kernel,
        out_shape=(
            jax.ShapeDtypeStruct((ROT + 1, MINE, LANES), BF16),
            jax.ShapeDtypeStruct((ROT + 1, OWN, LANES), BF16),
        ),
        in_specs=[hbm] * 5,
        out_specs=(vmem, vmem),
        scratch_shapes=[
            pltpu.VMEM((MINE, wide), BF16),
            pltpu.VMEM((OWN, wide), BF16),
            pltpu.VMEM((1, OWN), BF16),
            pltpu.VMEM((TRANS, 2, MINE), jnp.int32),
            pltpu.VMEM((1, MINE), jnp.int32),
            pltpu.VMEM((2, PAIRS * 8, HALF), F32),
            pltpu.VMEM((2, PAIRS * 8, HALF), F32),
            pltpu.VMEM((2, MINE * 40, HALF), F32),
            pltpu.VMEM((2, MINE * 40, HALF), F32),
            pltpu.SemaphoreType.DMA((5,)),
        ],
        compiler_params=pltpu.CompilerParams(vmem_limit_bytes=VMEM_LIMIT),
        name="arrange",
    )(*(in_hbm(v) for v in (images, references, prior, offsets, defocus)))


def score_kernel(
    own_ref,
    i0, i2, i13,
    r0, r1, r2, r3,
    ctf_hbm, noise_hbm, table_hbm,
    exp_out, stat_out, ins_out, sq_out,
    ctf_ref, noise_ref, table, pictures, back, acc, sems,
):
    chunk = ROT // 6
    copies = fetch(
        [(ctf_hbm, ctf_ref), (noise_hbm, noise_ref)]
        + [(table_hbm.at[pl.ds(n * chunk, chunk)], table.at[pl.ds(n * chunk, chunk)]) for n in range(6)],
        sems,
    )
    own = own_ref[0]
    for step, source in enumerate((i0, i13.at[0], i2, i13.at[1])):
        pictures[own ^ step] = source[...]
    square = jnp.zeros((KS, LANES), F32)
    for b in range(ROT):
        block = jnp.concatenate([r[b].astype(F32) for r in (r0, r1, r2, r3)], axis=0)
        square = square + block * block
        m = (ROT - b) % ROT
        back[pl.ds(m * KS, KS), :] = block.astype(BF16)
        back[pl.ds((m + ROT) * KS, KS), :] = block.astype(BF16)
    prior = jnp.concatenate([r[ROT].astype(F32) for r in (r0, r1, r2, r3)], axis=0)[:, :HALF]

    extra = jnp.concatenate([pictures[k, ROT].astype(F32) for k in range(BLOCKS)], axis=0)
    dx = jnp.concatenate([extra[:, 2 * t : 2 * t + 1] for t in range(TRANS)], axis=0)
    dy = jnp.concatenate([extra[:, 2 * t + 1 : 2 * t + 2] for t in range(TRANS)], axis=0)
    combo = (dx + REACH) * (2 * REACH + 1) + (dy + REACH)
    slot = lax.broadcasted_iota(jnp.int32, (US, 192), 1) % 64
    hot = jnp.where(slot.astype(F32) == combo, 1.0, 0.0).astype(BF16)
    group = lax.broadcasted_iota(jnp.int32, (MINE * BLOCKS, NDEF), 1).astype(F32)
    which = jnp.where(group == extra[:, 8:9], 1.0, 0.0)
    copies[0].wait()
    copies[1].wait()
    ctf4 = jnp.concatenate([ctf_ref[...]] * STEP, axis=1)
    contrast = jnp.dot(which, ctf4, precision=HIGHEST, preferred_element_type=F32)
    noise = jnp.concatenate([noise_ref[...]] * STEP, axis=1)
    whiten = contrast / noise
    squared = contrast * contrast
    coef = squared / (2.0 * noise)
    four = lambda v: jnp.concatenate([v] * TRANS, axis=0)
    sq_out[:, :HALF] = four(squared)
    sq_out[:, HALF:] = jnp.ones((US, HALF), F32)
    coef_rows = four(jnp.concatenate([coef, coef], axis=1))
    penalty = nt(square, coef_rows, precision=HIGHEST)
    near = -(dx * dx + dy * dy) / (2.0 * offset_sigma * offset_sigma)
    near_row = as_row(near, US)
    base = prior - penalty + near_row

    contrast4 = four(contrast)
    whiten4 = four(whiten)
    cross = None
    for h in range(ROT // 2):
        pair = []
        for b in (2 * h, 2 * h + 1):
            if b % chunk == 0:
                copies[2 + b // chunk].wait()
            turn = jnp.dot(hot, table[b], preferred_element_type=F32)
            cosine, sine = turn[:, :HALF], turn[:, HALF:]
            block = jnp.concatenate([pictures[k, b].astype(F32) for k in range(BLOCKS)], axis=0)
            real, imag = four(block[:, :HALF]), four(block[:, HALF:])
            shifted_real = real * cosine - imag * sine
            shifted_imag = real * sine + imag * cosine
            rows = slice(b * US, (b + 1) * US)
            ins_out[rows, :HALF] = (shifted_real * contrast4).astype(BF16)
            ins_out[rows, HALF:] = (shifted_imag * contrast4).astype(BF16)
            both = [shifted_real * whiten4, shifted_imag * whiten4]
            pair.append(jnp.concatenate(both, axis=1).astype(BF16))
        part = nt(
            back[(ROT - 2 * h) * KS : (2 * ROT - 2 * h) * KS, :], jnp.concatenate(pair, axis=0)
        )
        cross = part if cross is None else cross + part
    acc[...] = cross

    peak = jnp.full((KS, US), -jnp.inf, F32)
    for r in range(ROT):
        last = (r - 1) % ROT
        logp = acc[r * KS : (r + 1) * KS, :HALF] + acc[last * KS : (last + 1) * KS, HALF:] + base
        exp_out[r * KS : (r + 1) * KS, :] = logp
        peak = jnp.maximum(peak, logp)
    peak = jnp.max(peak, axis=0, keepdims=True)
    peak = jnp.broadcast_to(peak, (8, US))
    peak = jnp.maximum(peak, pltpu.roll(peak, 32, 1))
    peak = jnp.maximum(peak, pltpu.roll(peak, 64, 1))
    wide = jnp.broadcast_to(peak[:1], (KS, US))
    total = jnp.zeros((KS, US), F32)
    for r in range(ROT):
        value = jnp.exp(exp_out[r * KS : (r + 1) * KS, :] - wide)
        exp_out[r * KS : (r + 1) * KS, :] = value
        total = total + value
    total = jnp.broadcast_to(jnp.sum(total, axis=0, keepdims=True), (8, US))
    total = total + pltpu.roll(total, 32, 1)
    total = total + pltpu.roll(total, 64, 1)
    pair = jnp.concatenate([peak[:1], total[:1]], axis=0)[:, : US // TRANS]
    for j in range(32):
        stat_out[j] = pair


def score(own, imgs, refs, ctf_table, noise_power, table):
    vmem = pl.BlockSpec(memory_space=pltpu.VMEM)
    smem = pl.BlockSpec(memory_space=pltpu.SMEM)
    return pl.pallas_call(
        score_kernel,
        out_shape=(
            jax.ShapeDtypeStruct((ROWS, US), F32),
            jax.ShapeDtypeStruct((32, 2, US // TRANS), F32),
            jax.ShapeDtypeStruct((ROT * US, LANES), BF16),
            jax.ShapeDtypeStruct((US, LANES), F32),
        ),
        in_specs=[smem] + [vmem] * 7 + [pl.BlockSpec(memory_space=pltpu.HBM)] * 3,
        out_specs=(vmem,) * 4,
        scratch_shapes=[
            pltpu.VMEM((NDEF, CYCLES), F32),
            pltpu.VMEM((1, CYCLES), F32),
            pltpu.VMEM((ROT, 192, LANES), BF16),
            pltpu.VMEM((BLOCKS, ROT + 1, MINE, LANES), BF16),
            pltpu.VMEM((2 * ROWS, LANES), BF16),
            pltpu.VMEM((ROWS, LANES), F32),
            pltpu.SemaphoreType.DMA((8,)),
        ],
        compiler_params=pltpu.CompilerParams(vmem_limit_bytes=VMEM_LIMIT),
        name="score",
    )(own, *imgs, *refs, *(in_hbm(v) for v in (ctf_table, noise_power, table)))


def insert_kernel(own_ref, exp_ref, pair_ref, all_ref, ins_ref, sq_ref, own_out, s1, s2, s3, like_out, post, acc):
    peaks = jnp.concatenate([all_ref[j, 0:1, :] for j in range(32)], axis=0)
    totals = jnp.concatenate([all_ref[j, 1:2, :] for j in range(32)], axis=0)
    peak = jnp.max(peaks, axis=0, keepdims=True)
    total = jnp.sum(totals * jnp.exp(peaks - peak), axis=0, keepdims=True)
    scale = jnp.exp(pair_ref[0, 0:1, :] - peak) / total
    scale = jnp.broadcast_to(jnp.concatenate([scale] * TRANS, axis=1), (KS, US))
    like = jnp.concatenate([peak + jnp.log(total)] * TRANS, axis=1)
    shift = (US - own_ref[0] * MINE) % US
    like_out[...] = pltpu.roll(jnp.broadcast_to(like, (8, US)), shift, 1)[:1, :MINE]
    count = jnp.zeros((KS, US), F32)
    for r in range(ROT):
        value = (exp_ref[r * KS : (r + 1) * KS, :] * scale).astype(BF16)
        count = count + value.astype(F32)
        for side in range(2):
            m = (side - r) % ROT
            for again in (m, m + ROT):
                post[again * KS : (again + 1) * KS, side * HALF : (side + 1) * HALF] = value

    acc[...] = sum(
        jnp.dot(
            post[(ROT - 2 * h) * KS : (2 * ROT - 2 * h) * KS, :],
            ins_ref[h * 2 * US : (h + 1) * 2 * US, :],
            preferred_element_type=F32,
        )
        for h in range(ROT // 2)
    )
    sums = jnp.dot(count, sq_ref[...], precision=HIGHEST, preferred_element_type=F32)
    high = sums.astype(BF16)
    low = (sums - high.astype(F32)).astype(BF16)
    for b in range(ROT):
        block = acc[b * KS : (b + 1) * KS, :]
        own_out[b] = block[:OWN]
        for d, out in ((1, s1), (2, s2), (3, s3)):
            out[b] = block[d * OWN : (d + 1) * OWN].astype(BF16)
    own_out[ROT] = sums[:OWN]
    own_out[ROT + 1] = jnp.zeros((OWN, LANES), F32)
    for d, out in ((1, s1), (2, s2), (3, s3)):
        part = sums[d * OWN : (d + 1) * OWN]
        high = part.astype(BF16)
        out[ROT] = high
        out[ROT + 1] = (part - high.astype(F32)).astype(BF16)


def insert(own, exps, stats, gathered, ins, sq):
    vmem = pl.BlockSpec(memory_space=pltpu.VMEM)
    smem = pl.BlockSpec(memory_space=pltpu.SMEM)
    piece = (ROT + 2, OWN, LANES)
    return pl.pallas_call(
        insert_kernel,
        out_shape=(
            jax.ShapeDtypeStruct(piece, F32),
            jax.ShapeDtypeStruct(piece, BF16),
            jax.ShapeDtypeStruct(piece, BF16),
            jax.ShapeDtypeStruct(piece, BF16),
            jax.ShapeDtypeStruct((1, MINE), F32),
        ),
        in_specs=[smem] + [vmem] * 5,
        out_specs=(vmem,) * 5,
        scratch_shapes=[
            pltpu.VMEM((2 * ROWS, LANES), BF16),
            pltpu.VMEM((ROWS, LANES), F32),
        ],
        compiler_params=pltpu.CompilerParams(vmem_limit_bytes=VMEM_LIMIT),
        name="insert",
    )(own, exps, stats, gathered, ins, sq)


def finish_kernel(own_ref, g1, g2, g3, tau_ref, out_ref, weight_out, fresh, turned, lines):
    parts = [own_ref, g1, g2, g3]
    sums = sum(p[ROT].astype(F32) + p[ROT + 1].astype(F32) for p in parts)
    tau = jnp.concatenate([tau_ref[...]] * STEP, axis=1)
    denom = sums[:, :HALF] + 1.0 / tau
    denom = jnp.concatenate([denom, denom], axis=1)
    weight_out[...] = as_row(sums[:, HALF : HALF + 1], OWN) / (MINE * 16)
    for b in range(ROT):
        total = own_ref[b] + g1[b].astype(F32) + g2[b].astype(F32) + g3[b].astype(F32)
        total = total / denom
        fresh[0, pl.ds(b * 8, OWN), :] = total[:, :HALF]
        fresh[1, pl.ds(b * 8, OWN), :] = total[:, HALF:]
    for k in range(OWN):
        one = [fresh.at[p][pl.ds(k, ROT, stride=8), :] for p in range(2)]
        for c in range(STEP):
            pair = [one[p][:, c * CYCLES : (c + 1) * CYCLES] for p in range(2)]
            turned[pl.ds(c, ROT, stride=STEP), :] = jnp.concatenate(pair + pair, axis=1)
        first = turned[0:128, :].T
        second = turned[128:256, :].T
        lines[0, pl.ds(k * PAIRS, PAIRS), :] = first[:PAIRS]
        lines[1, pl.ds(k * PAIRS, PAIRS), :] = second[:PAIRS]
    for j in range(PAIRS):
        line = [lines.at[n][pl.ds(j, OWN, stride=PAIRS), :] for n in range(2)]
        out_ref[:, j * ANG : (j + 1) * ANG] = jnp.concatenate(line, axis=1)[:, :ANG]


def finish(own, got, tau):
    vmem = pl.BlockSpec(memory_space=pltpu.VMEM)
    return pl.pallas_call(
        finish_kernel,
        out_shape=(
            jax.ShapeDtypeStruct((OWN, 2 * CYCLES * ANG), F32),
            jax.ShapeDtypeStruct((1, OWN), F32),
        ),
        in_specs=[vmem] * 5,
        out_specs=(vmem, vmem),
        scratch_shapes=[
            pltpu.VMEM((2, ROT * 8, HALF), F32),
            pltpu.VMEM((256, 128), F32),
            pltpu.VMEM((2, OWN * PAIRS, HALF), F32),
        ],
        compiler_params=pltpu.CompilerParams(vmem_limit_bytes=VMEM_LIMIT),
        name="finish",
    )(own, *got, tau)


def along_y(value, distance):
    return lax.ppermute(
        value, "img", [(i, ((i // 4 + distance) % 4) * 4 + i % 4) for i in range(16)]
    )


def beside(value, img_flip, cls_flip):
    pairs = [
        (i * 8 + c, (i ^ img_flip) * 8 + (c ^ cls_flip)) for i in range(16) for c in range(8)
    ]
    return lax.ppermute(value, ("img", "cls"), pairs)


def per_device(
    table, images, references, class_logprior, ctf_table, noise_power, tau_power, defocus, offsets
):
    own = (lax.axis_index("img") % BLOCKS).astype(jnp.int32).reshape(1)
    img, ref = arrange(
        images,
        references,
        class_logprior.reshape(1, OWN),
        offsets.transpose(1, 2, 0),
        defocus.reshape(1, MINE),
    )
    next_chip = beside(img, 2, 1)
    refs = (ref, along_y(ref, 3), along_y(ref, 2), along_y(ref, 1))
    next_chip, refs = lax.optimization_barrier((next_chip, refs))
    other_core = beside(jnp.stack([img, next_chip]), 1, 0)
    exps, stats, ins, sq = score(
        own, (img, next_chip, other_core), refs, ctf_table, noise_power.reshape(1, CYCLES), table
    )
    same_images = [[(y * 4 + r) * 8 + c for r in range(4) for c in range(8)] for y in range(4)]
    gathered = lax.all_to_all(
        stats, ("img", "cls"), 0, 0, tiled=True, axis_index_groups=same_images
    )
    numer, s1, s2, s3, like = insert(own, exps, stats, gathered, ins, sq)
    got = (along_y(s1, 1), along_y(s2, 2), along_y(s3, 3))
    fresh, weight = finish(numer, got, tau_power.reshape(1, CYCLES))
    return fresh, weight.reshape(OWN), like.reshape(MINE)


def solution(mesh):
    body = functools.partial(per_device, jnp.asarray(phase_parts()))
    return jax.shard_map(
        body,
        mesh=mesh,
        in_specs=(
            P("img", None),
            P(("img", "cls"), None),
            P(("img", "cls")),
            P(),
            P(),
            P(),
            P("img"),
            P("img", None, None),
        ),
        out_specs=(P(("img", "cls"), None), P(("img", "cls")), P("img")),
        check_vma=False,
    )
```

time: 71.7 us -> 47.6 us (0.66)
  Pallas kernels: 28.6 us -> 11.7 us
  blocking collectives: 0 us -> 13.2 us
  local copies, waits for them, and re-layouts: 9.1 us -> 0.01 us
  starting transfers between devices: 19 us -> 13.1 us
  waiting for transfers between devices: 13.9 us -> 8.78 us
    all_to_all x0 -> x1, blocking collectives: none -> 13.2 us  [per_device(): lax.all_to_all(stats, ('img', 'cls'), 0, 0, tiled=True, axis_index_groups...]
    pallas_call x1, Pallas kernels: 16.7 us -> 6.2 us  [score(): pl.pallas_call(score_kernel, out_shape=(jax.ShapeDtypeStruct((ROWS, US),...]
    all_to_all x1 -> x0, starting transfers between devices: 7.91 us -> none  [per_device(): lax.all_to_all(stats, ('img', 'cls'), 0, 0, tiled=True, axis_index_groups...]
    all_to_all x1 -> x0, waiting for transfers between devices: 6.82 us -> none  [per_device(): lax.all_to_all(stats, ('img', 'cls'), 0, 0, tiled=True, axis_index_groups...]
    pallas_call x1, Pallas kernels: 7.11 us -> 2.19 us  [insert(): pl.pallas_call(insert_kernel, out_shape=(jax.ShapeDtypeStruct(piece, F32)...]
    unnamed x23 -> x2, local copies, waits for them, and re-layouts: 3.38 us -> 0.01 us
    another operation x6 -> x0, local copies, waits for them, and re-layouts: 3.23 us -> none  [the longest x2 1.38 us: per_device(): ctf4 = jnp.tile(ctf_table, (1, STEP))]
    ppermute x6, starting transfers between devices: 8.03 us -> 10.1 us  [along_y(): lax.ppermute(value, 'img', [(i, (i // 4 + distance) % 4 * 4 + i % 4) for...]
  transfers between devices with their start and end apart: 10 -> 8, of which waited for: 5 -> 7; matrix products, arithmetic and copies ran while one was open for 6% -> 0% of each run, Pallas kernels for 0% -> 0%
where the time goes in v2:
time: 47.6 us; the launch traced here: 47.5 us
  blocking collectives  13.2 us (28%)
  starting transfers between devices  13.1 us (28%)
  Pallas kernels  11.7 us (25%)
  waiting for transfers between devices  8.78 us (18%)
  between operations  0.68 us (1%)
    all_to_all x1, blocking collectives, per_device(): lax.all_to_all(stats, ('img', 'cls'), 0, 0, tiled=True, axis_index_groups...  13.2 us
    ppermute x6, starting transfers between devices, along_y(): lax.ppermute(value, 'img', [(i, (i // 4 + distance) % 4 * 4 + i % 4) for...  10.1 us
    ppermute x6, waiting for transfers between devices, along_y(): lax.ppermute(value, 'img', [(i, (i // 4 + distance) % 4 * 4 + i % 4) for...  7.21 us
    pallas_call x1, Pallas kernels, score(): pl.pallas_call(score_kernel, out_shape=(jax.ShapeDtypeStruct((ROWS, US),...  6.2 us
    ppermute x2, starting transfers between devices, beside(): return lax.ppermute(value, ('img', 'cls'), pairs)  3.01 us
    pallas_call x1, Pallas kernels, insert(): pl.pallas_call(insert_kernel, out_shape=(jax.ShapeDtypeStruct(piece, F32)...  2.19 us
    pallas_call x1, Pallas kernels, arrange(): pl.pallas_call(arrange_kernel, out_shape=(jax.ShapeDtypeStruct((ROT + 1,...  2.03 us
    ppermute x2, waiting for transfers between devices, beside(): return lax.ppermute(value, ('img', 'cls'), pairs)  1.57 us
  transfers between devices with their start and end apart: 8, of which 7 were waited for; matrix products, arithmetic and copies ran while one was open for 0% of the time, Pallas kernels for 0%

profile of v2, /device:TPU:0, one launch (start us, length us, event | category | flops | bytes accessed | tf_op | source)
XLA Modules:
  0.0 47.5 jit_solution(6135032719518167531)
XLA Ops:
  0.6 2.0 %arrange.1 = (bf16[37,8,256]{2,1,0:T(8,128)(2,1)S(1)}, bf16[37,4,256]{2,1,0:T(4,128)(2,1)S(1)}) custom-call(bf16[8,9216]{1,0:T(8,128)(2,1)} %img_hbm.1, bf16[4,9216]{1,0:T(4,128)(2,1)} %ref_hbm.1, bf16[1,4]{1,0:T(2,128)(2,1)} %bitcast.14, s32[4,2,8]{2,1,0:T(2,128)} %bitcast.13, s32[1,8]{1,0:T(1,128)} %bitcast.15), custom_call_target="tpu_custom_call" | custom-call | tf_op jit(solution)/shard_map/arrange/pallas_call | solution.py:156
  2.7 2.9 %collective-permute-start = (bf16[37,8,256]{2,1,0:T(8,128)(2,1)S(1)}, bf16[37,8,256]{2,1,0:T(8,128)(2,1)S(1)}, u32[]{:S(2)}, u32[]{:S(2)}) collective-permute-start(bf16[37,8,256]{2,1,0:T(8,128)(2,1)S(1)} %get-tuple-element.21.i0), channel_id=1, source_target_pairs={{0,17},{1,16},{2,19},{3,18},{4,21},{5,20},{6,23},{7,22},{8,25},{9,... | collective-permute-start | bytes 454664 | tf_op jit(solution)/shard_map/ppermute | solution.py:432
  5.6 1.6 %collective-permute-start.3 = (bf16[37,4,256]{2,1,0:T(4,128)(2,1)S(1)}, bf16[37,4,256]{2,1,0:T(4,128)(2,1)S(1)}, u32[]{:S(2)}, u32[]{:S(2)}) collective-permute-start(bf16[37,4,256]{2,1,0:T(4,128)(2,1)S(1)} %get-tuple-element.24.r0), channel_id=1, source_target_pairs={{0,32},{8,40},{16,48},{24,56},{32,64},{40,72},{48,80},{56,88},{64,... | collective-permute-start | bytes 227336 | tf_op jit(solution)/shard_map/ppermute | solution.py:423
  7.2 2.9 %collective-permute-start.2 = (bf16[37,4,256]{2,1,0:T(4,128)(2,1)S(1)}, bf16[37,4,256]{2,1,0:T(4,128)(2,1)S(1)}, u32[]{:S(2)}, u32[]{:S(2)}) collective-permute-start(bf16[37,4,256]{2,1,0:T(4,128)(2,1)S(1)} %get-tuple-element.24.r0), channel_id=1, source_target_pairs={{0,64},{8,72},{16,80},{24,88},{32,96},{40,104},{48,112},{56,120},{... | collective-permute-start | bytes 227336 | tf_op jit(solution)/shard_map/ppermute | solution.py:423
  10.1 1.3 %collective-permute-start.1 = (bf16[37,4,256]{2,1,0:T(4,128)(2,1)S(1)}, bf16[37,4,256]{2,1,0:T(4,128)(2,1)S(1)}, u32[]{:S(2)}, u32[]{:S(2)}) collective-permute-start(bf16[37,4,256]{2,1,0:T(4,128)(2,1)S(1)} %get-tuple-element.24.r0), channel_id=1, source_target_pairs={{0,96},{8,104},{16,112},{24,120},{32,0},{40,8},{48,16},{56,24},{64... | collective-permute-start | bytes 227336 | tf_op jit(solution)/shard_map/ppermute | solution.py:423
  11.4 0.6 %collective-permute-done.3.r3 = bf16[37,4,256]{2,1,0:T(4,128)(2,1)S(1)} collective-permute-done((bf16[37,4,256]{2,1,0:T(4,128)(2,1)S(1)}, bf16[37,4,256]{2,1,0:T(4,128)(2,1)S(1)}, u32[]{:S(2)}, u32[]{:S(2)}) %collective-permute-start.3) | collective-permute-done | bytes 75808 | tf_op jit(solution)/shard_map/ppermute | solution.py:423
  12.0 1.5 %collective-permute-done.2.r2 = bf16[37,4,256]{2,1,0:T(4,128)(2,1)S(1)} collective-permute-done((bf16[37,4,256]{2,1,0:T(4,128)(2,1)S(1)}, bf16[37,4,256]{2,1,0:T(4,128)(2,1)S(1)}, u32[]{:S(2)}, u32[]{:S(2)}) %collective-permute-start.2) | collective-permute-done | bytes 75808 | tf_op jit(solution)/shard_map/ppermute | solution.py:423
  13.4 1.0 %collective-permute-done.1.r1 = bf16[37,4,256]{2,1,0:T(4,128)(2,1)S(1)} collective-permute-done((bf16[37,4,256]{2,1,0:T(4,128)(2,1)S(1)}, bf16[37,4,256]{2,1,0:T(4,128)(2,1)S(1)}, u32[]{:S(2)}, u32[]{:S(2)}) %collective-permute-start.1) | collective-permute-done | bytes 75808 | tf_op jit(solution)/shard_map/ppermute | solution.py:423
  14.4 0.0 collective-permute-done.i2
  14.5 0.1 collective-permute-start.4
  14.6 1.6 %collective-permute-done.4.i13 = bf16[2,37,8,256]{3,2,1,0:T(8,128)(2,1)S(1)} collective-permute-done((bf16[2,37,8,256]{3,2,1,0:T(8,128)(2,1)S(1)}, bf16[2,37,8,256]{3,2,1,0:T(8,128)(2,1)S(1)}, u32[]{:S(2)}, u32[]{:S(2)}) %collective-permute-start.4) | collective-permute-done | bytes 303136 | tf_op jit(solution)/shard_map/ppermute | solution.py:432
  16.2 0.0 copy-start
  16.2 6.2 %score.1 = (f32[576,128]{1,0:T(8,128)S(1)}, f32[32,2,32]{2,1,0:T(2,128)S(1)}, bf16[4608,256]{1,0:T(8,128)(2,1)S(1)}, f32[128,256]{1,0:T(8,128)S(1)}) custom-call(s32[1]{0:T(128)} %bitcast.own_ref, bf16[37,8,256]{2,1,0:T(8,128)(2,1)S(1)} %get-tuple-element.21.i0, bf16[37,8,256]{2,1,0:T(8,128)(2,1)S(1)} %collective-permute-done.i2, ...), custom_call_target="tpu_custom_call" | custom-call | tf_op jit(solution)/shard_map/score/pallas_call | solution.py:284
  22.4 13.2 %all_to_all.5.all_ref = f32[32,2,32]{2,1,0:T(2,128)S(1)} all-to-all(f32[32,2,32]{2,1,0:T(2,128)S(1)} %get-tuple-element.29.pair_ref), channel_id=1, replica_groups={{0,1,2,3,4,5,6,7,8,9,10,11,12,13,14,15,16,17,18,19,20,21,22,23,24,25,26..., dimensions={0} | all-to-all | bytes 16384 | tf_op jit(solution)/shard_map/all_to_all | solution.py:454
  35.5 2.2 %insert.1 = (f32[38,4,256]{2,1,0:T(4,128)S(1)}, bf16[38,4,256]{2,1,0:T(4,128)(2,1)S(1)}, bf16[38,4,256]{2,1,0:T(4,128)(2,1)S(1)}, bf16[38,4,256]{2,1,0:T(4,128)(2,1)S(1)}, f32[1,8]{1,0:T(1,128)}) custom-call(s32[1]{0:T(128)} %bitcast.own_ref, f32[576,128]{1,0:T(8,128)S(1)} %get-tuple-element.28.exp_ref, f32[32,2,32]{2,1,0:T(2,128)S(1)} %get-tuple-element.29.pair_ref, ...), custom_call_target="tpu_custom_call" | custom-call | tf_op jit(solution)/shard_map/insert/pallas_call | solution.py:356
  37.7 0.4 collective-permute-start.5
  38.2 3.6 %collective-permute-start.6 = (bf16[38,4,256]{2,1,0:T(4,128)(2,1)S(1)}, bf16[38,4,256]{2,1,0:T(4,128)(2,1)S(1)}, u32[]{:S(2)}, u32[]{:S(2)}) collective-permute-start(bf16[38,4,256]{2,1,0:T(4,128)(2,1)S(1)} %get-tuple-element.34), channel_id=1, source_target_pairs={{0,64},{8,72},{16,80},{24,88},{32,96},{40,104},{48,112},{56,120},{... | collective-permute-start | bytes 233480 | tf_op jit(solution)/shard_map/ppermute | solution.py:423
  41.8 0.2 collective-permute-start.7
  42.0 1.4 %collective-permute-done.5.g1 = bf16[38,4,256]{2,1,0:T(4,128)(2,1)S(1)} collective-permute-done((bf16[38,4,256]{2,1,0:T(4,128)(2,1)S(1)}, bf16[38,4,256]{2,1,0:T(4,128)(2,1)S(1)}, u32[]{:S(2)}, u32[]{:S(2)}) %collective-permute-start.5) | collective-permute-done | bytes 77856 | tf_op jit(solution)/shard_map/ppermute | solution.py:423
  43.4 2.4 %collective-permute-done.6.g2 = bf16[38,4,256]{2,1,0:T(4,128)(2,1)S(1)} collective-permute-done((bf16[38,4,256]{2,1,0:T(4,128)(2,1)S(1)}, bf16[38,4,256]{2,1,0:T(4,128)(2,1)S(1)}, u32[]{:S(2)}, u32[]{:S(2)}) %collective-permute-start.6) | collective-permute-done | bytes 77856 | tf_op jit(solution)/shard_map/ppermute | solution.py:423
  45.8 0.4 collective-permute-done.7.g3
  46.2 0.0 copy-done
  46.2 1.3 %finish.1 = (f32[4,9216]{1,0:T(4,128)}, f32[1,4]{1,0:T(1,128)}) custom-call(f32[38,4,256]{2,1,0:T(4,128)S(1)} %get-tuple-element.32.own_ref, bf16[38,4,256]{2,1,0:T(4,128)(2,1)S(1)} %collective-permute-done.5.g1, bf16[38,4,256]{2,1,0:T(4,128)(2,1)S(1)} %collective-permute-done.6.g2, bf16[38,4,256]{2,1,0:T(4,128)(2,1)S(1)} %collective-permute-done.7.g3, ...), custom_call_target="tpu_custom_call" | custom-call | tf_op jit(solution)/shard_map/finish/pallas_call | solution.py:404
  (1 shorter events, 0.0 us)
Async XLA Ops:
  2.7 11.8 %collective-permute-start = (bf16[37,8,256]{2,1,0:T(8,128)(2,1)S(1)}, bf16[37,8,256]{2,1,0:T(8,128)(2,1)S(1)}, u32[]{:S(2)}, u32[]{:S(2)}) collective-permute-start(bf16[37,8,256]{2,1,0:T(8,128)(2,1)S(1)} %get-tuple-element.21.i0), channel_id=1, source_target_pairs={{0,17},{1,16},{2,19},{3,18},{4,21},{5,20},{6,23},{7,22},{8,25},{9,... | collective-permute-start | bytes 454664 | tf_op jit(solution)/shard_map/ppermute | solution.py:432
  5.6 6.4 %collective-permute-start.3 = (bf16[37,4,256]{2,1,0:T(4,128)(2,1)S(1)}, bf16[37,4,256]{2,1,0:T(4,128)(2,1)S(1)}, u32[]{:S(2)}, u32[]{:S(2)}) collective-permute-start(bf16[37,4,256]{2,1,0:T(4,128)(2,1)S(1)} %get-tuple-element.24.r0), channel_id=1, source_target_pairs={{0,32},{8,40},{16,48},{24,56},{32,64},{40,72},{48,80},{56,88},{64,... | collective-permute-start | bytes 227336 | tf_op jit(solution)/shard_map/ppermute | solution.py:423
  7.2 6.3 %collective-permute-start.2 = (bf16[37,4,256]{2,1,0:T(4,128)(2,1)S(1)}, bf16[37,4,256]{2,1,0:T(4,128)(2,1)S(1)}, u32[]{:S(2)}, u32[]{:S(2)}) collective-permute-start(bf16[37,4,256]{2,1,0:T(4,128)(2,1)S(1)} %get-tuple-element.24.r0), channel_id=1, source_target_pairs={{0,64},{8,72},{16,80},{24,88},{32,96},{40,104},{48,112},{56,120},{... | collective-permute-start | bytes 227336 | tf_op jit(solution)/shard_map/ppermute | solution.py:423
  10.1 4.4 %collective-permute-start.1 = (bf16[37,4,256]{2,1,0:T(4,128)(2,1)S(1)}, bf16[37,4,256]{2,1,0:T(4,128)(2,1)S(1)}, u32[]{:S(2)}, u32[]{:S(2)}) collective-permute-start(bf16[37,4,256]{2,1,0:T(4,128)(2,1)S(1)} %get-tuple-element.24.r0), channel_id=1, source_target_pairs={{0,96},{8,104},{16,112},{24,120},{32,0},{40,8},{48,16},{56,24},{64... | collective-permute-start | bytes 227336 | tf_op jit(solution)/shard_map/ppermute | solution.py:423
  14.5 1.7 %collective-permute-start.4 = (bf16[2,37,8,256]{3,2,1,0:T(8,128)(2,1)S(1)}, bf16[2,37,8,256]{3,2,1,0:T(8,128)(2,1)S(1)}, u32[]{:S(2)}, u32[]{:S(2)}) collective-permute-start(bf16[2,37,8,256]{3,2,1,0:T(8,128)(2,1)S(1)} %pad_maximum_fusion), channel_id=1, source_target_pairs={{0,8},{1,9},{2,10},{3,11},{4,12},{5,13},{6,14},{7,15},{8,0},{9,1},... | collective-permute-start | bytes 909320 | tf_op jit(solution)/shard_map/ppermute | solution.py:432
  16.2 30.0 %copy-start = (f32[32]{0:T(128)S(1)}, f32[32]{0:T(128)}, u32[]{:S(2)}) copy-start(f32[32]{0:T(128)} %param.14) | copy-start | bytes 388
  37.7 5.6 %collective-permute-start.5 = (bf16[38,4,256]{2,1,0:T(4,128)(2,1)S(1)}, bf16[38,4,256]{2,1,0:T(4,128)(2,1)S(1)}, u32[]{:S(2)}, u32[]{:S(2)}) collective-permute-start(bf16[38,4,256]{2,1,0:T(4,128)(2,1)S(1)} %get-tuple-element.33), channel_id=1, source_target_pairs={{0,32},{8,40},{16,48},{24,56},{32,64},{40,72},{48,80},{56,88},{64,... | collective-permute-start | bytes 233480 | tf_op jit(solution)/shard_map/ppermute | solution.py:423
  38.2 7.6 %collective-permute-start.6 = (bf16[38,4,256]{2,1,0:T(4,128)(2,1)S(1)}, bf16[38,4,256]{2,1,0:T(4,128)(2,1)S(1)}, u32[]{:S(2)}, u32[]{:S(2)}) collective-permute-start(bf16[38,4,256]{2,1,0:T(4,128)(2,1)S(1)} %get-tuple-element.34), channel_id=1, source_target_pairs={{0,64},{8,72},{16,80},{24,88},{32,96},{40,104},{48,112},{56,120},{... | collective-permute-start | bytes 233480 | tf_op jit(solution)/shard_map/ppermute | solution.py:423
  41.8 4.4 %collective-permute-start.7 = (bf16[38,4,256]{2,1,0:T(4,128)(2,1)S(1)}, bf16[38,4,256]{2,1,0:T(4,128)(2,1)S(1)}, u32[]{:S(2)}, u32[]{:S(2)}) collective-permute-start(bf16[38,4,256]{2,1,0:T(4,128)(2,1)S(1)} %get-tuple-element.35), channel_id=1, source_target_pairs={{0,96},{8,104},{16,112},{24,120},{32,0},{40,8},{48,16},{56,24},{64... | collective-permute-start | bytes 233480 | tf_op jit(solution)/shard_map/ppermute | solution.py:423

commit v3 on v2

--- a/solution.py
+++ b/solution.py
@@ -26,11 +26,13 @@
 US = MINE * BLOCKS * TRANS
 ROWS = ROT * KS
 REACH = 3
+MIDDLE = 24
+SLOTS = 32
 offset_sigma = 2.0
 F32 = jnp.float32
 BF16 = jnp.bfloat16
 HIGHEST = lax.Precision.HIGHEST
-VMEM_LIMIT = 24 * 1024 * 1024
+VMEM_LIMIT = 20 * 1024 * 1024
 
 
 def phase_parts():
@@ -45,9 +47,9 @@
         * math.pi
         * (shift[:, None, None, None] * fx + shift[None, :, None, None] * fy)
         / (2.0 * CYCLES)
-    ).reshape(span * span, ROT, HALF)
+    ).reshape(span * span, ROT, HALF)[MIDDLE:]
     table = np.concatenate([np.cos(phi), np.sin(phi)], axis=2).transpose(1, 0, 2)
-    table = np.pad(table, ((0, 0), (0, 64 - span * span), (0, 0)))
+    table = np.pad(table, ((0, 0), (0, SLOTS - table.shape[1]), (0, 0)))
     parts = []
     rest = table
     for _ in range(3):
@@ -119,8 +121,10 @@
 
 
 def arrange_kernel(
-    img_hbm, ref_hbm, prior_hbm, off_hbm, def_hbm, img_out, ref_out,
-    img_ref, ref_ref, prior_ref, off_ref, def_ref, cut, cut2, flat, flat2, sems,
+    img_hbm, ref_hbm, prior_hbm, off_hbm, def_hbm, ctf_hbm, noise_hbm, tau_hbm, table_hbm,
+    img_out, ref_out, ctf_out, noise_out, tau_out, table_out,
+    img_ref, ref_ref, prior_ref, off_ref, def_ref, ctf_ref, noise_ref, tau_ref,
+    cut, cut2, flat, flat2, sems,
 ):
     copies = fetch(
         (
@@ -129,6 +133,10 @@
             (prior_hbm, prior_ref),
             (off_hbm, off_ref),
             (def_hbm, def_ref),
+            (ctf_hbm, ctf_ref),
+            (noise_hbm, noise_ref),
+            (tau_hbm, tau_ref),
+            (table_hbm, table_out),
         ),
         sems,
     )
@@ -147,9 +155,11 @@
     img_out[ROT] = extra.astype(BF16)
     column = as_column(prior_ref[...].astype(F32), OWN)
     ref_out[ROT] = jnp.broadcast_to(column, (OWN, LANES)).astype(BF16)
-
-
-def arrange(images, references, prior, offsets, defocus):
+    for small, out in ((ctf_ref, ctf_out), (noise_ref, noise_out), (tau_ref, tau_out)):
+        out[...] = jnp.concatenate([small[...]] * STEP, axis=1)
+
+
+def arrange(images, references, prior, offsets, defocus, ctf_table, noise, tau, table):
     vmem = pl.BlockSpec(memory_space=pltpu.VMEM)
     hbm = pl.BlockSpec(memory_space=pltpu.HBM)
     wide = 2 * CYCLES * ANG
@@ -158,43 +168,137 @@
         out_shape=(
             jax.ShapeDtypeStruct((ROT + 1, MINE, LANES), BF16),
             jax.ShapeDtypeStruct((ROT + 1, OWN, LANES), BF16),
-        ),
-        in_specs=[hbm] * 5,
-        out_specs=(vmem, vmem),
+            jax.ShapeDtypeStruct((NDEF, HALF), F32),
+            jax.ShapeDtypeStruct((1, HALF), F32),
+            jax.ShapeDtypeStruct((1, HALF), F32),
+            jax.ShapeDtypeStruct((ROT, 3 * SLOTS, LANES), BF16),
+        ),
+        in_specs=[hbm] * 9,
+        out_specs=(vmem,) * 6,
         scratch_shapes=[
             pltpu.VMEM((MINE, wide), BF16),
             pltpu.VMEM((OWN, wide), BF16),
             pltpu.VMEM((1, OWN), BF16),
             pltpu.VMEM((TRANS, 2, MINE), jnp.int32),
             pltpu.VMEM((1, MINE), jnp.int32),
+            pltpu.VMEM((NDEF, CYCLES), F32),
+            pltpu.VMEM((1, CYCLES), F32),
+            pltpu.VMEM((1, CYCLES), F32),
             pltpu.VMEM((2, PAIRS * 8, HALF), F32),
             pltpu.VMEM((2, PAIRS * 8, HALF), F32),
             pltpu.VMEM((2, MINE * 40, HALF), F32),
             pltpu.VMEM((2, MINE * 40, HALF), F32),
-            pltpu.SemaphoreType.DMA((5,)),
+            pltpu.SemaphoreType.DMA((9,)),
         ],
         compiler_params=pltpu.CompilerParams(vmem_limit_bytes=VMEM_LIMIT),
         name="arrange",
-    )(*(in_hbm(v) for v in (images, references, prior, offsets, defocus)))
+    )(
+        *(
+            in_hbm(v)
+            for v in (images, references, prior, offsets, defocus, ctf_table, noise, tau, table)
+        )
+    )
+
+
+def four(value):
+    return jnp.concatenate([value] * TRANS, axis=0)
+
+
+def image_rows(near, far):
+    extra = jnp.concatenate([near[ROT].astype(F32), far[ROT].astype(F32)], axis=0)
+    dx = jnp.concatenate([extra[:, 2 * t : 2 * t + 1] for t in range(TRANS)], axis=0)
+    dy = jnp.concatenate([extra[:, 2 * t + 1 : 2 * t + 2] for t in range(TRANS)], axis=0)
+    return dx, dy, extra[:, 8:9]
+
+
+def contrast_of(group, ctf_ref):
+    known = lax.broadcasted_iota(jnp.int32, (group.shape[0], NDEF), 1).astype(F32)
+    which = jnp.where(known == group, 1.0, 0.0)
+    return jnp.dot(which, ctf_ref[...], precision=HIGHEST, preferred_element_type=F32)
+
+
+def shift_half(near, far, dx, dy, contrast, noise, table, weighted, inserted):
+    pair = dx * (2 * REACH + 1) + dy
+    slot = lax.broadcasted_iota(jnp.int32, (US // 2, 3 * SLOTS), 1) % SLOTS
+    hot = jnp.where(slot.astype(F32) == jnp.abs(pair), 1.0, 0.0).astype(BF16)
+    sign = jnp.broadcast_to(jnp.where(pair < 0, -1.0, 1.0), (US // 2, HALF))
+    contrast4 = four(contrast)
+    whiten4 = four(contrast / noise)
+    for b in range(ROT):
+        turn = jnp.dot(hot, table[b], preferred_element_type=F32)
+        cosine, sine = turn[:, :HALF], turn[:, HALF:] * sign
+        block = jnp.concatenate([near[b].astype(F32), far[b].astype(F32)], axis=0)
+        real, imag = four(block[:, :HALF]), four(block[:, HALF:])
+        shifted_real = real * cosine - imag * sine
+        shifted_imag = real * sine + imag * cosine
+        rows = slice(b * US // 2, (b + 1) * US // 2)
+        weighted[rows, :HALF] = (shifted_real * whiten4).astype(BF16)
+        weighted[rows, HALF:] = (shifted_imag * whiten4).astype(BF16)
+        inserted[rows, :HALF] = (shifted_real * contrast4).astype(BF16)
+        inserted[rows, HALF:] = (shifted_imag * contrast4).astype(BF16)
+
+
+def shift_kernel(near, far, ctf_ref, noise_ref, table, weighted, inserted):
+    dx, dy, group = image_rows(near, far)
+    contrast = contrast_of(group, ctf_ref)
+    shift_half(near, far, dx, dy, contrast, noise_ref[...], table, weighted, inserted)
+
+
+def shift(near, far, ctf4, noise4, table):
+    vmem = pl.BlockSpec(memory_space=pltpu.VMEM)
+    half = jax.ShapeDtypeStruct((ROT * US // 2, LANES), BF16)
+    return pl.pallas_call(
+        shift_kernel,
+        out_shape=(half, half),
+        in_specs=[vmem] * 5,
+        out_specs=(vmem, vmem),
+        compiler_params=pltpu.CompilerParams(vmem_limit_bytes=VMEM_LIMIT),
+        name="shift",
+    )(near, far, ctf4, noise4, table)
+
+
+def swapped(row, own):
+    lane = lax.broadcasted_iota(jnp.int32, row.shape, 1)
+    for bit in range(2):
+        size = MINE << bit
+        other = jnp.where(
+            (lane // size) % 2 == 0, pltpu.roll(row, US - size, 1), pltpu.roll(row, size, 1)
+        )
+        flip = jnp.broadcast_to((own >> bit) & 1, row.shape) == 1
+        row = jnp.where(flip, other, row)
+    return row
+
+
+def over_shifts(row, combine):
+    lane = lax.broadcasted_iota(jnp.int32, row.shape, 1)
+    for size in (16, 32):
+        turned = jnp.where(
+            lane % 64 >= size, pltpu.roll(row, size, 1), pltpu.roll(row, size + 64, 1)
+        )
+        row = combine(row, turned)
+    return row
+
+
+def by_block(row):
+    lane = lax.broadcasted_iota(jnp.int32, row.shape, 1) // MINE
+    row = jnp.where(
+        lane == 0,
+        row,
+        jnp.where(
+            lane == 1,
+            pltpu.roll(row, 72, 1),
+            jnp.where(lane == 2, pltpu.roll(row, 8, 1), pltpu.roll(row, 80, 1)),
+        ),
+    )
+    return row
 
 
 def score_kernel(
-    own_ref,
-    i0, i2, i13,
-    r0, r1, r2, r3,
-    ctf_hbm, noise_hbm, table_hbm,
+    own_ref, i0, i2, i13, w_near, r0, r1, r2, r3, ctf_ref, noise_ref, table,
     exp_out, stat_out, ins_out, sq_out,
-    ctf_ref, noise_ref, table, pictures, back, acc, sems,
+    w_far, back, acc,
 ):
-    chunk = ROT // 6
-    copies = fetch(
-        [(ctf_hbm, ctf_ref), (noise_hbm, noise_ref)]
-        + [(table_hbm.at[pl.ds(n * chunk, chunk)], table.at[pl.ds(n * chunk, chunk)]) for n in range(6)],
-        sems,
-    )
     own = own_ref[0]
-    for step, source in enumerate((i0, i13.at[0], i2, i13.at[1])):
-        pictures[own ^ step] = source[...]
     square = jnp.zeros((KS, LANES), F32)
     for b in range(ROT):
         block = jnp.concatenate([r[b].astype(F32) for r in (r0, r1, r2, r3)], axis=0)
@@ -204,55 +308,39 @@
         back[pl.ds((m + ROT) * KS, KS), :] = block.astype(BF16)
     prior = jnp.concatenate([r[ROT].astype(F32) for r in (r0, r1, r2, r3)], axis=0)[:, :HALF]
 
-    extra = jnp.concatenate([pictures[k, ROT].astype(F32) for k in range(BLOCKS)], axis=0)
-    dx = jnp.concatenate([extra[:, 2 * t : 2 * t + 1] for t in range(TRANS)], axis=0)
-    dy = jnp.concatenate([extra[:, 2 * t + 1 : 2 * t + 2] for t in range(TRANS)], axis=0)
-    combo = (dx + REACH) * (2 * REACH + 1) + (dy + REACH)
-    slot = lax.broadcasted_iota(jnp.int32, (US, 192), 1) % 64
-    hot = jnp.where(slot.astype(F32) == combo, 1.0, 0.0).astype(BF16)
-    group = lax.broadcasted_iota(jnp.int32, (MINE * BLOCKS, NDEF), 1).astype(F32)
-    which = jnp.where(group == extra[:, 8:9], 1.0, 0.0)
-    copies[0].wait()
-    copies[1].wait()
-    ctf4 = jnp.concatenate([ctf_ref[...]] * STEP, axis=1)
-    contrast = jnp.dot(which, ctf4, precision=HIGHEST, preferred_element_type=F32)
-    noise = jnp.concatenate([noise_ref[...]] * STEP, axis=1)
-    whiten = contrast / noise
+    i1, i3 = i13.at[0], i13.at[1]
+    dx0, dy0, group0 = image_rows(i0, i2)
+    dx1, dy1, group1 = image_rows(i1, i3)
+    noise = noise_ref[...]
+    contrast = contrast_of(jnp.concatenate([group0, group1], axis=0), ctf_ref)
+    far_contrast = contrast[2 * MINE :]
     squared = contrast * contrast
+    squared = jnp.concatenate([four(squared[: 2 * MINE]), four(squared[2 * MINE :])], axis=0)
+    sq_out[:, :HALF] = squared
+    sq_out[:, HALF:] = jnp.ones((US, HALF), F32)
     coef = squared / (2.0 * noise)
-    four = lambda v: jnp.concatenate([v] * TRANS, axis=0)
-    sq_out[:, :HALF] = four(squared)
-    sq_out[:, HALF:] = jnp.ones((US, HALF), F32)
-    coef_rows = four(jnp.concatenate([coef, coef], axis=1))
-    penalty = nt(square, coef_rows, precision=HIGHEST)
+    penalty = nt(square, jnp.concatenate([coef, coef], axis=1), precision=HIGHEST)
+    dx = jnp.concatenate([dx0, dx1], axis=0)
+    dy = jnp.concatenate([dy0, dy1], axis=0)
     near = -(dx * dx + dy * dy) / (2.0 * offset_sigma * offset_sigma)
-    near_row = as_row(near, US)
-    base = prior - penalty + near_row
-
-    contrast4 = four(contrast)
-    whiten4 = four(whiten)
-    cross = None
-    for h in range(ROT // 2):
-        pair = []
-        for b in (2 * h, 2 * h + 1):
-            if b % chunk == 0:
-                copies[2 + b // chunk].wait()
-            turn = jnp.dot(hot, table[b], preferred_element_type=F32)
-            cosine, sine = turn[:, :HALF], turn[:, HALF:]
-            block = jnp.concatenate([pictures[k, b].astype(F32) for k in range(BLOCKS)], axis=0)
-            real, imag = four(block[:, :HALF]), four(block[:, HALF:])
-            shifted_real = real * cosine - imag * sine
-            shifted_imag = real * sine + imag * cosine
-            rows = slice(b * US, (b + 1) * US)
-            ins_out[rows, :HALF] = (shifted_real * contrast4).astype(BF16)
-            ins_out[rows, HALF:] = (shifted_imag * contrast4).astype(BF16)
-            both = [shifted_real * whiten4, shifted_imag * whiten4]
-            pair.append(jnp.concatenate(both, axis=1).astype(BF16))
-        part = nt(
-            back[(ROT - 2 * h) * KS : (2 * ROT - 2 * h) * KS, :], jnp.concatenate(pair, axis=0)
+    base = prior - penalty + as_row(near, US)
+
+    shift_half(i1, i3, dx1, dy1, far_contrast, noise, table, w_far, ins_out)
+    half = US // 2
+    acc[...] = sum(
+        nt(
+            back[(ROT - 2 * h) * KS : (2 * ROT - 2 * h) * KS, :],
+            jnp.concatenate(
+                [
+                    w[b * half : (b + 1) * half, :]
+                    for b in (2 * h, 2 * h + 1)
+                    for w in (w_near, w_far)
+                ],
+                axis=0,
+            ),
         )
-        cross = part if cross is None else cross + part
-    acc[...] = cross
+        for h in range(ROT // 2)
+    )
 
     peak = jnp.full((KS, US), -jnp.inf, F32)
     for r in range(ROT):
@@ -260,10 +348,8 @@
         logp = acc[r * KS : (r + 1) * KS, :HALF] + acc[last * KS : (last + 1) * KS, HALF:] + base
         exp_out[r * KS : (r + 1) * KS, :] = logp
         peak = jnp.maximum(peak, logp)
-    peak = jnp.max(peak, axis=0, keepdims=True)
-    peak = jnp.broadcast_to(peak, (8, US))
-    peak = jnp.maximum(peak, pltpu.roll(peak, 32, 1))
-    peak = jnp.maximum(peak, pltpu.roll(peak, 64, 1))
+    peak = jnp.broadcast_to(jnp.max(peak, axis=0, keepdims=True), (8, US))
+    peak = over_shifts(peak, jnp.maximum)
     wide = jnp.broadcast_to(peak[:1], (KS, US))
     total = jnp.zeros((KS, US), F32)
     for r in range(ROT):
@@ -271,14 +357,14 @@
         exp_out[r * KS : (r + 1) * KS, :] = value
         total = total + value
     total = jnp.broadcast_to(jnp.sum(total, axis=0, keepdims=True), (8, US))
-    total = total + pltpu.roll(total, 32, 1)
-    total = total + pltpu.roll(total, 64, 1)
-    pair = jnp.concatenate([peak[:1], total[:1]], axis=0)[:, : US // TRANS]
+    total = over_shifts(total, jnp.add)
+    pair = [swapped(by_block(v), own)[:1, : US // TRANS] for v in (peak, total)]
+    pair = jnp.concatenate(pair, axis=0)
     for j in range(32):
         stat_out[j] = pair
 
 
-def score(own, imgs, refs, ctf_table, noise_power, table):
+def score(own, imgs, w_near, refs, ctf4, noise4, table):
     vmem = pl.BlockSpec(memory_space=pltpu.VMEM)
     smem = pl.BlockSpec(memory_space=pltpu.SMEM)
     return pl.pallas_call(
@@ -286,35 +372,40 @@
         out_shape=(
             jax.ShapeDtypeStruct((ROWS, US), F32),
             jax.ShapeDtypeStruct((32, 2, US // TRANS), F32),
-            jax.ShapeDtypeStruct((ROT * US, LANES), BF16),
+            jax.ShapeDtypeStruct((ROT * US // 2, LANES), BF16),
             jax.ShapeDtypeStruct((US, LANES), F32),
         ),
-        in_specs=[smem] + [vmem] * 7 + [pl.BlockSpec(memory_space=pltpu.HBM)] * 3,
+        in_specs=[smem] + [vmem] * 11,
         out_specs=(vmem,) * 4,
         scratch_shapes=[
-            pltpu.VMEM((NDEF, CYCLES), F32),
-            pltpu.VMEM((1, CYCLES), F32),
-            pltpu.VMEM((ROT, 192, LANES), BF16),
-            pltpu.VMEM((BLOCKS, ROT + 1, MINE, LANES), BF16),
+            pltpu.VMEM((ROT * US // 2, LANES), BF16),
             pltpu.VMEM((2 * ROWS, LANES), BF16),
             pltpu.VMEM((ROWS, LANES), F32),
-            pltpu.SemaphoreType.DMA((8,)),
         ],
         compiler_params=pltpu.CompilerParams(vmem_limit_bytes=VMEM_LIMIT),
         name="score",
-    )(own, *imgs, *refs, *(in_hbm(v) for v in (ctf_table, noise_power, table)))
-
-
-def insert_kernel(own_ref, exp_ref, pair_ref, all_ref, ins_ref, sq_ref, own_out, s1, s2, s3, like_out, post, acc):
+    )(own, *imgs, w_near, *refs, ctf4, noise4, table)
+
+
+def insert_kernel(
+    own_ref, exp_ref, pair_ref, all_ref, near_ref, far_ref, sq_ref,
+    own_out, s1, s2, s3, like_out, post, acc,
+):
+    own = own_ref[0]
     peaks = jnp.concatenate([all_ref[j, 0:1, :] for j in range(32)], axis=0)
     totals = jnp.concatenate([all_ref[j, 1:2, :] for j in range(32)], axis=0)
     peak = jnp.max(peaks, axis=0, keepdims=True)
     total = jnp.sum(totals * jnp.exp(peaks - peak), axis=0, keepdims=True)
     scale = jnp.exp(pair_ref[0, 0:1, :] - peak) / total
-    scale = jnp.broadcast_to(jnp.concatenate([scale] * TRANS, axis=1), (KS, US))
-    like = jnp.concatenate([peak + jnp.log(total)] * TRANS, axis=1)
-    shift = (US - own_ref[0] * MINE) % US
-    like_out[...] = pltpu.roll(jnp.broadcast_to(like, (8, US)), shift, 1)[:1, :MINE]
+    like = peak + jnp.log(total)
+    scale, like = (
+        swapped(jnp.broadcast_to(jnp.concatenate([v] * TRANS, axis=1), (8, US)), own)[:1]
+        for v in (scale, like)
+    )
+    like_out[...] = like[:, :MINE]
+    piece = [scale[:, d * MINE : (d + 1) * MINE] for d in range(BLOCKS)]
+    scale = jnp.concatenate([piece[0], piece[2]] * TRANS + [piece[1], piece[3]] * TRANS, axis=1)
+    scale = jnp.broadcast_to(scale, (KS, US))
     count = jnp.zeros((KS, US), F32)
     for r in range(ROT):
         value = (exp_ref[r * KS : (r + 1) * KS, :] * scale).astype(BF16)
@@ -324,17 +415,23 @@
             for again in (m, m + ROT):
                 post[again * KS : (again + 1) * KS, side * HALF : (side + 1) * HALF] = value
 
+    half = US // 2
     acc[...] = sum(
         jnp.dot(
             post[(ROT - 2 * h) * KS : (2 * ROT - 2 * h) * KS, :],
-            ins_ref[h * 2 * US : (h + 1) * 2 * US, :],
+            jnp.concatenate(
+                [
+                    v[b * half : (b + 1) * half, :]
+                    for b in (2 * h, 2 * h + 1)
+                    for v in (near_ref, far_ref)
+                ],
+                axis=0,
+            ),
             preferred_element_type=F32,
         )
         for h in range(ROT // 2)
     )
     sums = jnp.dot(count, sq_ref[...], precision=HIGHEST, preferred_element_type=F32)
-    high = sums.astype(BF16)
-    low = (sums - high.astype(F32)).astype(BF16)
     for b in range(ROT):
         block = acc[b * KS : (b + 1) * KS, :]
         own_out[b] = block[:OWN]
@@ -349,7 +446,7 @@
         out[ROT + 1] = (part - high.astype(F32)).astype(BF16)
 
 
-def insert(own, exps, stats, gathered, ins, sq):
+def insert(own, exps, stats, gathered, near, far, sq):
     vmem = pl.BlockSpec(memory_space=pltpu.VMEM)
     smem = pl.BlockSpec(memory_space=pltpu.SMEM)
     piece = (ROT + 2, OWN, LANES)
@@ -362,7 +459,7 @@
             jax.ShapeDtypeStruct(piece, BF16),
             jax.ShapeDtypeStruct((1, MINE), F32),
         ),
-        in_specs=[smem] + [vmem] * 5,
+        in_specs=[smem] + [vmem] * 6,
         out_specs=(vmem,) * 5,
         scratch_shapes=[
             pltpu.VMEM((2 * ROWS, LANES), BF16),
@@ -370,14 +467,13 @@
         ],
         compiler_params=pltpu.CompilerParams(vmem_limit_bytes=VMEM_LIMIT),
         name="insert",
-    )(own, exps, stats, gathered, ins, sq)
+    )(own, exps, stats, gathered, near, far, sq)
 
 
 def finish_kernel(own_ref, g1, g2, g3, tau_ref, out_ref, weight_out, fresh, turned, lines):
     parts = [own_ref, g1, g2, g3]
     sums = sum(p[ROT].astype(F32) + p[ROT + 1].astype(F32) for p in parts)
-    tau = jnp.concatenate([tau_ref[...]] * STEP, axis=1)
-    denom = sums[:, :HALF] + 1.0 / tau
+    denom = sums[:, :HALF] + 1.0 / tau_ref[...]
     denom = jnp.concatenate([denom, denom], axis=1)
     weight_out[...] = as_row(sums[:, HALF : HALF + 1], OWN) / (MINE * 16)
     for b in range(ROT):
@@ -436,27 +532,32 @@
     table, images, references, class_logprior, ctf_table, noise_power, tau_power, defocus, offsets
 ):
     own = (lax.axis_index("img") % BLOCKS).astype(jnp.int32).reshape(1)
-    img, ref = arrange(
+    img, ref, ctf4, noise4, tau4, table = arrange(
         images,
         references,
         class_logprior.reshape(1, OWN),
         offsets.transpose(1, 2, 0),
         defocus.reshape(1, MINE),
+        ctf_table,
+        noise_power.reshape(1, CYCLES),
+        tau_power.reshape(1, CYCLES),
+        table,
     )
     next_chip = beside(img, 2, 1)
     refs = (ref, along_y(ref, 3), along_y(ref, 2), along_y(ref, 1))
     next_chip, refs = lax.optimization_barrier((next_chip, refs))
     other_core = beside(jnp.stack([img, next_chip]), 1, 0)
-    exps, stats, ins, sq = score(
-        own, (img, next_chip, other_core), refs, ctf_table, noise_power.reshape(1, CYCLES), table
+    w_near, near = shift(img, next_chip, ctf4, noise4, table)
+    exps, stats, far, sq = score(
+        own, (img, next_chip, other_core), w_near, refs, ctf4, noise4, table
     )
     same_images = [[(y * 4 + r) * 8 + c for r in range(4) for c in range(8)] for y in range(4)]
     gathered = lax.all_to_all(
         stats, ("img", "cls"), 0, 0, tiled=True, axis_index_groups=same_images
     )
-    numer, s1, s2, s3, like = insert(own, exps, stats, gathered, ins, sq)
+    numer, s1, s2, s3, like = insert(own, exps, stats, gathered, near, far, sq)
     got = (along_y(s1, 1), along_y(s2, 2), along_y(s3, 3))
-    fresh, weight = finish(numer, got, tau_power.reshape(1, CYCLES))
+    fresh, weight = finish(numer, got, tau4)
     return fresh, weight.reshape(OWN), like.reshape(MINE)
 
 

time: 47.6 us -> 44.5 us (0.935)
  Pallas kernels: 11.7 us -> 9.72 us
  waiting for transfers between devices: 8.78 us -> 7.71 us
    pallas_call x1, Pallas kernels: 6.2 us -> 2.93 us  [score(): pl.pallas_call(score_kernel, out_shape=(jax.ShapeDtypeStruct((ROWS, US),...]
    ppermute x2, waiting for transfers between devices: 1.57 us -> 0.49 us  [beside(): return lax.ppermute(value, ('img', 'cls'), pairs)]
    pallas_call x0 -> x1, Pallas kernels: none -> 1.07 us  [shift(): pl.pallas_call(shift_kernel, out_shape=(half, half), in_specs=[vmem] * 5,...]
  transfers between devices with their start and end apart: 8 -> 8, of which waited for: 7 -> 7; matrix products, arithmetic and copies ran while one was open for 0% -> 0% of each run, Pallas kernels for 0% -> 2%
where the time goes in v3:
time: 44.5 us; the launch traced here: 44.4 us
  blocking collectives  13.2 us (30%)
  starting transfers between devices  13.1 us (29%)
  Pallas kernels  9.72 us (22%)
  waiting for transfers between devices  7.71 us (17%)
  between operations  0.69 us (2%)
    all_to_all x1, blocking collectives, per_device(): lax.all_to_all(stats, ('img', 'cls'), 0, 0, tiled=True, axis_index_groups...  13.2 us
    ppermute x6, starting transfers between devices, along_y(): lax.ppermute(value, 'img', [(i, (i // 4 + distance) % 4 * 4 + i % 4) for...  10 us
    ppermute x6, waiting for transfers between devices, along_y(): lax.ppermute(value, 'img', [(i, (i // 4 + distance) % 4 * 4 + i % 4) for...  7.21 us
    ppermute x2, starting transfers between devices, beside(): return lax.ppermute(value, ('img', 'cls'), pairs)  3.01 us
    pallas_call x1, Pallas kernels, score(): pl.pallas_call(score_kernel, out_shape=(jax.ShapeDtypeStruct((ROWS, US),...  2.93 us
    pallas_call x1, Pallas kernels, insert(): pl.pallas_call(insert_kernel, out_shape=(jax.ShapeDtypeStruct(piece, F32)...  2.38 us
    pallas_call x1, Pallas kernels, arrange(): pl.pallas_call(arrange_kernel, out_shape=(jax.ShapeDtypeStruct((ROT + 1,...  2.09 us
    pallas_call x1, Pallas kernels, finish(): pl.pallas_call(finish_kernel, out_shape=(jax.ShapeDtypeStruct((OWN, 2 * C...  1.25 us
  transfers between devices with their start and end apart: 8, of which 7 were waited for; matrix products, arithmetic and copies ran while one was open for 0% of the time, Pallas kernels for 2%

profile of v3, /device:TPU:0, one launch (start us, length us, event | category | flops | bytes accessed | tf_op | source)
XLA Modules:
  0.0 44.4 jit_solution(15505276599435310848)
XLA Ops:
  0.6 2.1 %arrange.1 = (bf16[37,8,256]{2,1,0:T(8,128)(2,1)S(1)}, bf16[37,4,256]{2,1,0:T(4,128)(2,1)S(1)}, f32[16,128]{1,0:T(8,128)S(1)}, f32[1,128]{1,0:T(1,128)S(1)}, f32...) custom-call(bf16[8,9216]{1,0:T(8,128)(2,1)} %img_hbm.1, bf16[4,9216]{1,0:T(4,128)(2,1)} %ref_hbm.1, ...), custom_call_target="tpu_custom_call" | custom-call | tf_op jit(solution)/shard_map/arrange/pallas_call | solution.py:166
  2.7 2.9 %collective-permute-start = (bf16[37,8,256]{2,1,0:T(8,128)(2,1)S(1)}, bf16[37,8,256]{2,1,0:T(8,128)(2,1)S(1)}, u32[]{:S(2)}, u32[]{:S(2)}) collective-permute-start(bf16[37,8,256]{2,1,0:T(8,128)(2,1)S(1)} %get-tuple-element.27.near.i0), channel_id=1, source_target_pairs={{0,17},{1,16},{2,19},{3,18},{4,21},{5,20},{6,23},{7,22},{8,25},{9,... | collective-permute-start | bytes 454664 | tf_op jit(solution)/shard_map/ppermute | solution.py:528
  5.7 1.6 %collective-permute-start.3 = (bf16[37,4,256]{2,1,0:T(4,128)(2,1)S(1)}, bf16[37,4,256]{2,1,0:T(4,128)(2,1)S(1)}, u32[]{:S(2)}, u32[]{:S(2)}) collective-permute-start(bf16[37,4,256]{2,1,0:T(4,128)(2,1)S(1)} %get-tuple-element.34.r0), channel_id=1, source_target_pairs={{0,32},{8,40},{16,48},{24,56},{32,64},{40,72},{48,80},{56,88},{64,... | collective-permute-start | bytes 227336 | tf_op jit(solution)/shard_map/ppermute | solution.py:519
  7.2 2.9 %collective-permute-start.2 = (bf16[37,4,256]{2,1,0:T(4,128)(2,1)S(1)}, bf16[37,4,256]{2,1,0:T(4,128)(2,1)S(1)}, u32[]{:S(2)}, u32[]{:S(2)}) collective-permute-start(bf16[37,4,256]{2,1,0:T(4,128)(2,1)S(1)} %get-tuple-element.34.r0), channel_id=1, source_target_pairs={{0,64},{8,72},{16,80},{24,88},{32,96},{40,104},{48,112},{56,120},{... | collective-permute-start | bytes 227336 | tf_op jit(solution)/shard_map/ppermute | solution.py:519
  10.1 1.3 %collective-permute-start.1 = (bf16[37,4,256]{2,1,0:T(4,128)(2,1)S(1)}, bf16[37,4,256]{2,1,0:T(4,128)(2,1)S(1)}, u32[]{:S(2)}, u32[]{:S(2)}) collective-permute-start(bf16[37,4,256]{2,1,0:T(4,128)(2,1)S(1)} %get-tuple-element.34.r0), channel_id=1, source_target_pairs={{0,96},{8,104},{16,112},{24,120},{32,0},{40,8},{48,16},{56,24},{64... | collective-permute-start | bytes 227336 | tf_op jit(solution)/shard_map/ppermute | solution.py:519
  11.5 0.6 %collective-permute-done.3.r3 = bf16[37,4,256]{2,1,0:T(4,128)(2,1)S(1)} collective-permute-done((bf16[37,4,256]{2,1,0:T(4,128)(2,1)S(1)}, bf16[37,4,256]{2,1,0:T(4,128)(2,1)S(1)}, u32[]{:S(2)}, u32[]{:S(2)}) %collective-permute-start.3) | collective-permute-done | bytes 75808 | tf_op jit(solution)/shard_map/ppermute | solution.py:519
  12.1 1.4 %collective-permute-done.2.r2 = bf16[37,4,256]{2,1,0:T(4,128)(2,1)S(1)} collective-permute-done((bf16[37,4,256]{2,1,0:T(4,128)(2,1)S(1)}, bf16[37,4,256]{2,1,0:T(4,128)(2,1)S(1)}, u32[]{:S(2)}, u32[]{:S(2)}) %collective-permute-start.2) | collective-permute-done | bytes 75808 | tf_op jit(solution)/shard_map/ppermute | solution.py:519
  13.5 1.0 %collective-permute-done.1.r1 = bf16[37,4,256]{2,1,0:T(4,128)(2,1)S(1)} collective-permute-done((bf16[37,4,256]{2,1,0:T(4,128)(2,1)S(1)}, bf16[37,4,256]{2,1,0:T(4,128)(2,1)S(1)}, u32[]{:S(2)}, u32[]{:S(2)}) %collective-permute-start.1) | collective-permute-done | bytes 75808 | tf_op jit(solution)/shard_map/ppermute | solution.py:519
  14.5 0.0 collective-permute-done.far.i2
  14.5 0.1 collective-permute-start.4
  14.6 1.1 %shift.1 = (bf16[2304,256]{1,0:T(8,128)(2,1)S(1)}, bf16[2304,256]{1,0:T(8,128)(2,1)S(1)}) custom-call(bf16[37,8,256]{2,1,0:T(8,128)(2,1)S(1)} %get-tuple-element.27.near.i0, bf16[37,8,256]{2,1,0:T(8,128)(2,1)S(1)} %collective-permute-done.far.i2, f32[16,128]{1,0:T(8,128)S(1)} %get-tuple-element.30.ctf_ref, f32[1,128]{1,0:T(1,128)S(1)} %get-tuple-element.31.noise_ref, ...), custom_call_target="tpu_custom_call" | custom-call | tf_op jit(solution)/shard_map/shift/pallas_call | solution.py:250
  15.7 0.5 %collective-permute-done.4.i13 = bf16[2,37,8,256]{3,2,1,0:T(8,128)(2,1)S(1)} collective-permute-done((bf16[2,37,8,256]{3,2,1,0:T(8,128)(2,1)S(1)}, bf16[2,37,8,256]{3,2,1,0:T(8,128)(2,1)S(1)}, u32[]{:S(2)}, u32[]{:S(2)}) %collective-permute-start.4) | collective-permute-done | bytes 303136 | tf_op jit(solution)/shard_map/ppermute | solution.py:528
  16.2 2.9 %score.1 = (f32[576,128]{1,0:T(8,128)S(1)}, f32[32,2,32]{2,1,0:T(2,128)S(1)}, bf16[2304,256]{1,0:T(8,128)(2,1)S(1)}, f32[128,256]{1,0:T(8,128)S(1)}) custom-call(s32[1]{0:T(128)} %bitcast.own_ref, bf16[37,8,256]{2,1,0:T(8,128)(2,1)S(1)} %get-tuple-element.27.near.i0, bf16[37,8,256]{2,1,0:T(8,128)(2,1)S(1)} %collective-permute-done.far.i2, ...), custom_call_target="tpu_custom_call" | custom-call | tf_op jit(solution)/shard_map/score/pallas_call | solution.py:370
  19.2 13.2 %all_to_all.5.all_ref = f32[32,2,32]{2,1,0:T(2,128)S(1)} all-to-all(f32[32,2,32]{2,1,0:T(2,128)S(1)} %get-tuple-element.39.pair_ref), channel_id=1, replica_groups={{0,1,2,3,4,5,6,7,8,9,10,11,12,13,14,15,16,17,18,19,20,21,22,23,24,25,26..., dimensions={0} | all-to-all | bytes 16384 | tf_op jit(solution)/shard_map/all_to_all | solution.py:555
  32.3 2.4 %insert.1 = (f32[38,4,256]{2,1,0:T(4,128)S(1)}, bf16[38,4,256]{2,1,0:T(4,128)(2,1)S(1)}, bf16[38,4,256]{2,1,0:T(4,128)(2,1)S(1)}, bf16[38,4,256]{2,1,0:T(4,128)(2,1)S(1)}, f32[1,8]{1,0:T(1,128)}) custom-call(s32[1]{0:T(128)} %bitcast.own_ref, f32[576,128]{1,0:T(8,128)S(1)} %get-tuple-element.38.exp_ref, f32[32,2,32]{2,1,0:T(2,128)S(1)} %get-tuple-element.39.pair_ref, ...), custom_call_target="tpu_custom_call" | custom-call | tf_op jit(solution)/shard_map/insert/pallas_call | solution.py:453
  34.7 0.4 collective-permute-start.5
  35.1 3.6 %collective-permute-start.6 = (bf16[38,4,256]{2,1,0:T(4,128)(2,1)S(1)}, bf16[38,4,256]{2,1,0:T(4,128)(2,1)S(1)}, u32[]{:S(2)}, u32[]{:S(2)}) collective-permute-start(bf16[38,4,256]{2,1,0:T(4,128)(2,1)S(1)} %get-tuple-element.45), channel_id=1, source_target_pairs={{0,64},{8,72},{16,80},{24,88},{32,96},{40,104},{48,112},{56,120},{... | collective-permute-start | bytes 233480 | tf_op jit(solution)/shard_map/ppermute | solution.py:519
  38.7 0.2 collective-permute-start.7
  38.9 1.4 %collective-permute-done.5.g1 = bf16[38,4,256]{2,1,0:T(4,128)(2,1)S(1)} collective-permute-done((bf16[38,4,256]{2,1,0:T(4,128)(2,1)S(1)}, bf16[38,4,256]{2,1,0:T(4,128)(2,1)S(1)}, u32[]{:S(2)}, u32[]{:S(2)}) %collective-permute-start.5) | collective-permute-done | bytes 77856 | tf_op jit(solution)/shard_map/ppermute | solution.py:519
  40.3 2.4 %collective-permute-done.6.g2 = bf16[38,4,256]{2,1,0:T(4,128)(2,1)S(1)} collective-permute-done((bf16[38,4,256]{2,1,0:T(4,128)(2,1)S(1)}, bf16[38,4,256]{2,1,0:T(4,128)(2,1)S(1)}, u32[]{:S(2)}, u32[]{:S(2)}) %collective-permute-start.6) | collective-permute-done | bytes 77856 | tf_op jit(solution)/shard_map/ppermute | solution.py:519
  42.7 0.4 collective-permute-done.7.g3
  43.1 1.3 %finish.1 = (f32[4,9216]{1,0:T(4,128)}, f32[1,4]{1,0:T(1,128)}) custom-call(f32[38,4,256]{2,1,0:T(4,128)S(1)} %get-tuple-element.43.own_ref, bf16[38,4,256]{2,1,0:T(4,128)(2,1)S(1)} %collective-permute-done.5.g1, bf16[38,4,256]{2,1,0:T(4,128)(2,1)S(1)} %collective-permute-done.6.g2, bf16[38,4,256]{2,1,0:T(4,128)(2,1)S(1)} %collective-permute-done.7.g3, ...), custom_call_target="tpu_custom_call" | custom-call | tf_op jit(solution)/shard_map/finish/pallas_call | solution.py:500
  (1 shorter events, 0.0 us)
Async XLA Ops:
  2.7 11.8 %collective-permute-start = (bf16[37,8,256]{2,1,0:T(8,128)(2,1)S(1)}, bf16[37,8,256]{2,1,0:T(8,128)(2,1)S(1)}, u32[]{:S(2)}, u32[]{:S(2)}) collective-permute-start(bf16[37,8,256]{2,1,0:T(8,128)(2,1)S(1)} %get-tuple-element.27.near.i0), channel_id=1, source_target_pairs={{0,17},{1,16},{2,19},{3,18},{4,21},{5,20},{6,23},{7,22},{8,25},{9,... | collective-permute-start | bytes 454664 | tf_op jit(solution)/shard_map/ppermute | solution.py:528
  5.7 6.4 %collective-permute-start.3 = (bf16[37,4,256]{2,1,0:T(4,128)(2,1)S(1)}, bf16[37,4,256]{2,1,0:T(4,128)(2,1)S(1)}, u32[]{:S(2)}, u32[]{:S(2)}) collective-permute-start(bf16[37,4,256]{2,1,0:T(4,128)(2,1)S(1)} %get-tuple-element.34.r0), channel_id=1, source_target_pairs={{0,32},{8,40},{16,48},{24,56},{32,64},{40,72},{48,80},{56,88},{64,... | collective-permute-start | bytes 227336 | tf_op jit(solution)/shard_map/ppermute | solution.py:519
  7.2 6.3 %collective-permute-start.2 = (bf16[37,4,256]{2,1,0:T(4,128)(2,1)S(1)}, bf16[37,4,256]{2,1,0:T(4,128)(2,1)S(1)}, u32[]{:S(2)}, u32[]{:S(2)}) collective-permute-start(bf16[37,4,256]{2,1,0:T(4,128)(2,1)S(1)} %get-tuple-element.34.r0), channel_id=1, source_target_pairs={{0,64},{8,72},{16,80},{24,88},{32,96},{40,104},{48,112},{56,120},{... | collective-permute-start | bytes 227336 | tf_op jit(solution)/shard_map/ppermute | solution.py:519
  10.1 4.4 %collective-permute-start.1 = (bf16[37,4,256]{2,1,0:T(4,128)(2,1)S(1)}, bf16[37,4,256]{2,1,0:T(4,128)(2,1)S(1)}, u32[]{:S(2)}, u32[]{:S(2)}) collective-permute-start(bf16[37,4,256]{2,1,0:T(4,128)(2,1)S(1)} %get-tuple-element.34.r0), channel_id=1, source_target_pairs={{0,96},{8,104},{16,112},{24,120},{32,0},{40,8},{48,16},{56,24},{64... | collective-permute-start | bytes 227336 | tf_op jit(solution)/shard_map/ppermute | solution.py:519
  14.5 1.7 %collective-permute-start.4 = (bf16[2,37,8,256]{3,2,1,0:T(8,128)(2,1)S(1)}, bf16[2,37,8,256]{3,2,1,0:T(8,128)(2,1)S(1)}, u32[]{:S(2)}, u32[]{:S(2)}) collective-permute-start(bf16[2,37,8,256]{3,2,1,0:T(8,128)(2,1)S(1)} %pad_maximum_fusion), channel_id=1, source_target_pairs={{0,8},{1,9},{2,10},{3,11},{4,12},{5,13},{6,14},{7,15},{8,0},{9,1},... | collective-permute-start | bytes 909320 | tf_op jit(solution)/shard_map/ppermute | solution.py:528
  34.7 5.6 %collective-permute-start.5 = (bf16[38,4,256]{2,1,0:T(4,128)(2,1)S(1)}, bf16[38,4,256]{2,1,0:T(4,128)(2,1)S(1)}, u32[]{:S(2)}, u32[]{:S(2)}) collective-permute-start(bf16[38,4,256]{2,1,0:T(4,128)(2,1)S(1)} %get-tuple-element.44), channel_id=1, source_target_pairs={{0,32},{8,40},{16,48},{24,56},{32,64},{40,72},{48,80},{56,88},{64,... | collective-permute-start | bytes 233480 | tf_op jit(solution)/shard_map/ppermute | solution.py:519
  35.1 7.6 %collective-permute-start.6 = (bf16[38,4,256]{2,1,0:T(4,128)(2,1)S(1)}, bf16[38,4,256]{2,1,0:T(4,128)(2,1)S(1)}, u32[]{:S(2)}, u32[]{:S(2)}) collective-permute-start(bf16[38,4,256]{2,1,0:T(4,128)(2,1)S(1)} %get-tuple-element.45), channel_id=1, source_target_pairs={{0,64},{8,72},{16,80},{24,88},{32,96},{40,104},{48,112},{56,120},{... | collective-permute-start | bytes 233480 | tf_op jit(solution)/shard_map/ppermute | solution.py:519
  38.7 4.4 %collective-permute-start.7 = (bf16[38,4,256]{2,1,0:T(4,128)(2,1)S(1)}, bf16[38,4,256]{2,1,0:T(4,128)(2,1)S(1)}, u32[]{:S(2)}, u32[]{:S(2)}) collective-permute-start(bf16[38,4,256]{2,1,0:T(4,128)(2,1)S(1)} %get-tuple-element.46), channel_id=1, source_target_pairs={{0,96},{8,104},{16,112},{24,120},{32,0},{40,8},{48,16},{56,24},{64... | collective-permute-start | bytes 233480 | tf_op jit(solution)/shard_map/ppermute | solution.py:519

commit v4 on v3

--- a/solution.py
+++ b/solution.py
@@ -28,6 +28,7 @@
 REACH = 3
 MIDDLE = 24
 SLOTS = 32
+WINDOW = 20_000_000_000
 offset_sigma = 2.0
 F32 = jnp.float32
 BF16 = jnp.bfloat16
@@ -254,6 +255,7 @@
         out_specs=(vmem, vmem),
         compiler_params=pltpu.CompilerParams(vmem_limit_bytes=VMEM_LIMIT),
         name="shift",
+        cost_estimate=pl.CostEstimate(flops=WINDOW, bytes_accessed=1000, transcendentals=0),
     )(near, far, ctf4, noise4, table)
 
 
@@ -545,7 +547,6 @@
     )
     next_chip = beside(img, 2, 1)
     refs = (ref, along_y(ref, 3), along_y(ref, 2), along_y(ref, 1))
-    next_chip, refs = lax.optimization_barrier((next_chip, refs))
     other_core = beside(jnp.stack([img, next_chip]), 1, 0)
     w_near, near = shift(img, next_chip, ctf4, noise4, table)
     exps, stats, far, sq = score(

time: 44.5 us -> 42.8 us (0.962)
  waiting for transfers between devices: 7.71 us -> 5.48 us
  starting transfers between devices: 13.1 us -> 13.6 us
    ppermute x6, waiting for transfers between devices: 7.21 us -> 5.47 us  [along_y(): lax.ppermute(value, 'img', [(i, (i // 4 + distance) % 4 * 4 + i % 4) for...]
    ppermute x6, starting transfers between devices: 10 us -> 10.6 us  [along_y(): lax.ppermute(value, 'img', [(i, (i // 4 + distance) % 4 * 4 + i % 4) for...]
    ppermute x2, waiting for transfers between devices: 0.49 us -> 0.01 us  [beside(): return lax.ppermute(value, ('img', 'cls'), pairs)]
  transfers between devices with their start and end apart: 8 -> 8, of which waited for: 7 -> 5; matrix products, arithmetic and copies ran while one was open for 0% -> 0% of each run, Pallas kernels for 2% -> 3%
where the time goes in v4:
time: 42.8 us; the launch traced here: 42.7 us
  starting transfers between devices  13.6 us (32%)
  blocking collectives  13.2 us (31%)
  Pallas kernels  9.72 us (23%)
  waiting for transfers between devices  5.48 us (13%)
  between operations  0.68 us (2%)
    all_to_all x1, blocking collectives, per_device(): lax.all_to_all(stats, ('img', 'cls'), 0, 0, tiled=True, axis_index_groups...  13.2 us
    ppermute x6, starting transfers between devices, along_y(): lax.ppermute(value, 'img', [(i, (i // 4 + distance) % 4 * 4 + i % 4) for...  10.6 us
    ppermute x6, waiting for transfers between devices, along_y(): lax.ppermute(value, 'img', [(i, (i // 4 + distance) % 4 * 4 + i % 4) for...  5.47 us
    ppermute x2, starting transfers between devices, beside(): return lax.ppermute(value, ('img', 'cls'), pairs)  3.01 us
    pallas_call x1, Pallas kernels, score(): pl.pallas_call(score_kernel, out_shape=(jax.ShapeDtypeStruct((ROWS, US),...  2.93 us
    pallas_call x1, Pallas kernels, insert(): pl.pallas_call(insert_kernel, out_shape=(jax.ShapeDtypeStruct(piece, F32)...  2.38 us
    pallas_call x1, Pallas kernels, arrange(): pl.pallas_call(arrange_kernel, out_shape=(jax.ShapeDtypeStruct((ROT + 1,...  2.09 us
    pallas_call x1, Pallas kernels, finish(): pl.pallas_call(finish_kernel, out_shape=(jax.ShapeDtypeStruct((OWN, 2 * C...  1.25 us
  transfers between devices with their start and end apart: 8, of which 5 were waited for; matrix products, arithmetic and copies ran while one was open for 0% of the time, Pallas kernels for 3%

profile of v4, /device:TPU:0, one launch (start us, length us, event | category | flops | bytes accessed | tf_op | source)
XLA Modules:
  0.0 42.7 jit_solution(17051782473140784919)
XLA Ops:
  0.6 2.1 %arrange.1 = (bf16[37,8,256]{2,1,0:T(8,128)(2,1)S(1)}, bf16[37,4,256]{2,1,0:T(4,128)(2,1)S(1)}, f32[16,128]{1,0:T(8,128)S(1)}, f32[1,128]{1,0:T(1,128)S(1)}, f32...) custom-call(bf16[8,9216]{1,0:T(8,128)(2,1)} %img_hbm.1, bf16[4,9216]{1,0:T(4,128)(2,1)} %ref_hbm.1, ...), custom_call_target="tpu_custom_call" | custom-call | tf_op jit(solution)/shard_map/arrange/pallas_call | solution.py:167
  2.7 2.9 %collective-permute-start = (bf16[37,8,256]{2,1,0:T(8,128)(2,1)S(1)}, bf16[37,8,256]{2,1,0:T(8,128)(2,1)S(1)}, u32[]{:S(2)}, u32[]{:S(2)}) collective-permute-start(bf16[37,8,256]{2,1,0:T(8,128)(2,1)S(1)} %get-tuple-element.22.near.i0), channel_id=1, source_target_pairs={{0,17},{1,16},{2,19},{3,18},{4,21},{5,20},{6,23},{7,22},{8,25},{9,... | collective-permute-start | bytes 454664 | tf_op jit(solution)/shard_map/ppermute | solution.py:530
  5.7 1.6 %collective-permute-start.4 = (bf16[37,4,256]{2,1,0:T(4,128)(2,1)S(1)}, bf16[37,4,256]{2,1,0:T(4,128)(2,1)S(1)}, u32[]{:S(2)}, u32[]{:S(2)}) collective-permute-start(bf16[37,4,256]{2,1,0:T(4,128)(2,1)S(1)} %get-tuple-element.27.r0), channel_id=1, source_target_pairs={{0,32},{8,40},{16,48},{24,56},{32,64},{40,72},{48,80},{56,88},{64,... | collective-permute-start | bytes 227336 | tf_op jit(solution)/shard_map/ppermute | solution.py:521
  7.2 2.9 %collective-permute-start.3 = (bf16[37,4,256]{2,1,0:T(4,128)(2,1)S(1)}, bf16[37,4,256]{2,1,0:T(4,128)(2,1)S(1)}, u32[]{:S(2)}, u32[]{:S(2)}) collective-permute-start(bf16[37,4,256]{2,1,0:T(4,128)(2,1)S(1)} %get-tuple-element.27.r0), channel_id=1, source_target_pairs={{0,64},{8,72},{16,80},{24,88},{32,96},{40,104},{48,112},{56,120},{... | collective-permute-start | bytes 227336 | tf_op jit(solution)/shard_map/ppermute | solution.py:521
  10.1 1.3 %collective-permute-start.2 = (bf16[37,4,256]{2,1,0:T(4,128)(2,1)S(1)}, bf16[37,4,256]{2,1,0:T(4,128)(2,1)S(1)}, u32[]{:S(2)}, u32[]{:S(2)}) collective-permute-start(bf16[37,4,256]{2,1,0:T(4,128)(2,1)S(1)} %get-tuple-element.27.r0), channel_id=1, source_target_pairs={{0,96},{8,104},{16,112},{24,120},{32,0},{40,8},{48,16},{56,24},{64... | collective-permute-start | bytes 227336 | tf_op jit(solution)/shard_map/ppermute | solution.py:521
  11.5 0.0 collective-permute-done.far.i2
  11.5 0.1 collective-permute-start.1
  11.6 1.1 %shift.1 = (bf16[2304,256]{1,0:T(8,128)(2,1)S(1)}, bf16[2304,256]{1,0:T(8,128)(2,1)S(1)}) custom-call(bf16[37,8,256]{2,1,0:T(8,128)(2,1)S(1)} %get-tuple-element.22.near.i0, bf16[37,8,256]{2,1,0:T(8,128)(2,1)S(1)} %collective-permute-done.far.i2, f32[16,128]{1,0:T(8,128)S(1)} %get-tuple-element.23.ctf_ref, f32[1,128]{1,0:T(1,128)S(1)} %get-tuple-element.24.noise_ref, ...), custom_call_target="tpu_custom_call" | custom-call | flops 20000000000 | bytes 1000 | tf_op jit(solution)/shard_map/shift/pallas_call | solution.py:251
  12.7 0.0 collective-permute-done.4.r3
  12.7 0.8 %collective-permute-done.3.r2 = bf16[37,4,256]{2,1,0:T(4,128)(2,1)S(1)} collective-permute-done((bf16[37,4,256]{2,1,0:T(4,128)(2,1)S(1)}, bf16[37,4,256]{2,1,0:T(4,128)(2,1)S(1)}, u32[]{:S(2)}, u32[]{:S(2)}) %collective-permute-start.3) | collective-permute-done | bytes 75808 | tf_op jit(solution)/shard_map/ppermute | solution.py:521
  13.5 1.0 %collective-permute-done.2.r1 = bf16[37,4,256]{2,1,0:T(4,128)(2,1)S(1)} collective-permute-done((bf16[37,4,256]{2,1,0:T(4,128)(2,1)S(1)}, bf16[37,4,256]{2,1,0:T(4,128)(2,1)S(1)}, u32[]{:S(2)}, u32[]{:S(2)}) %collective-permute-start.2) | collective-permute-done | bytes 75808 | tf_op jit(solution)/shard_map/ppermute | solution.py:521
  14.5 0.0 collective-permute-done.1.i13
  14.5 2.9 %score.1 = (f32[576,128]{1,0:T(8,128)S(1)}, f32[32,2,32]{2,1,0:T(2,128)S(1)}, bf16[2304,256]{1,0:T(8,128)(2,1)S(1)}, f32[128,256]{1,0:T(8,128)S(1)}) custom-call(s32[1]{0:T(128)} %bitcast.own_ref, bf16[37,8,256]{2,1,0:T(8,128)(2,1)S(1)} %get-tuple-element.22.near.i0, bf16[37,8,256]{2,1,0:T(8,128)(2,1)S(1)} %collective-permute-done.far.i2, ...), custom_call_target="tpu_custom_call" | custom-call | tf_op jit(solution)/shard_map/score/pallas_call | solution.py:372
  17.4 13.2 %all_to_all.5.all_ref = f32[32,2,32]{2,1,0:T(2,128)S(1)} all-to-all(f32[32,2,32]{2,1,0:T(2,128)S(1)} %get-tuple-element.29.pair_ref), channel_id=1, replica_groups={{0,1,2,3,4,5,6,7,8,9,10,11,12,13,14,15,16,17,18,19,20,21,22,23,24,25,26..., dimensions={0} | all-to-all | bytes 16384 | tf_op jit(solution)/shard_map/all_to_all | solution.py:556
  30.6 2.4 %insert.1 = (f32[38,4,256]{2,1,0:T(4,128)S(1)}, bf16[38,4,256]{2,1,0:T(4,128)(2,1)S(1)}, bf16[38,4,256]{2,1,0:T(4,128)(2,1)S(1)}, bf16[38,4,256]{2,1,0:T(4,128)(2,1)S(1)}, f32[1,8]{1,0:T(1,128)}) custom-call(s32[1]{0:T(128)} %bitcast.own_ref, f32[576,128]{1,0:T(8,128)S(1)} %get-tuple-element.28.exp_ref, f32[32,2,32]{2,1,0:T(2,128)S(1)} %get-tuple-element.29.pair_ref, ...), custom_call_target="tpu_custom_call" | custom-call | tf_op jit(solution)/shard_map/insert/pallas_call | solution.py:455
  33.0 0.5 %collective-permute-start.5 = (bf16[38,4,256]{2,1,0:T(4,128)(2,1)S(1)}, bf16[38,4,256]{2,1,0:T(4,128)(2,1)S(1)}, u32[]{:S(2)}, u32[]{:S(2)}) collective-permute-start(bf16[38,4,256]{2,1,0:T(4,128)(2,1)S(1)} %get-tuple-element.34), channel_id=1, source_target_pairs={{0,32},{8,40},{16,48},{24,56},{32,64},{40,72},{48,80},{56,88},{64,... | collective-permute-start | bytes 233480 | tf_op jit(solution)/shard_map/ppermute | solution.py:521
  33.5 3.5 %collective-permute-start.6 = (bf16[38,4,256]{2,1,0:T(4,128)(2,1)S(1)}, bf16[38,4,256]{2,1,0:T(4,128)(2,1)S(1)}, u32[]{:S(2)}, u32[]{:S(2)}) collective-permute-start(bf16[38,4,256]{2,1,0:T(4,128)(2,1)S(1)} %get-tuple-element.35), channel_id=1, source_target_pairs={{0,64},{8,72},{16,80},{24,88},{32,96},{40,104},{48,112},{56,120},{... | collective-permute-start | bytes 233480 | tf_op jit(solution)/shard_map/ppermute | solution.py:521
  37.0 0.7 %collective-permute-start.7 = (bf16[38,4,256]{2,1,0:T(4,128)(2,1)S(1)}, bf16[38,4,256]{2,1,0:T(4,128)(2,1)S(1)}, u32[]{:S(2)}, u32[]{:S(2)}) collective-permute-start(bf16[38,4,256]{2,1,0:T(4,128)(2,1)S(1)} %get-tuple-element.36), channel_id=1, source_target_pairs={{0,96},{8,104},{16,112},{24,120},{32,0},{40,8},{48,16},{56,24},{64... | collective-permute-start | bytes 233480 | tf_op jit(solution)/shard_map/ppermute | solution.py:521
  37.8 0.9 %collective-permute-done.5.g1 = bf16[38,4,256]{2,1,0:T(4,128)(2,1)S(1)} collective-permute-done((bf16[38,4,256]{2,1,0:T(4,128)(2,1)S(1)}, bf16[38,4,256]{2,1,0:T(4,128)(2,1)S(1)}, u32[]{:S(2)}, u32[]{:S(2)}) %collective-permute-start.5) | collective-permute-done | bytes 77856 | tf_op jit(solution)/shard_map/ppermute | solution.py:521
  38.6 2.4 %collective-permute-done.6.g2 = bf16[38,4,256]{2,1,0:T(4,128)(2,1)S(1)} collective-permute-done((bf16[38,4,256]{2,1,0:T(4,128)(2,1)S(1)}, bf16[38,4,256]{2,1,0:T(4,128)(2,1)S(1)}, u32[]{:S(2)}, u32[]{:S(2)}) %collective-permute-start.6) | collective-permute-done | bytes 77856 | tf_op jit(solution)/shard_map/ppermute | solution.py:521
  41.0 0.4 collective-permute-done.7.g3
  41.4 1.3 %finish.1 = (f32[4,9216]{1,0:T(4,128)}, f32[1,4]{1,0:T(1,128)}) custom-call(f32[38,4,256]{2,1,0:T(4,128)S(1)} %get-tuple-element.33.own_ref, bf16[38,4,256]{2,1,0:T(4,128)(2,1)S(1)} %collective-permute-done.5.g1, bf16[38,4,256]{2,1,0:T(4,128)(2,1)S(1)} %collective-permute-done.6.g2, bf16[38,4,256]{2,1,0:T(4,128)(2,1)S(1)} %collective-permute-done.7.g3, ...), custom_call_target="tpu_custom_call" | custom-call | tf_op jit(solution)/shard_map/finish/pallas_call | solution.py:502
  (1 shorter events, 0.0 us)
Async XLA Ops:
  2.7 8.7 %collective-permute-start = (bf16[37,8,256]{2,1,0:T(8,128)(2,1)S(1)}, bf16[37,8,256]{2,1,0:T(8,128)(2,1)S(1)}, u32[]{:S(2)}, u32[]{:S(2)}) collective-permute-start(bf16[37,8,256]{2,1,0:T(8,128)(2,1)S(1)} %get-tuple-element.22.near.i0), channel_id=1, source_target_pairs={{0,17},{1,16},{2,19},{3,18},{4,21},{5,20},{6,23},{7,22},{8,25},{9,... | collective-permute-start | bytes 454664 | tf_op jit(solution)/shard_map/ppermute | solution.py:530
  5.7 7.0 %collective-permute-start.4 = (bf16[37,4,256]{2,1,0:T(4,128)(2,1)S(1)}, bf16[37,4,256]{2,1,0:T(4,128)(2,1)S(1)}, u32[]{:S(2)}, u32[]{:S(2)}) collective-permute-start(bf16[37,4,256]{2,1,0:T(4,128)(2,1)S(1)} %get-tuple-element.27.r0), channel_id=1, source_target_pairs={{0,32},{8,40},{16,48},{24,56},{32,64},{40,72},{48,80},{56,88},{64,... | collective-permute-start | bytes 227336 | tf_op jit(solution)/shard_map/ppermute | solution.py:521
  7.2 6.3 %collective-permute-start.3 = (bf16[37,4,256]{2,1,0:T(4,128)(2,1)S(1)}, bf16[37,4,256]{2,1,0:T(4,128)(2,1)S(1)}, u32[]{:S(2)}, u32[]{:S(2)}) collective-permute-start(bf16[37,4,256]{2,1,0:T(4,128)(2,1)S(1)} %get-tuple-element.27.r0), channel_id=1, source_target_pairs={{0,64},{8,72},{16,80},{24,88},{32,96},{40,104},{48,112},{56,120},{... | collective-permute-start | bytes 227336 | tf_op jit(solution)/shard_map/ppermute | solution.py:521
  10.1 4.4 %collective-permute-start.2 = (bf16[37,4,256]{2,1,0:T(4,128)(2,1)S(1)}, bf16[37,4,256]{2,1,0:T(4,128)(2,1)S(1)}, u32[]{:S(2)}, u32[]{:S(2)}) collective-permute-start(bf16[37,4,256]{2,1,0:T(4,128)(2,1)S(1)} %get-tuple-element.27.r0), channel_id=1, source_target_pairs={{0,96},{8,104},{16,112},{24,120},{32,0},{40,8},{48,16},{56,24},{64... | collective-permute-start | bytes 227336 | tf_op jit(solution)/shard_map/ppermute | solution.py:521
  11.5 3.0 %collective-permute-start.1 = (bf16[2,37,8,256]{3,2,1,0:T(8,128)(2,1)S(1)}, bf16[2,37,8,256]{3,2,1,0:T(8,128)(2,1)S(1)}, u32[]{:S(2)}, u32[]{:S(2)}) collective-permute-start(bf16[2,37,8,256]{3,2,1,0:T(8,128)(2,1)S(1)} %pad_maximum_fusion), channel_id=1, source_target_pairs={{0,8},{1,9},{2,10},{3,11},{4,12},{5,13},{6,14},{7,15},{8,0},{9,1},... | collective-permute-start | bytes 909320 | tf_op jit(solution)/shard_map/ppermute | solution.py:530
  33.0 5.6 %collective-permute-start.5 = (bf16[38,4,256]{2,1,0:T(4,128)(2,1)S(1)}, bf16[38,4,256]{2,1,0:T(4,128)(2,1)S(1)}, u32[]{:S(2)}, u32[]{:S(2)}) collective-permute-start(bf16[38,4,256]{2,1,0:T(4,128)(2,1)S(1)} %get-tuple-element.34), channel_id=1, source_target_pairs={{0,32},{8,40},{16,48},{24,56},{32,64},{40,72},{48,80},{56,88},{64,... | collective-permute-start | bytes 233480 | tf_op jit(solution)/shard_map/ppermute | solution.py:521
  33.5 7.5 %collective-permute-start.6 = (bf16[38,4,256]{2,1,0:T(4,128)(2,1)S(1)}, bf16[38,4,256]{2,1,0:T(4,128)(2,1)S(1)}, u32[]{:S(2)}, u32[]{:S(2)}) collective-permute-start(bf16[38,4,256]{2,1,0:T(4,128)(2,1)S(1)} %get-tuple-element.35), channel_id=1, source_target_pairs={{0,64},{8,72},{16,80},{24,88},{32,96},{40,104},{48,112},{56,120},{... | collective-permute-start | bytes 233480 | tf_op jit(solution)/shard_map/ppermute | solution.py:521
  37.0 4.4 %collective-permute-start.7 = (bf16[38,4,256]{2,1,0:T(4,128)(2,1)S(1)}, bf16[38,4,256]{2,1,0:T(4,128)(2,1)S(1)}, u32[]{:S(2)}, u32[]{:S(2)}) collective-permute-start(bf16[38,4,256]{2,1,0:T(4,128)(2,1)S(1)} %get-tuple-element.36), channel_id=1, source_target_pairs={{0,96},{8,104},{16,112},{24,120},{32,0},{40,8},{48,16},{56,24},{64... | collective-permute-start | bytes 233480 | tf_op jit(solution)/shard_map/ppermute | solution.py:521

commit v5 on v4

--- a/solution.py
+++ b/solution.py
@@ -404,7 +404,7 @@
         swapped(jnp.broadcast_to(jnp.concatenate([v] * TRANS, axis=1), (8, US)), own)[:1]
         for v in (scale, like)
     )
-    like_out[...] = like[:, :MINE]
+    like_out[...] = jnp.broadcast_to(like, (8, US))
     piece = [scale[:, d * MINE : (d + 1) * MINE] for d in range(BLOCKS)]
     scale = jnp.concatenate([piece[0], piece[2]] * TRANS + [piece[1], piece[3]] * TRANS, axis=1)
     scale = jnp.broadcast_to(scale, (KS, US))
@@ -459,7 +459,7 @@
             jax.ShapeDtypeStruct(piece, BF16),
             jax.ShapeDtypeStruct(piece, BF16),
             jax.ShapeDtypeStruct(piece, BF16),
-            jax.ShapeDtypeStruct((1, MINE), F32),
+            jax.ShapeDtypeStruct((8, US), F32),
         ),
         in_specs=[smem] + [vmem] * 6,
         out_specs=(vmem,) * 5,
@@ -472,7 +472,8 @@
     )(own, exps, stats, gathered, near, far, sq)
 
 
-def finish_kernel(own_ref, g1, g2, g3, tau_ref, out_ref, weight_out, fresh, turned, lines):
+def finish_kernel(own_ref, g1, g2, g3, tau_ref, like_ref, out_ref, weight_out, like_out, fresh, turned, lines):
+    like_out[...] = like_ref[:1, :MINE]
     parts = [own_ref, g1, g2, g3]
     sums = sum(p[ROT].astype(F32) + p[ROT + 1].astype(F32) for p in parts)
     denom = sums[:, :HALF] + 1.0 / tau_ref[...]
@@ -497,16 +498,17 @@
         out_ref[:, j * ANG : (j + 1) * ANG] = jnp.concatenate(line, axis=1)[:, :ANG]
 
 
-def finish(own, got, tau):
+def finish(own, got, tau, like):
     vmem = pl.BlockSpec(memory_space=pltpu.VMEM)
     return pl.pallas_call(
         finish_kernel,
         out_shape=(
             jax.ShapeDtypeStruct((OWN, 2 * CYCLES * ANG), F32),
             jax.ShapeDtypeStruct((1, OWN), F32),
-        ),
-        in_specs=[vmem] * 5,
-        out_specs=(vmem, vmem),
+            jax.ShapeDtypeStruct((1, MINE), F32),
+        ),
+        in_specs=[vmem] * 6,
+        out_specs=(vmem,) * 3,
         scratch_shapes=[
             pltpu.VMEM((2, ROT * 8, HALF), F32),
             pltpu.VMEM((256, 128), F32),
@@ -514,7 +516,7 @@
         ],
         compiler_params=pltpu.CompilerParams(vmem_limit_bytes=VMEM_LIMIT),
         name="finish",
-    )(own, *got, tau)
+    )(own, *got, tau, like)
 
 
 def along_y(value, distance):
@@ -558,7 +560,7 @@
     )
     numer, s1, s2, s3, like = insert(own, exps, stats, gathered, near, far, sq)
     got = (along_y(s1, 1), along_y(s2, 2), along_y(s3, 3))
-    fresh, weight = finish(numer, got, tau4)
+    fresh, weight, like = finish(numer, got, tau4, like)
     return fresh, weight.reshape(OWN), like.reshape(MINE)
 
 

time: 42.8 us -> 42.5 us (level)
  Pallas kernels: 9.72 us -> 9.27 us
    pallas_call x1, Pallas kernels: 2.38 us -> 1.93 us  [insert(): pl.pallas_call(insert_kernel, out_shape=(jax.ShapeDtypeStruct(piece, F32)...]
where the time goes in v5:
time: 42.5 us; the launch traced here: 42.3 us
  starting transfers between devices  13.7 us (32%)
  blocking collectives  13.2 us (31%)
  Pallas kernels  9.27 us (22%)
  waiting for transfers between devices  5.48 us (13%)
  between operations  0.69 us (2%)
    all_to_all x1, blocking collectives, per_device(): lax.all_to_all(stats, ('img', 'cls'), 0, 0, tiled=True, axis_index_groups...  13.2 us
    ppermute x6, starting transfers between devices, along_y(): lax.ppermute(value, 'img', [(i, (i // 4 + distance) % 4 * 4 + i % 4) for...  10.6 us
    ppermute x6, waiting for transfers between devices, along_y(): lax.ppermute(value, 'img', [(i, (i // 4 + distance) % 4 * 4 + i % 4) for...  5.47 us
    ppermute x2, starting transfers between devices, beside(): return lax.ppermute(value, ('img', 'cls'), pairs)  3.01 us
    pallas_call x1, Pallas kernels, score(): pl.pallas_call(score_kernel, out_shape=(jax.ShapeDtypeStruct((ROWS, US),...  2.93 us
    pallas_call x1, Pallas kernels, arrange(): pl.pallas_call(arrange_kernel, out_shape=(jax.ShapeDtypeStruct((ROT + 1,...  2.09 us
    pallas_call x1, Pallas kernels, insert(): pl.pallas_call(insert_kernel, out_shape=(jax.ShapeDtypeStruct(piece, F32)...  1.93 us
    pallas_call x1, Pallas kernels, finish(): pl.pallas_call(finish_kernel, out_shape=(jax.ShapeDtypeStruct((OWN, 2 * C...  1.25 us
  transfers between devices with their start and end apart: 8, of which 5 were waited for; matrix products, arithmetic and copies ran while one was open for 0% of the time, Pallas kernels for 3%

profile of v5, /device:TPU:0, one launch (start us, length us, event | category | flops | bytes accessed | tf_op | source)
XLA Modules:
  0.0 42.3 jit_solution(15836195297015717681)
XLA Ops:
  0.6 2.1 %arrange.1 = (bf16[37,8,256]{2,1,0:T(8,128)(2,1)S(1)}, bf16[37,4,256]{2,1,0:T(4,128)(2,1)S(1)}, f32[16,128]{1,0:T(8,128)S(1)}, f32[1,128]{1,0:T(1,128)S(1)}, f32...) custom-call(bf16[8,9216]{1,0:T(8,128)(2,1)} %img_hbm.1, bf16[4,9216]{1,0:T(4,128)(2,1)} %ref_hbm.1, ...), custom_call_target="tpu_custom_call" | custom-call | tf_op jit(solution)/shard_map/arrange/pallas_call | solution.py:167
  2.7 2.9 %collective-permute-start = (bf16[37,8,256]{2,1,0:T(8,128)(2,1)S(1)}, bf16[37,8,256]{2,1,0:T(8,128)(2,1)S(1)}, u32[]{:S(2)}, u32[]{:S(2)}) collective-permute-start(bf16[37,8,256]{2,1,0:T(8,128)(2,1)S(1)} %get-tuple-element.23.near.i0), channel_id=1, source_target_pairs={{0,17},{1,16},{2,19},{3,18},{4,21},{5,20},{6,23},{7,22},{8,25},{9,... | collective-permute-start | bytes 454664 | tf_op jit(solution)/shard_map/ppermute | solution.py:532
  5.7 1.6 %collective-permute-start.4 = (bf16[37,4,256]{2,1,0:T(4,128)(2,1)S(1)}, bf16[37,4,256]{2,1,0:T(4,128)(2,1)S(1)}, u32[]{:S(2)}, u32[]{:S(2)}) collective-permute-start(bf16[37,4,256]{2,1,0:T(4,128)(2,1)S(1)} %get-tuple-element.28.r0), channel_id=1, source_target_pairs={{0,32},{8,40},{16,48},{24,56},{32,64},{40,72},{48,80},{56,88},{64,... | collective-permute-start | bytes 227336 | tf_op jit(solution)/shard_map/ppermute | solution.py:523
  7.2 2.9 %collective-permute-start.3 = (bf16[37,4,256]{2,1,0:T(4,128)(2,1)S(1)}, bf16[37,4,256]{2,1,0:T(4,128)(2,1)S(1)}, u32[]{:S(2)}, u32[]{:S(2)}) collective-permute-start(bf16[37,4,256]{2,1,0:T(4,128)(2,1)S(1)} %get-tuple-element.28.r0), channel_id=1, source_target_pairs={{0,64},{8,72},{16,80},{24,88},{32,96},{40,104},{48,112},{56,120},{... | collective-permute-start | bytes 227336 | tf_op jit(solution)/shard_map/ppermute | solution.py:523
  10.1 1.3 %collective-permute-start.2 = (bf16[37,4,256]{2,1,0:T(4,128)(2,1)S(1)}, bf16[37,4,256]{2,1,0:T(4,128)(2,1)S(1)}, u32[]{:S(2)}, u32[]{:S(2)}) collective-permute-start(bf16[37,4,256]{2,1,0:T(4,128)(2,1)S(1)} %get-tuple-element.28.r0), channel_id=1, source_target_pairs={{0,96},{8,104},{16,112},{24,120},{32,0},{40,8},{48,16},{56,24},{64... | collective-permute-start | bytes 227336 | tf_op jit(solution)/shard_map/ppermute | solution.py:523
  11.5 0.0 collective-permute-done.far.i2
  11.5 0.1 collective-permute-start.1
  11.6 1.1 %shift.1 = (bf16[2304,256]{1,0:T(8,128)(2,1)S(1)}, bf16[2304,256]{1,0:T(8,128)(2,1)S(1)}) custom-call(bf16[37,8,256]{2,1,0:T(8,128)(2,1)S(1)} %get-tuple-element.23.near.i0, bf16[37,8,256]{2,1,0:T(8,128)(2,1)S(1)} %collective-permute-done.far.i2, f32[16,128]{1,0:T(8,128)S(1)} %get-tuple-element.24.ctf_ref, f32[1,128]{1,0:T(1,128)S(1)} %get-tuple-element.25.noise_ref, ...), custom_call_target="tpu_custom_call" | custom-call | flops 20000000000 | bytes 1000 | tf_op jit(solution)/shard_map/shift/pallas_call | solution.py:251
  12.7 0.0 collective-permute-done.4.r3
  12.7 0.8 %collective-permute-done.3.r2 = bf16[37,4,256]{2,1,0:T(4,128)(2,1)S(1)} collective-permute-done((bf16[37,4,256]{2,1,0:T(4,128)(2,1)S(1)}, bf16[37,4,256]{2,1,0:T(4,128)(2,1)S(1)}, u32[]{:S(2)}, u32[]{:S(2)}) %collective-permute-start.3) | collective-permute-done | bytes 75808 | tf_op jit(solution)/shard_map/ppermute | solution.py:523
  13.5 1.0 %collective-permute-done.2.r1 = bf16[37,4,256]{2,1,0:T(4,128)(2,1)S(1)} collective-permute-done((bf16[37,4,256]{2,1,0:T(4,128)(2,1)S(1)}, bf16[37,4,256]{2,1,0:T(4,128)(2,1)S(1)}, u32[]{:S(2)}, u32[]{:S(2)}) %collective-permute-start.2) | collective-permute-done | bytes 75808 | tf_op jit(solution)/shard_map/ppermute | solution.py:523
  14.5 0.0 collective-permute-done.1.i13
  14.5 2.9 %score.1 = (f32[576,128]{1,0:T(8,128)S(1)}, f32[32,2,32]{2,1,0:T(2,128)S(1)}, bf16[2304,256]{1,0:T(8,128)(2,1)S(1)}, f32[128,256]{1,0:T(8,128)S(1)}) custom-call(s32[1]{0:T(128)} %bitcast.own_ref, bf16[37,8,256]{2,1,0:T(8,128)(2,1)S(1)} %get-tuple-element.23.near.i0, bf16[37,8,256]{2,1,0:T(8,128)(2,1)S(1)} %collective-permute-done.far.i2, ...), custom_call_target="tpu_custom_call" | custom-call | tf_op jit(solution)/shard_map/score/pallas_call | solution.py:372
  17.4 13.2 %all_to_all.5.all_ref = f32[32,2,32]{2,1,0:T(2,128)S(1)} all-to-all(f32[32,2,32]{2,1,0:T(2,128)S(1)} %get-tuple-element.30.pair_ref), channel_id=1, replica_groups={{0,1,2,3,4,5,6,7,8,9,10,11,12,13,14,15,16,17,18,19,20,21,22,23,24,25,26..., dimensions={0} | all-to-all | bytes 16384 | tf_op jit(solution)/shard_map/all_to_all | solution.py:558
  30.6 1.9 %insert.1 = (f32[38,4,256]{2,1,0:T(4,128)S(1)}, bf16[38,4,256]{2,1,0:T(4,128)(2,1)S(1)}, bf16[38,4,256]{2,1,0:T(4,128)(2,1)S(1)}, bf16[38,4,256]{2,1,0:T(4,128)(2,1)S(1)}, f32[8,128]{1,0:T(8,128)S(1)}) custom-call(s32[1]{0:T(128)} %bitcast.own_ref, f32[576,128]{1,0:T(8,128)S(1)} %get-tuple-element.29.exp_ref, f32[32,2,32]{2,1,0:T(2,128)S(1)} %get-tuple-element.30.pair_ref, ...), custom_call_target="tpu_custom_call" | custom-call | tf_op jit(solution)/shard_map/insert/pallas_call | solution.py:455
  32.6 0.6 %collective-permute-start.5 = (bf16[38,4,256]{2,1,0:T(4,128)(2,1)S(1)}, bf16[38,4,256]{2,1,0:T(4,128)(2,1)S(1)}, u32[]{:S(2)}, u32[]{:S(2)}) collective-permute-start(bf16[38,4,256]{2,1,0:T(4,128)(2,1)S(1)} %get-tuple-element.35), channel_id=1, source_target_pairs={{0,32},{8,40},{16,48},{24,56},{32,64},{40,72},{48,80},{56,88},{64,... | collective-permute-start | bytes 233480 | tf_op jit(solution)/shard_map/ppermute | solution.py:523
  33.1 3.5 %collective-permute-start.6 = (bf16[38,4,256]{2,1,0:T(4,128)(2,1)S(1)}, bf16[38,4,256]{2,1,0:T(4,128)(2,1)S(1)}, u32[]{:S(2)}, u32[]{:S(2)}) collective-permute-start(bf16[38,4,256]{2,1,0:T(4,128)(2,1)S(1)} %get-tuple-element.36), channel_id=1, source_target_pairs={{0,64},{8,72},{16,80},{24,88},{32,96},{40,104},{48,112},{56,120},{... | collective-permute-start | bytes 233480 | tf_op jit(solution)/shard_map/ppermute | solution.py:523
  36.7 0.7 %collective-permute-start.7 = (bf16[38,4,256]{2,1,0:T(4,128)(2,1)S(1)}, bf16[38,4,256]{2,1,0:T(4,128)(2,1)S(1)}, u32[]{:S(2)}, u32[]{:S(2)}) collective-permute-start(bf16[38,4,256]{2,1,0:T(4,128)(2,1)S(1)} %get-tuple-element.37), channel_id=1, source_target_pairs={{0,96},{8,104},{16,112},{24,120},{32,0},{40,8},{48,16},{56,24},{64... | collective-permute-start | bytes 233480 | tf_op jit(solution)/shard_map/ppermute | solution.py:523
  37.4 0.9 %collective-permute-done.5.g1 = bf16[38,4,256]{2,1,0:T(4,128)(2,1)S(1)} collective-permute-done((bf16[38,4,256]{2,1,0:T(4,128)(2,1)S(1)}, bf16[38,4,256]{2,1,0:T(4,128)(2,1)S(1)}, u32[]{:S(2)}, u32[]{:S(2)}) %collective-permute-start.5) | collective-permute-done | bytes 77856 | tf_op jit(solution)/shard_map/ppermute | solution.py:523
  38.2 2.4 %collective-permute-done.6.g2 = bf16[38,4,256]{2,1,0:T(4,128)(2,1)S(1)} collective-permute-done((bf16[38,4,256]{2,1,0:T(4,128)(2,1)S(1)}, bf16[38,4,256]{2,1,0:T(4,128)(2,1)S(1)}, u32[]{:S(2)}, u32[]{:S(2)}) %collective-permute-start.6) | collective-permute-done | bytes 77856 | tf_op jit(solution)/shard_map/ppermute | solution.py:523
  40.7 0.4 collective-permute-done.7.g3
  41.0 1.2 %finish.1 = (f32[4,9216]{1,0:T(4,128)}, f32[1,4]{1,0:T(1,128)}, f32[1,8]{1,0:T(1,128)}) custom-call(f32[38,4,256]{2,1,0:T(4,128)S(1)} %get-tuple-element.34.own_ref, bf16[38,4,256]{2,1,0:T(4,128)(2,1)S(1)} %collective-permute-done.5.g1, bf16[38,4,256]{2,1,0:T(4,128)(2,1)S(1)} %collective-permute-done.6.g2, ...), custom_call_target="tpu_custom_call" | custom-call | tf_op jit(solution)/shard_map/finish/pallas_call | solution.py:503
  (1 shorter events, 0.0 us)
Async XLA Ops:
  2.7 8.7 %collective-permute-start = (bf16[37,8,256]{2,1,0:T(8,128)(2,1)S(1)}, bf16[37,8,256]{2,1,0:T(8,128)(2,1)S(1)}, u32[]{:S(2)}, u32[]{:S(2)}) collective-permute-start(bf16[37,8,256]{2,1,0:T(8,128)(2,1)S(1)} %get-tuple-element.23.near.i0), channel_id=1, source_target_pairs={{0,17},{1,16},{2,19},{3,18},{4,21},{5,20},{6,23},{7,22},{8,25},{9,... | collective-permute-start | bytes 454664 | tf_op jit(solution)/shard_map/ppermute | solution.py:532
  5.7 7.0 %collective-permute-start.4 = (bf16[37,4,256]{2,1,0:T(4,128)(2,1)S(1)}, bf16[37,4,256]{2,1,0:T(4,128)(2,1)S(1)}, u32[]{:S(2)}, u32[]{:S(2)}) collective-permute-start(bf16[37,4,256]{2,1,0:T(4,128)(2,1)S(1)} %get-tuple-element.28.r0), channel_id=1, source_target_pairs={{0,32},{8,40},{16,48},{24,56},{32,64},{40,72},{48,80},{56,88},{64,... | collective-permute-start | bytes 227336 | tf_op jit(solution)/shard_map/ppermute | solution.py:523
  7.2 6.3 %collective-permute-start.3 = (bf16[37,4,256]{2,1,0:T(4,128)(2,1)S(1)}, bf16[37,4,256]{2,1,0:T(4,128)(2,1)S(1)}, u32[]{:S(2)}, u32[]{:S(2)}) collective-permute-start(bf16[37,4,256]{2,1,0:T(4,128)(2,1)S(1)} %get-tuple-element.28.r0), channel_id=1, source_target_pairs={{0,64},{8,72},{16,80},{24,88},{32,96},{40,104},{48,112},{56,120},{... | collective-permute-start | bytes 227336 | tf_op jit(solution)/shard_map/ppermute | solution.py:523
  10.1 4.4 %collective-permute-start.2 = (bf16[37,4,256]{2,1,0:T(4,128)(2,1)S(1)}, bf16[37,4,256]{2,1,0:T(4,128)(2,1)S(1)}, u32[]{:S(2)}, u32[]{:S(2)}) collective-permute-start(bf16[37,4,256]{2,1,0:T(4,128)(2,1)S(1)} %get-tuple-element.28.r0), channel_id=1, source_target_pairs={{0,96},{8,104},{16,112},{24,120},{32,0},{40,8},{48,16},{56,24},{64... | collective-permute-start | bytes 227336 | tf_op jit(solution)/shard_map/ppermute | solution.py:523
  11.5 3.0 %collective-permute-start.1 = (bf16[2,37,8,256]{3,2,1,0:T(8,128)(2,1)S(1)}, bf16[2,37,8,256]{3,2,1,0:T(8,128)(2,1)S(1)}, u32[]{:S(2)}, u32[]{:S(2)}) collective-permute-start(bf16[2,37,8,256]{3,2,1,0:T(8,128)(2,1)S(1)} %pad_maximum_fusion), channel_id=1, source_target_pairs={{0,8},{1,9},{2,10},{3,11},{4,12},{5,13},{6,14},{7,15},{8,0},{9,1},... | collective-permute-start | bytes 909320 | tf_op jit(solution)/shard_map/ppermute | solution.py:532
  32.6 5.7 %collective-permute-start.5 = (bf16[38,4,256]{2,1,0:T(4,128)(2,1)S(1)}, bf16[38,4,256]{2,1,0:T(4,128)(2,1)S(1)}, u32[]{:S(2)}, u32[]{:S(2)}) collective-permute-start(bf16[38,4,256]{2,1,0:T(4,128)(2,1)S(1)} %get-tuple-element.35), channel_id=1, source_target_pairs={{0,32},{8,40},{16,48},{24,56},{32,64},{40,72},{48,80},{56,88},{64,... | collective-permute-start | bytes 233480 | tf_op jit(solution)/shard_map/ppermute | solution.py:523
  33.1 7.5 %collective-permute-start.6 = (bf16[38,4,256]{2,1,0:T(4,128)(2,1)S(1)}, bf16[38,4,256]{2,1,0:T(4,128)(2,1)S(1)}, u32[]{:S(2)}, u32[]{:S(2)}) collective-permute-start(bf16[38,4,256]{2,1,0:T(4,128)(2,1)S(1)} %get-tuple-element.36), channel_id=1, source_target_pairs={{0,64},{8,72},{16,80},{24,88},{32,96},{40,104},{48,112},{56,120},{... | collective-permute-start | bytes 233480 | tf_op jit(solution)/shard_map/ppermute | solution.py:523
  36.7 4.4 %collective-permute-start.7 = (bf16[38,4,256]{2,1,0:T(4,128)(2,1)S(1)}, bf16[38,4,256]{2,1,0:T(4,128)(2,1)S(1)}, u32[]{:S(2)}, u32[]{:S(2)}) collective-permute-start(bf16[38,4,256]{2,1,0:T(4,128)(2,1)S(1)} %get-tuple-element.37), channel_id=1, source_target_pairs={{0,96},{8,104},{16,112},{24,120},{32,0},{40,8},{48,16},{56,24},{64... | collective-permute-start | bytes 233480 | tf_op jit(solution)/shard_map/ppermute | solution.py:523

commit v6 on v5

--- a/solution.py
+++ b/solution.py
@@ -261,14 +261,12 @@
 
 def swapped(row, own):
     lane = lax.broadcasted_iota(jnp.int32, row.shape, 1)
-    for bit in range(2):
-        size = MINE << bit
-        other = jnp.where(
-            (lane // size) % 2 == 0, pltpu.roll(row, US - size, 1), pltpu.roll(row, size, 1)
-        )
-        flip = jnp.broadcast_to((own >> bit) & 1, row.shape) == 1
-        row = jnp.where(flip, other, row)
-    return row
+    chosen = lambda bit: jnp.broadcast_to((own >> bit) & 1, row.shape) == 1
+    row = jnp.where(chosen(0), pltpu.roll(row, US // 2, 1), row)
+    other = jnp.where(
+        (lane // MINE) % 2 == 0, pltpu.roll(row, US - MINE, 1), pltpu.roll(row, MINE, 1)
+    )
+    return jnp.where(chosen(1), other, row)
 
 
 def over_shifts(row, combine):
@@ -278,20 +276,6 @@
             lane % 64 >= size, pltpu.roll(row, size, 1), pltpu.roll(row, size + 64, 1)
         )
         row = combine(row, turned)
-    return row
-
-
-def by_block(row):
-    lane = lax.broadcasted_iota(jnp.int32, row.shape, 1) // MINE
-    row = jnp.where(
-        lane == 0,
-        row,
-        jnp.where(
-            lane == 1,
-            pltpu.roll(row, 72, 1),
-            jnp.where(lane == 2, pltpu.roll(row, 8, 1), pltpu.roll(row, 80, 1)),
-        ),
-    )
     return row
 
 
@@ -351,7 +335,6 @@
         exp_out[r * KS : (r + 1) * KS, :] = logp
         peak = jnp.maximum(peak, logp)
     peak = jnp.broadcast_to(jnp.max(peak, axis=0, keepdims=True), (8, US))
-    peak = over_shifts(peak, jnp.maximum)
     wide = jnp.broadcast_to(peak[:1], (KS, US))
     total = jnp.zeros((KS, US), F32)
     for r in range(ROT):
@@ -359,9 +342,8 @@
         exp_out[r * KS : (r + 1) * KS, :] = value
         total = total + value
     total = jnp.broadcast_to(jnp.sum(total, axis=0, keepdims=True), (8, US))
-    total = over_shifts(total, jnp.add)
-    pair = [swapped(by_block(v), own)[:1, : US // TRANS] for v in (peak, total)]
-    pair = jnp.concatenate(pair, axis=0)
+    row = lax.broadcasted_iota(jnp.int32, (8, US), 0)
+    pair = swapped(jnp.where(row == 0, peak, total), own)[:2]
     for j in range(32):
         stat_out[j] = pair
 
@@ -373,7 +355,7 @@
         score_kernel,
         out_shape=(
             jax.ShapeDtypeStruct((ROWS, US), F32),
-            jax.ShapeDtypeStruct((32, 2, US // TRANS), F32),
+            jax.ShapeDtypeStruct((32, 2, US), F32),
             jax.ShapeDtypeStruct((ROT * US // 2, LANES), BF16),
             jax.ShapeDtypeStruct((US, LANES), F32),
         ),
@@ -396,18 +378,14 @@
     own = own_ref[0]
     peaks = jnp.concatenate([all_ref[j, 0:1, :] for j in range(32)], axis=0)
     totals = jnp.concatenate([all_ref[j, 1:2, :] for j in range(32)], axis=0)
-    peak = jnp.max(peaks, axis=0, keepdims=True)
-    total = jnp.sum(totals * jnp.exp(peaks - peak), axis=0, keepdims=True)
+    lane_peak = jnp.max(peaks, axis=0, keepdims=True)
+    lane_total = jnp.sum(totals * jnp.exp(peaks - lane_peak), axis=0, keepdims=True)
+    lane_peak = jnp.broadcast_to(lane_peak, (8, US))
+    peak = over_shifts(lane_peak, jnp.maximum)
+    total = over_shifts(lane_total * jnp.exp(lane_peak - peak), jnp.add)
     scale = jnp.exp(pair_ref[0, 0:1, :] - peak) / total
-    like = peak + jnp.log(total)
-    scale, like = (
-        swapped(jnp.broadcast_to(jnp.concatenate([v] * TRANS, axis=1), (8, US)), own)[:1]
-        for v in (scale, like)
-    )
-    like_out[...] = jnp.broadcast_to(like, (8, US))
-    piece = [scale[:, d * MINE : (d + 1) * MINE] for d in range(BLOCKS)]
-    scale = jnp.concatenate([piece[0], piece[2]] * TRANS + [piece[1], piece[3]] * TRANS, axis=1)
-    scale = jnp.broadcast_to(scale, (KS, US))
+    like_out[...] = swapped(peak + jnp.log(total), own)
+    scale = jnp.broadcast_to(swapped(scale, own)[:1], (KS, US))
     count = jnp.zeros((KS, US), F32)
     for r in range(ROT):
         value = (exp_ref[r * KS : (r + 1) * KS, :] * scale).astype(BF16)

time: 42.5 us -> 42.2 us (level)
  no operation moved by 1% of the time
where the time goes in v6:
time: 42.2 us; the launch traced here: 42.1 us
  starting transfers between devices  13.7 us (32%)
  blocking collectives  13.2 us (31%)
  Pallas kernels  9.06 us (21%)
  waiting for transfers between devices  5.48 us (13%)
  between operations  0.69 us (2%)
    all_to_all x1, blocking collectives, per_device(): lax.all_to_all(stats, ('img', 'cls'), 0, 0, tiled=True, axis_index_groups...  13.2 us
    ppermute x6, starting transfers between devices, along_y(): lax.ppermute(value, 'img', [(i, (i // 4 + distance) % 4 * 4 + i % 4) for...  10.6 us
    ppermute x6, waiting for transfers between devices, along_y(): lax.ppermute(value, 'img', [(i, (i // 4 + distance) % 4 * 4 + i % 4) for...  5.47 us
    ppermute x2, starting transfers between devices, beside(): return lax.ppermute(value, ('img', 'cls'), pairs)  3.01 us
    pallas_call x1, Pallas kernels, score(): pl.pallas_call(score_kernel, out_shape=(jax.ShapeDtypeStruct((ROWS, US),...  2.59 us
    pallas_call x1, Pallas kernels, arrange(): pl.pallas_call(arrange_kernel, out_shape=(jax.ShapeDtypeStruct((ROT + 1,...  2.09 us
    pallas_call x1, Pallas kernels, insert(): pl.pallas_call(insert_kernel, out_shape=(jax.ShapeDtypeStruct(piece, F32)...  2.06 us
    pallas_call x1, Pallas kernels, finish(): pl.pallas_call(finish_kernel, out_shape=(jax.ShapeDtypeStruct((OWN, 2 * C...  1.25 us
  transfers between devices with their start and end apart: 8, of which 5 were waited for; matrix products, arithmetic and copies ran while one was open for 0% of the time, Pallas kernels for 3%

profile of v6, /device:TPU:0, one launch (start us, length us, event | category | flops | bytes accessed | tf_op | source)
XLA Modules:
  0.0 42.1 jit_solution(12914794698244598101)
XLA Ops:
  0.6 2.1 %arrange.1 = (bf16[37,8,256]{2,1,0:T(8,128)(2,1)S(1)}, bf16[37,4,256]{2,1,0:T(4,128)(2,1)S(1)}, f32[16,128]{1,0:T(8,128)S(1)}, f32[1,128]{1,0:T(1,128)S(1)}, f32...) custom-call(bf16[8,9216]{1,0:T(8,128)(2,1)} %img_hbm.1, bf16[4,9216]{1,0:T(4,128)(2,1)} %ref_hbm.1, ...), custom_call_target="tpu_custom_call" | custom-call | tf_op jit(solution)/shard_map/arrange/pallas_call | solution.py:167
  2.7 2.9 %collective-permute-start = (bf16[37,8,256]{2,1,0:T(8,128)(2,1)S(1)}, bf16[37,8,256]{2,1,0:T(8,128)(2,1)S(1)}, u32[]{:S(2)}, u32[]{:S(2)}) collective-permute-start(bf16[37,8,256]{2,1,0:T(8,128)(2,1)S(1)} %get-tuple-element.23.near.i0), channel_id=1, source_target_pairs={{0,17},{1,16},{2,19},{3,18},{4,21},{5,20},{6,23},{7,22},{8,25},{9,... | collective-permute-start | bytes 454664 | tf_op jit(solution)/shard_map/ppermute | solution.py:510
  5.7 1.6 %collective-permute-start.4 = (bf16[37,4,256]{2,1,0:T(4,128)(2,1)S(1)}, bf16[37,4,256]{2,1,0:T(4,128)(2,1)S(1)}, u32[]{:S(2)}, u32[]{:S(2)}) collective-permute-start(bf16[37,4,256]{2,1,0:T(4,128)(2,1)S(1)} %get-tuple-element.28.r0), channel_id=1, source_target_pairs={{0,32},{8,40},{16,48},{24,56},{32,64},{40,72},{48,80},{56,88},{64,... | collective-permute-start | bytes 227336 | tf_op jit(solution)/shard_map/ppermute | solution.py:501
  7.2 2.9 %collective-permute-start.3 = (bf16[37,4,256]{2,1,0:T(4,128)(2,1)S(1)}, bf16[37,4,256]{2,1,0:T(4,128)(2,1)S(1)}, u32[]{:S(2)}, u32[]{:S(2)}) collective-permute-start(bf16[37,4,256]{2,1,0:T(4,128)(2,1)S(1)} %get-tuple-element.28.r0), channel_id=1, source_target_pairs={{0,64},{8,72},{16,80},{24,88},{32,96},{40,104},{48,112},{56,120},{... | collective-permute-start | bytes 227336 | tf_op jit(solution)/shard_map/ppermute | solution.py:501
  10.1 1.3 %collective-permute-start.2 = (bf16[37,4,256]{2,1,0:T(4,128)(2,1)S(1)}, bf16[37,4,256]{2,1,0:T(4,128)(2,1)S(1)}, u32[]{:S(2)}, u32[]{:S(2)}) collective-permute-start(bf16[37,4,256]{2,1,0:T(4,128)(2,1)S(1)} %get-tuple-element.28.r0), channel_id=1, source_target_pairs={{0,96},{8,104},{16,112},{24,120},{32,0},{40,8},{48,16},{56,24},{64... | collective-permute-start | bytes 227336 | tf_op jit(solution)/shard_map/ppermute | solution.py:501
  11.5 0.0 collective-permute-done.far.i2
  11.5 0.1 collective-permute-start.1
  11.6 1.1 %shift.1 = (bf16[2304,256]{1,0:T(8,128)(2,1)S(1)}, bf16[2304,256]{1,0:T(8,128)(2,1)S(1)}) custom-call(bf16[37,8,256]{2,1,0:T(8,128)(2,1)S(1)} %get-tuple-element.23.near.i0, bf16[37,8,256]{2,1,0:T(8,128)(2,1)S(1)} %collective-permute-done.far.i2, f32[16,128]{1,0:T(8,128)S(1)} %get-tuple-element.24.ctf_ref, f32[1,128]{1,0:T(1,128)S(1)} %get-tuple-element.25.noise_ref, ...), custom_call_target="tpu_custom_call" | custom-call | flops 20000000000 | bytes 1000 | tf_op jit(solution)/shard_map/shift/pallas_call | solution.py:251
  12.7 0.0 collective-permute-done.4.r3
  12.7 0.8 %collective-permute-done.3.r2 = bf16[37,4,256]{2,1,0:T(4,128)(2,1)S(1)} collective-permute-done((bf16[37,4,256]{2,1,0:T(4,128)(2,1)S(1)}, bf16[37,4,256]{2,1,0:T(4,128)(2,1)S(1)}, u32[]{:S(2)}, u32[]{:S(2)}) %collective-permute-start.3) | collective-permute-done | bytes 75808 | tf_op jit(solution)/shard_map/ppermute | solution.py:501
  13.5 1.0 %collective-permute-done.2.r1 = bf16[37,4,256]{2,1,0:T(4,128)(2,1)S(1)} collective-permute-done((bf16[37,4,256]{2,1,0:T(4,128)(2,1)S(1)}, bf16[37,4,256]{2,1,0:T(4,128)(2,1)S(1)}, u32[]{:S(2)}, u32[]{:S(2)}) %collective-permute-start.2) | collective-permute-done | bytes 75808 | tf_op jit(solution)/shard_map/ppermute | solution.py:501
  14.5 0.0 collective-permute-done.1.i13
  14.5 2.6 %score.1 = (f32[576,128]{1,0:T(8,128)S(1)}, f32[32,2,128]{2,1,0:T(2,128)S(1)}, bf16[2304,256]{1,0:T(8,128)(2,1)S(1)}, f32[128,256]{1,0:T(8,128)S(1)}) custom-call(s32[1]{0:T(128)} %bitcast.own_ref, bf16[37,8,256]{2,1,0:T(8,128)(2,1)S(1)} %get-tuple-element.23.near.i0, bf16[37,8,256]{2,1,0:T(8,128)(2,1)S(1)} %collective-permute-done.far.i2, ...), custom_call_target="tpu_custom_call" | custom-call | tf_op jit(solution)/shard_map/score/pallas_call | solution.py:354
  17.1 13.2 %all_to_all.5.all_ref = f32[32,2,128]{2,1,0:T(2,128)S(1)} all-to-all(f32[32,2,128]{2,1,0:T(2,128)S(1)} %get-tuple-element.30.pair_ref), channel_id=1, replica_groups={{0,1,2,3,4,5,6,7,8,9,10,11,12,13,14,15,16,17,18,19,20,21,22,23,24,25,26..., dimensions={0} | all-to-all | bytes 65536 | tf_op jit(solution)/shard_map/all_to_all | solution.py:536
  30.3 2.1 %insert.1 = (f32[38,4,256]{2,1,0:T(4,128)S(1)}, bf16[38,4,256]{2,1,0:T(4,128)(2,1)S(1)}, bf16[38,4,256]{2,1,0:T(4,128)(2,1)S(1)}, bf16[38,4,256]{2,1,0:T(4,128)(2,1)S(1)}, f32[8,128]{1,0:T(8,128)S(1)}) custom-call(s32[1]{0:T(128)} %bitcast.own_ref, f32[576,128]{1,0:T(8,128)S(1)} %get-tuple-element.29.exp_ref, f32[32,2,128]{2,1,0:T(2,128)S(1)} %get-tuple-element.30.pair_ref, ...), custom_call_target="tpu_custom_call" | custom-call | tf_op jit(solution)/shard_map/insert/pallas_call | solution.py:433
  32.3 0.6 %collective-permute-start.5 = (bf16[38,4,256]{2,1,0:T(4,128)(2,1)S(1)}, bf16[38,4,256]{2,1,0:T(4,128)(2,1)S(1)}, u32[]{:S(2)}, u32[]{:S(2)}) collective-permute-start(bf16[38,4,256]{2,1,0:T(4,128)(2,1)S(1)} %get-tuple-element.35), channel_id=1, source_target_pairs={{0,32},{8,40},{16,48},{24,56},{32,64},{40,72},{48,80},{56,88},{64,... | collective-permute-start | bytes 233480 | tf_op jit(solution)/shard_map/ppermute | solution.py:501
  32.9 3.5 %collective-permute-start.6 = (bf16[38,4,256]{2,1,0:T(4,128)(2,1)S(1)}, bf16[38,4,256]{2,1,0:T(4,128)(2,1)S(1)}, u32[]{:S(2)}, u32[]{:S(2)}) collective-permute-start(bf16[38,4,256]{2,1,0:T(4,128)(2,1)S(1)} %get-tuple-element.36), channel_id=1, source_target_pairs={{0,64},{8,72},{16,80},{24,88},{32,96},{40,104},{48,112},{56,120},{... | collective-permute-start | bytes 233480 | tf_op jit(solution)/shard_map/ppermute | solution.py:501
  36.4 0.7 %collective-permute-start.7 = (bf16[38,4,256]{2,1,0:T(4,128)(2,1)S(1)}, bf16[38,4,256]{2,1,0:T(4,128)(2,1)S(1)}, u32[]{:S(2)}, u32[]{:S(2)}) collective-permute-start(bf16[38,4,256]{2,1,0:T(4,128)(2,1)S(1)} %get-tuple-element.37), channel_id=1, source_target_pairs={{0,96},{8,104},{16,112},{24,120},{32,0},{40,8},{48,16},{56,24},{64... | collective-permute-start | bytes 233480 | tf_op jit(solution)/shard_map/ppermute | solution.py:501
  37.2 0.9 %collective-permute-done.5.g1 = bf16[38,4,256]{2,1,0:T(4,128)(2,1)S(1)} collective-permute-done((bf16[38,4,256]{2,1,0:T(4,128)(2,1)S(1)}, bf16[38,4,256]{2,1,0:T(4,128)(2,1)S(1)}, u32[]{:S(2)}, u32[]{:S(2)}) %collective-permute-start.5) | collective-permute-done | bytes 77856 | tf_op jit(solution)/shard_map/ppermute | solution.py:501
  38.0 2.4 %collective-permute-done.6.g2 = bf16[38,4,256]{2,1,0:T(4,128)(2,1)S(1)} collective-permute-done((bf16[38,4,256]{2,1,0:T(4,128)(2,1)S(1)}, bf16[38,4,256]{2,1,0:T(4,128)(2,1)S(1)}, u32[]{:S(2)}, u32[]{:S(2)}) %collective-permute-start.6) | collective-permute-done | bytes 77856 | tf_op jit(solution)/shard_map/ppermute | solution.py:501
  40.4 0.4 collective-permute-done.7.g3
  40.8 1.2 %finish.1 = (f32[4,9216]{1,0:T(4,128)}, f32[1,4]{1,0:T(1,128)}, f32[1,8]{1,0:T(1,128)}) custom-call(f32[38,4,256]{2,1,0:T(4,128)S(1)} %get-tuple-element.34.own_ref, bf16[38,4,256]{2,1,0:T(4,128)(2,1)S(1)} %collective-permute-done.5.g1, bf16[38,4,256]{2,1,0:T(4,128)(2,1)S(1)} %collective-permute-done.6.g2, ...), custom_call_target="tpu_custom_call" | custom-call | tf_op jit(solution)/shard_map/finish/pallas_call | solution.py:481
  (1 shorter events, 0.0 us)
Async XLA Ops:
  2.7 8.7 %collective-permute-start = (bf16[37,8,256]{2,1,0:T(8,128)(2,1)S(1)}, bf16[37,8,256]{2,1,0:T(8,128)(2,1)S(1)}, u32[]{:S(2)}, u32[]{:S(2)}) collective-permute-start(bf16[37,8,256]{2,1,0:T(8,128)(2,1)S(1)} %get-tuple-element.23.near.i0), channel_id=1, source_target_pairs={{0,17},{1,16},{2,19},{3,18},{4,21},{5,20},{6,23},{7,22},{8,25},{9,... | collective-permute-start | bytes 454664 | tf_op jit(solution)/shard_map/ppermute | solution.py:510
  5.7 7.0 %collective-permute-start.4 = (bf16[37,4,256]{2,1,0:T(4,128)(2,1)S(1)}, bf16[37,4,256]{2,1,0:T(4,128)(2,1)S(1)}, u32[]{:S(2)}, u32[]{:S(2)}) collective-permute-start(bf16[37,4,256]{2,1,0:T(4,128)(2,1)S(1)} %get-tuple-element.28.r0), channel_id=1, source_target_pairs={{0,32},{8,40},{16,48},{24,56},{32,64},{40,72},{48,80},{56,88},{64,... | collective-permute-start | bytes 227336 | tf_op jit(solution)/shard_map/ppermute | solution.py:501
  7.2 6.3 %collective-permute-start.3 = (bf16[37,4,256]{2,1,0:T(4,128)(2,1)S(1)}, bf16[37,4,256]{2,1,0:T(4,128)(2,1)S(1)}, u32[]{:S(2)}, u32[]{:S(2)}) collective-permute-start(bf16[37,4,256]{2,1,0:T(4,128)(2,1)S(1)} %get-tuple-element.28.r0), channel_id=1, source_target_pairs={{0,64},{8,72},{16,80},{24,88},{32,96},{40,104},{48,112},{56,120},{... | collective-permute-start | bytes 227336 | tf_op jit(solution)/shard_map/ppermute | solution.py:501
  10.1 4.4 %collective-permute-start.2 = (bf16[37,4,256]{2,1,0:T(4,128)(2,1)S(1)}, bf16[37,4,256]{2,1,0:T(4,128)(2,1)S(1)}, u32[]{:S(2)}, u32[]{:S(2)}) collective-permute-start(bf16[37,4,256]{2,1,0:T(4,128)(2,1)S(1)} %get-tuple-element.28.r0), channel_id=1, source_target_pairs={{0,96},{8,104},{16,112},{24,120},{32,0},{40,8},{48,16},{56,24},{64... | collective-permute-start | bytes 227336 | tf_op jit(solution)/shard_map/ppermute | solution.py:501
  11.5 3.0 %collective-permute-start.1 = (bf16[2,37,8,256]{3,2,1,0:T(8,128)(2,1)S(1)}, bf16[2,37,8,256]{3,2,1,0:T(8,128)(2,1)S(1)}, u32[]{:S(2)}, u32[]{:S(2)}) collective-permute-start(bf16[2,37,8,256]{3,2,1,0:T(8,128)(2,1)S(1)} %pad_maximum_fusion), channel_id=1, source_target_pairs={{0,8},{1,9},{2,10},{3,11},{4,12},{5,13},{6,14},{7,15},{8,0},{9,1},... | collective-permute-start | bytes 909320 | tf_op jit(solution)/shard_map/ppermute | solution.py:510
  32.3 5.7 %collective-permute-start.5 = (bf16[38,4,256]{2,1,0:T(4,128)(2,1)S(1)}, bf16[38,4,256]{2,1,0:T(4,128)(2,1)S(1)}, u32[]{:S(2)}, u32[]{:S(2)}) collective-permute-start(bf16[38,4,256]{2,1,0:T(4,128)(2,1)S(1)} %get-tuple-element.35), channel_id=1, source_target_pairs={{0,32},{8,40},{16,48},{24,56},{32,64},{40,72},{48,80},{56,88},{64,... | collective-permute-start | bytes 233480 | tf_op jit(solution)/shard_map/ppermute | solution.py:501
  32.9 7.5 %collective-permute-start.6 = (bf16[38,4,256]{2,1,0:T(4,128)(2,1)S(1)}, bf16[38,4,256]{2,1,0:T(4,128)(2,1)S(1)}, u32[]{:S(2)}, u32[]{:S(2)}) collective-permute-start(bf16[38,4,256]{2,1,0:T(4,128)(2,1)S(1)} %get-tuple-element.36), channel_id=1, source_target_pairs={{0,64},{8,72},{16,80},{24,88},{32,96},{40,104},{48,112},{56,120},{... | collective-permute-start | bytes 233480 | tf_op jit(solution)/shard_map/ppermute | solution.py:501
  36.4 4.4 %collective-permute-start.7 = (bf16[38,4,256]{2,1,0:T(4,128)(2,1)S(1)}, bf16[38,4,256]{2,1,0:T(4,128)(2,1)S(1)}, u32[]{:S(2)}, u32[]{:S(2)}) collective-permute-start(bf16[38,4,256]{2,1,0:T(4,128)(2,1)S(1)} %get-tuple-element.37), channel_id=1, source_target_pairs={{0,96},{8,104},{16,112},{24,120},{32,0},{40,8},{48,16},{56,24},{64... | collective-permute-start | bytes 233480 | tf_op jit(solution)/shard_map/ppermute | solution.py:501

commit v7 on v6

--- a/solution.py
+++ b/solution.py
@@ -141,12 +141,9 @@
         ),
         sems,
     )
-    copies[0].wait()
+    for copy in copies[:-1]:
+        copy.wait()
     turn_major(ref_ref, OWN, cut, flat, ref_out)
-    copies[1].wait()
-    turn_major(img_ref, MINE, cut2, flat2, img_out)
-    for copy in copies[2:]:
-        copy.wait()
     lane = lax.broadcasted_iota(jnp.int32, (MINE, LANES), 1)
     extra = jnp.where(lane == 8, as_column(def_ref[...].astype(F32), MINE), 0.0)
     for t in range(TRANS):
@@ -158,6 +155,8 @@
     ref_out[ROT] = jnp.broadcast_to(column, (OWN, LANES)).astype(BF16)
     for small, out in ((ctf_ref, ctf_out), (noise_ref, noise_out), (tau_ref, tau_out)):
         out[...] = jnp.concatenate([small[...]] * STEP, axis=1)
+    turn_major(img_ref, MINE, cut2, flat2, img_out)
+    copies[-1].wait()
 
 
 def arrange(images, references, prior, offsets, defocus, ctf_table, noise, tau, table):

time: 42.2 us -> 42 us (level)
  no operation moved by 1% of the time
where the time goes in v7:
time: 42 us; the launch traced here: 41.8 us
  starting transfers between devices  13.7 us (33%)
  blocking collectives  13.2 us (31%)
  Pallas kernels  8.77 us (21%)
  waiting for transfers between devices  5.47 us (13%)
  between operations  0.69 us (2%)
    all_to_all x1, blocking collectives, per_device(): lax.all_to_all(stats, ('img', 'cls'), 0, 0, tiled=True, axis_index_groups...  13.2 us
    ppermute x6, starting transfers between devices, along_y(): lax.ppermute(value, 'img', [(i, (i // 4 + distance) % 4 * 4 + i % 4) for...  10.7 us
    ppermute x6, waiting for transfers between devices, along_y(): lax.ppermute(value, 'img', [(i, (i // 4 + distance) % 4 * 4 + i % 4) for...  5.47 us
    ppermute x2, starting transfers between devices, beside(): return lax.ppermute(value, ('img', 'cls'), pairs)  3 us
    pallas_call x1, Pallas kernels, score(): pl.pallas_call(score_kernel, out_shape=(jax.ShapeDtypeStruct((ROWS, US),...  2.59 us
    pallas_call x1, Pallas kernels, insert(): pl.pallas_call(insert_kernel, out_shape=(jax.ShapeDtypeStruct(piece, F32)...  2.06 us
    pallas_call x1, Pallas kernels, arrange(): pl.pallas_call(arrange_kernel, out_shape=(jax.ShapeDtypeStruct((ROT + 1,...  1.81 us
    pallas_call x1, Pallas kernels, finish(): pl.pallas_call(finish_kernel, out_shape=(jax.ShapeDtypeStruct((OWN, 2 * C...  1.25 us
  transfers between devices with their start and end apart: 8, of which 5 were waited for; matrix products, arithmetic and copies ran while one was open for 0% of the time, Pallas kernels for 3%

profile of v7, /device:TPU:0, one launch (start us, length us, event | category | flops | bytes accessed | tf_op | source)
XLA Modules:
  0.0 41.8 jit_solution(1037819667448161142)
XLA Ops:
  0.6 1.8 %arrange.1 = (bf16[37,8,256]{2,1,0:T(8,128)(2,1)S(1)}, bf16[37,4,256]{2,1,0:T(4,128)(2,1)S(1)}, f32[16,128]{1,0:T(8,128)S(1)}, f32[1,128]{1,0:T(1,128)S(1)}, f32...) custom-call(bf16[8,9216]{1,0:T(8,128)(2,1)} %img_hbm.1, bf16[4,9216]{1,0:T(4,128)(2,1)} %ref_hbm.1, ...), custom_call_target="tpu_custom_call" | custom-call | tf_op jit(solution)/shard_map/arrange/pallas_call | solution.py:166
  2.4 2.9 %collective-permute-start = (bf16[37,8,256]{2,1,0:T(8,128)(2,1)S(1)}, bf16[37,8,256]{2,1,0:T(8,128)(2,1)S(1)}, u32[]{:S(2)}, u32[]{:S(2)}) collective-permute-start(bf16[37,8,256]{2,1,0:T(8,128)(2,1)S(1)} %get-tuple-element.23.near.i0), channel_id=1, source_target_pairs={{0,17},{1,16},{2,19},{3,18},{4,21},{5,20},{6,23},{7,22},{8,25},{9,... | collective-permute-start | bytes 454664 | tf_op jit(solution)/shard_map/ppermute | solution.py:509
  5.4 1.6 %collective-permute-start.4 = (bf16[37,4,256]{2,1,0:T(4,128)(2,1)S(1)}, bf16[37,4,256]{2,1,0:T(4,128)(2,1)S(1)}, u32[]{:S(2)}, u32[]{:S(2)}) collective-permute-start(bf16[37,4,256]{2,1,0:T(4,128)(2,1)S(1)} %get-tuple-element.28.r0), channel_id=1, source_target_pairs={{0,32},{8,40},{16,48},{24,56},{32,64},{40,72},{48,80},{56,88},{64,... | collective-permute-start | bytes 227336 | tf_op jit(solution)/shard_map/ppermute | solution.py:500
  6.9 2.9 %collective-permute-start.3 = (bf16[37,4,256]{2,1,0:T(4,128)(2,1)S(1)}, bf16[37,4,256]{2,1,0:T(4,128)(2,1)S(1)}, u32[]{:S(2)}, u32[]{:S(2)}) collective-permute-start(bf16[37,4,256]{2,1,0:T(4,128)(2,1)S(1)} %get-tuple-element.28.r0), channel_id=1, source_target_pairs={{0,64},{8,72},{16,80},{24,88},{32,96},{40,104},{48,112},{56,120},{... | collective-permute-start | bytes 227336 | tf_op jit(solution)/shard_map/ppermute | solution.py:500
  9.8 1.3 %collective-permute-start.2 = (bf16[37,4,256]{2,1,0:T(4,128)(2,1)S(1)}, bf16[37,4,256]{2,1,0:T(4,128)(2,1)S(1)}, u32[]{:S(2)}, u32[]{:S(2)}) collective-permute-start(bf16[37,4,256]{2,1,0:T(4,128)(2,1)S(1)} %get-tuple-element.28.r0), channel_id=1, source_target_pairs={{0,96},{8,104},{16,112},{24,120},{32,0},{40,8},{48,16},{56,24},{64... | collective-permute-start | bytes 227336 | tf_op jit(solution)/shard_map/ppermute | solution.py:500
  11.2 0.0 collective-permute-done.far.i2
  11.2 0.1 collective-permute-start.1
  11.3 1.1 %shift.1 = (bf16[2304,256]{1,0:T(8,128)(2,1)S(1)}, bf16[2304,256]{1,0:T(8,128)(2,1)S(1)}) custom-call(bf16[37,8,256]{2,1,0:T(8,128)(2,1)S(1)} %get-tuple-element.23.near.i0, bf16[37,8,256]{2,1,0:T(8,128)(2,1)S(1)} %collective-permute-done.far.i2, f32[16,128]{1,0:T(8,128)S(1)} %get-tuple-element.24.ctf_ref, f32[1,128]{1,0:T(1,128)S(1)} %get-tuple-element.25.noise_ref, ...), custom_call_target="tpu_custom_call" | custom-call | flops 20000000000 | bytes 1000 | tf_op jit(solution)/shard_map/shift/pallas_call | solution.py:250
  12.4 0.0 collective-permute-done.4.r3
  12.4 0.8 %collective-permute-done.3.r2 = bf16[37,4,256]{2,1,0:T(4,128)(2,1)S(1)} collective-permute-done((bf16[37,4,256]{2,1,0:T(4,128)(2,1)S(1)}, bf16[37,4,256]{2,1,0:T(4,128)(2,1)S(1)}, u32[]{:S(2)}, u32[]{:S(2)}) %collective-permute-start.3) | collective-permute-done | bytes 75808 | tf_op jit(solution)/shard_map/ppermute | solution.py:500
  13.2 1.0 %collective-permute-done.2.r1 = bf16[37,4,256]{2,1,0:T(4,128)(2,1)S(1)} collective-permute-done((bf16[37,4,256]{2,1,0:T(4,128)(2,1)S(1)}, bf16[37,4,256]{2,1,0:T(4,128)(2,1)S(1)}, u32[]{:S(2)}, u32[]{:S(2)}) %collective-permute-start.2) | collective-permute-done | bytes 75808 | tf_op jit(solution)/shard_map/ppermute | solution.py:500
  14.2 0.0 collective-permute-done.1.i13
  14.2 2.6 %score.1 = (f32[576,128]{1,0:T(8,128)S(1)}, f32[32,2,128]{2,1,0:T(2,128)S(1)}, bf16[2304,256]{1,0:T(8,128)(2,1)S(1)}, f32[128,256]{1,0:T(8,128)S(1)}) custom-call(s32[1]{0:T(128)} %bitcast.own_ref, bf16[37,8,256]{2,1,0:T(8,128)(2,1)S(1)} %get-tuple-element.23.near.i0, bf16[37,8,256]{2,1,0:T(8,128)(2,1)S(1)} %collective-permute-done.far.i2, ...), custom_call_target="tpu_custom_call" | custom-call | tf_op jit(solution)/shard_map/score/pallas_call | solution.py:353
  16.8 13.2 %all_to_all.5.all_ref = f32[32,2,128]{2,1,0:T(2,128)S(1)} all-to-all(f32[32,2,128]{2,1,0:T(2,128)S(1)} %get-tuple-element.30.pair_ref), channel_id=1, replica_groups={{0,1,2,3,4,5,6,7,8,9,10,11,12,13,14,15,16,17,18,19,20,21,22,23,24,25,26..., dimensions={0} | all-to-all | bytes 65536 | tf_op jit(solution)/shard_map/all_to_all | solution.py:535
  30.0 2.1 %insert.1 = (f32[38,4,256]{2,1,0:T(4,128)S(1)}, bf16[38,4,256]{2,1,0:T(4,128)(2,1)S(1)}, bf16[38,4,256]{2,1,0:T(4,128)(2,1)S(1)}, bf16[38,4,256]{2,1,0:T(4,128)(2,1)S(1)}, f32[8,128]{1,0:T(8,128)S(1)}) custom-call(s32[1]{0:T(128)} %bitcast.own_ref, f32[576,128]{1,0:T(8,128)S(1)} %get-tuple-element.29.exp_ref, f32[32,2,128]{2,1,0:T(2,128)S(1)} %get-tuple-element.30.pair_ref, ...), custom_call_target="tpu_custom_call" | custom-call | tf_op jit(solution)/shard_map/insert/pallas_call | solution.py:432
  32.1 0.6 %collective-permute-start.5 = (bf16[38,4,256]{2,1,0:T(4,128)(2,1)S(1)}, bf16[38,4,256]{2,1,0:T(4,128)(2,1)S(1)}, u32[]{:S(2)}, u32[]{:S(2)}) collective-permute-start(bf16[38,4,256]{2,1,0:T(4,128)(2,1)S(1)} %get-tuple-element.35), channel_id=1, source_target_pairs={{0,32},{8,40},{16,48},{24,56},{32,64},{40,72},{48,80},{56,88},{64,... | collective-permute-start | bytes 233480 | tf_op jit(solution)/shard_map/ppermute | solution.py:500
  32.6 3.5 %collective-permute-start.6 = (bf16[38,4,256]{2,1,0:T(4,128)(2,1)S(1)}, bf16[38,4,256]{2,1,0:T(4,128)(2,1)S(1)}, u32[]{:S(2)}, u32[]{:S(2)}) collective-permute-start(bf16[38,4,256]{2,1,0:T(4,128)(2,1)S(1)} %get-tuple-element.36), channel_id=1, source_target_pairs={{0,64},{8,72},{16,80},{24,88},{32,96},{40,104},{48,112},{56,120},{... | collective-permute-start | bytes 233480 | tf_op jit(solution)/shard_map/ppermute | solution.py:500
  36.1 0.7 %collective-permute-start.7 = (bf16[38,4,256]{2,1,0:T(4,128)(2,1)S(1)}, bf16[38,4,256]{2,1,0:T(4,128)(2,1)S(1)}, u32[]{:S(2)}, u32[]{:S(2)}) collective-permute-start(bf16[38,4,256]{2,1,0:T(4,128)(2,1)S(1)} %get-tuple-element.37), channel_id=1, source_target_pairs={{0,96},{8,104},{16,112},{24,120},{32,0},{40,8},{48,16},{56,24},{64... | collective-permute-start | bytes 233480 | tf_op jit(solution)/shard_map/ppermute | solution.py:500
  36.9 0.9 %collective-permute-done.5.g1 = bf16[38,4,256]{2,1,0:T(4,128)(2,1)S(1)} collective-permute-done((bf16[38,4,256]{2,1,0:T(4,128)(2,1)S(1)}, bf16[38,4,256]{2,1,0:T(4,128)(2,1)S(1)}, u32[]{:S(2)}, u32[]{:S(2)}) %collective-permute-start.5) | collective-permute-done | bytes 77856 | tf_op jit(solution)/shard_map/ppermute | solution.py:500
  37.7 2.4 %collective-permute-done.6.g2 = bf16[38,4,256]{2,1,0:T(4,128)(2,1)S(1)} collective-permute-done((bf16[38,4,256]{2,1,0:T(4,128)(2,1)S(1)}, bf16[38,4,256]{2,1,0:T(4,128)(2,1)S(1)}, u32[]{:S(2)}, u32[]{:S(2)}) %collective-permute-start.6) | collective-permute-done | bytes 77856 | tf_op jit(solution)/shard_map/ppermute | solution.py:500
  40.2 0.4 collective-permute-done.7.g3
  40.5 1.2 %finish.1 = (f32[4,9216]{1,0:T(4,128)}, f32[1,4]{1,0:T(1,128)}, f32[1,8]{1,0:T(1,128)}) custom-call(f32[38,4,256]{2,1,0:T(4,128)S(1)} %get-tuple-element.34.own_ref, bf16[38,4,256]{2,1,0:T(4,128)(2,1)S(1)} %collective-permute-done.5.g1, bf16[38,4,256]{2,1,0:T(4,128)(2,1)S(1)} %collective-permute-done.6.g2, ...), custom_call_target="tpu_custom_call" | custom-call | tf_op jit(solution)/shard_map/finish/pallas_call | solution.py:480
  (1 shorter events, 0.0 us)
Async XLA Ops:
  2.4 8.8 %collective-permute-start = (bf16[37,8,256]{2,1,0:T(8,128)(2,1)S(1)}, bf16[37,8,256]{2,1,0:T(8,128)(2,1)S(1)}, u32[]{:S(2)}, u32[]{:S(2)}) collective-permute-start(bf16[37,8,256]{2,1,0:T(8,128)(2,1)S(1)} %get-tuple-element.23.near.i0), channel_id=1, source_target_pairs={{0,17},{1,16},{2,19},{3,18},{4,21},{5,20},{6,23},{7,22},{8,25},{9,... | collective-permute-start | bytes 454664 | tf_op jit(solution)/shard_map/ppermute | solution.py:509
  5.4 7.0 %collective-permute-start.4 = (bf16[37,4,256]{2,1,0:T(4,128)(2,1)S(1)}, bf16[37,4,256]{2,1,0:T(4,128)(2,1)S(1)}, u32[]{:S(2)}, u32[]{:S(2)}) collective-permute-start(bf16[37,4,256]{2,1,0:T(4,128)(2,1)S(1)} %get-tuple-element.28.r0), channel_id=1, source_target_pairs={{0,32},{8,40},{16,48},{24,56},{32,64},{40,72},{48,80},{56,88},{64,... | collective-permute-start | bytes 227336 | tf_op jit(solution)/shard_map/ppermute | solution.py:500
  6.9 6.3 %collective-permute-start.3 = (bf16[37,4,256]{2,1,0:T(4,128)(2,1)S(1)}, bf16[37,4,256]{2,1,0:T(4,128)(2,1)S(1)}, u32[]{:S(2)}, u32[]{:S(2)}) collective-permute-start(bf16[37,4,256]{2,1,0:T(4,128)(2,1)S(1)} %get-tuple-element.28.r0), channel_id=1, source_target_pairs={{0,64},{8,72},{16,80},{24,88},{32,96},{40,104},{48,112},{56,120},{... | collective-permute-start | bytes 227336 | tf_op jit(solution)/shard_map/ppermute | solution.py:500
  9.8 4.4 %collective-permute-start.2 = (bf16[37,4,256]{2,1,0:T(4,128)(2,1)S(1)}, bf16[37,4,256]{2,1,0:T(4,128)(2,1)S(1)}, u32[]{:S(2)}, u32[]{:S(2)}) collective-permute-start(bf16[37,4,256]{2,1,0:T(4,128)(2,1)S(1)} %get-tuple-element.28.r0), channel_id=1, source_target_pairs={{0,96},{8,104},{16,112},{24,120},{32,0},{40,8},{48,16},{56,24},{64... | collective-permute-start | bytes 227336 | tf_op jit(solution)/shard_map/ppermute | solution.py:500
  11.2 3.0 %collective-permute-start.1 = (bf16[2,37,8,256]{3,2,1,0:T(8,128)(2,1)S(1)}, bf16[2,37,8,256]{3,2,1,0:T(8,128)(2,1)S(1)}, u32[]{:S(2)}, u32[]{:S(2)}) collective-permute-start(bf16[2,37,8,256]{3,2,1,0:T(8,128)(2,1)S(1)} %pad_maximum_fusion), channel_id=1, source_target_pairs={{0,8},{1,9},{2,10},{3,11},{4,12},{5,13},{6,14},{7,15},{8,0},{9,1},... | collective-permute-start | bytes 909320 | tf_op jit(solution)/shard_map/ppermute | solution.py:509
  32.1 5.7 %collective-permute-start.5 = (bf16[38,4,256]{2,1,0:T(4,128)(2,1)S(1)}, bf16[38,4,256]{2,1,0:T(4,128)(2,1)S(1)}, u32[]{:S(2)}, u32[]{:S(2)}) collective-permute-start(bf16[38,4,256]{2,1,0:T(4,128)(2,1)S(1)} %get-tuple-element.35), channel_id=1, source_target_pairs={{0,32},{8,40},{16,48},{24,56},{32,64},{40,72},{48,80},{56,88},{64,... | collective-permute-start | bytes 233480 | tf_op jit(solution)/shard_map/ppermute | solution.py:500
  32.6 7.5 %collective-permute-start.6 = (bf16[38,4,256]{2,1,0:T(4,128)(2,1)S(1)}, bf16[38,4,256]{2,1,0:T(4,128)(2,1)S(1)}, u32[]{:S(2)}, u32[]{:S(2)}) collective-permute-start(bf16[38,4,256]{2,1,0:T(4,128)(2,1)S(1)} %get-tuple-element.36), channel_id=1, source_target_pairs={{0,64},{8,72},{16,80},{24,88},{32,96},{40,104},{48,112},{56,120},{... | collective-permute-start | bytes 233480 | tf_op jit(solution)/shard_map/ppermute | solution.py:500
  36.1 4.4 %collective-permute-start.7 = (bf16[38,4,256]{2,1,0:T(4,128)(2,1)S(1)}, bf16[38,4,256]{2,1,0:T(4,128)(2,1)S(1)}, u32[]{:S(2)}, u32[]{:S(2)}) collective-permute-start(bf16[38,4,256]{2,1,0:T(4,128)(2,1)S(1)} %get-tuple-element.37), channel_id=1, source_target_pairs={{0,96},{8,104},{16,112},{24,120},{32,0},{40,8},{48,16},{56,24},{64... | collective-permute-start | bytes 233480 | tf_op jit(solution)/shard_map/ppermute | solution.py:500

commit v8 on v7

--- a/solution.py
+++ b/solution.py
@@ -38,17 +38,17 @@
 
 def phase_parts():
     span = 2 * REACH + 1
-    theta = 2.0 * math.pi * np.arange(ANG).reshape(ROT, STEP) / ANG
+    theta = 2.0 * math.pi * np.arange(ANG).reshape(ROT, STEP)[: ROT // 2] / ANG
     radius = np.arange(CYCLES) + 1.0
-    fx = (np.cos(theta)[:, :, None] * radius).reshape(ROT, HALF)
-    fy = (np.sin(theta)[:, :, None] * radius).reshape(ROT, HALF)
+    fx = (np.cos(theta)[:, :, None] * radius).reshape(ROT // 2, HALF)
+    fy = (np.sin(theta)[:, :, None] * radius).reshape(ROT // 2, HALF)
     shift = np.arange(span) - REACH
     phi = (
         -2.0
         * math.pi
         * (shift[:, None, None, None] * fx + shift[None, :, None, None] * fy)
         / (2.0 * CYCLES)
-    ).reshape(span * span, ROT, HALF)[MIDDLE:]
+    ).reshape(span * span, ROT // 2, HALF)[MIDDLE:]
     table = np.concatenate([np.cos(phi), np.sin(phi)], axis=2).transpose(1, 0, 2)
     table = np.pad(table, ((0, 0), (0, SLOTS - table.shape[1]), (0, 0)))
     parts = []
@@ -171,7 +171,7 @@
             jax.ShapeDtypeStruct((NDEF, HALF), F32),
             jax.ShapeDtypeStruct((1, HALF), F32),
             jax.ShapeDtypeStruct((1, HALF), F32),
-            jax.ShapeDtypeStruct((ROT, 3 * SLOTS, LANES), BF16),
+            jax.ShapeDtypeStruct((ROT // 2, 3 * SLOTS, LANES), BF16),
         ),
         in_specs=[hbm] * 9,
         out_specs=(vmem,) * 6,
@@ -224,18 +224,23 @@
     sign = jnp.broadcast_to(jnp.where(pair < 0, -1.0, 1.0), (US // 2, HALF))
     contrast4 = four(contrast)
     whiten4 = four(contrast / noise)
-    for b in range(ROT):
-        turn = jnp.dot(hot, table[b], preferred_element_type=F32)
+    for half in range(ROT // 2):
+        turn = jnp.dot(hot, table[half], preferred_element_type=F32)
         cosine, sine = turn[:, :HALF], turn[:, HALF:] * sign
-        block = jnp.concatenate([near[b].astype(F32), far[b].astype(F32)], axis=0)
-        real, imag = four(block[:, :HALF]), four(block[:, HALF:])
-        shifted_real = real * cosine - imag * sine
-        shifted_imag = real * sine + imag * cosine
-        rows = slice(b * US // 2, (b + 1) * US // 2)
-        weighted[rows, :HALF] = (shifted_real * whiten4).astype(BF16)
-        weighted[rows, HALF:] = (shifted_imag * whiten4).astype(BF16)
-        inserted[rows, :HALF] = (shifted_real * contrast4).astype(BF16)
-        inserted[rows, HALF:] = (shifted_imag * contrast4).astype(BF16)
+        for b, flip in ((half, False), (half + ROT // 2, True)):
+            block = jnp.concatenate([near[b].astype(F32), far[b].astype(F32)], axis=0)
+            real, imag = four(block[:, :HALF]), four(block[:, HALF:])
+            if flip:
+                shifted_real = real * cosine + imag * sine
+                shifted_imag = imag * cosine - real * sine
+            else:
+                shifted_real = real * cosine - imag * sine
+                shifted_imag = real * sine + imag * cosine
+            rows = slice(b * US // 2, (b + 1) * US // 2)
+            weighted[rows, :HALF] = (shifted_real * whiten4).astype(BF16)
+            weighted[rows, HALF:] = (shifted_imag * whiten4).astype(BF16)
+            inserted[rows, :HALF] = (shifted_real * contrast4).astype(BF16)
+            inserted[rows, HALF:] = (shifted_imag * contrast4).astype(BF16)
 
 
 def shift_kernel(near, far, ctf_ref, noise_ref, table, weighted, inserted):
@@ -324,7 +329,8 @@
                 axis=0,
             ),
         )
-        for h in range(ROT // 2)
+        for quarter in range(ROT // 4)
+        for h in (quarter, quarter + ROT // 4)
     )
 
     peak = jnp.full((KS, US), -jnp.inf, F32)

time: 42 us -> 41.9 us (level)
  transfers between devices with their start and end apart: 8 -> 8, of which waited for: 5 -> 5; matrix products, arithmetic and copies ran while one was open for 0% -> 0% of each run, Pallas kernels for 3% -> 2%
where the time goes in v8:
time: 41.9 us; the launch traced here: 41.7 us
  starting transfers between devices  13.7 us (33%)
  blocking collectives  13.2 us (32%)
  Pallas kernels  8.57 us (20%)
  waiting for transfers between devices  5.57 us (13%)
  between operations  0.69 us (2%)
    all_to_all x1, blocking collectives, per_device(): lax.all_to_all(stats, ('img', 'cls'), 0, 0, tiled=True, axis_index_groups...  13.2 us
    ppermute x6, starting transfers between devices, along_y(): lax.ppermute(value, 'img', [(i, (i // 4 + distance) % 4 * 4 + i % 4) for...  10.7 us
    ppermute x6, waiting for transfers between devices, along_y(): lax.ppermute(value, 'img', [(i, (i // 4 + distance) % 4 * 4 + i % 4) for...  5.57 us
    ppermute x2, starting transfers between devices, beside(): return lax.ppermute(value, ('img', 'cls'), pairs)  3 us
    pallas_call x1, Pallas kernels, score(): pl.pallas_call(score_kernel, out_shape=(jax.ShapeDtypeStruct((ROWS, US),...  2.49 us
    pallas_call x1, Pallas kernels, insert(): pl.pallas_call(insert_kernel, out_shape=(jax.ShapeDtypeStruct(piece, F32)...  2.06 us
    pallas_call x1, Pallas kernels, arrange(): pl.pallas_call(arrange_kernel, out_shape=(jax.ShapeDtypeStruct((ROT + 1,...  1.81 us
    pallas_call x1, Pallas kernels, finish(): pl.pallas_call(finish_kernel, out_shape=(jax.ShapeDtypeStruct((OWN, 2 * C...  1.25 us
  transfers between devices with their start and end apart: 8, of which 5 were waited for; matrix products, arithmetic and copies ran while one was open for 0% of the time, Pallas kernels for 2%

profile of v8, /device:TPU:0, one launch (start us, length us, event | category | flops | bytes accessed | tf_op | source)
XLA Modules:
  0.0 41.7 jit_solution(16759055728296930749)
XLA Ops:
  0.6 1.8 %arrange.1 = (bf16[37,8,256]{2,1,0:T(8,128)(2,1)S(1)}, bf16[37,4,256]{2,1,0:T(4,128)(2,1)S(1)}, f32[16,128]{1,0:T(8,128)S(1)}, f32[1,128]{1,0:T(1,128)S(1)}, f32...) custom-call(bf16[8,9216]{1,0:T(8,128)(2,1)} %img_hbm.1, bf16[4,9216]{1,0:T(4,128)(2,1)} %ref_hbm.1, ...), custom_call_target="tpu_custom_call" | custom-call | tf_op jit(solution)/shard_map/arrange/pallas_call | solution.py:166
  2.4 2.9 %collective-permute-start = (bf16[37,8,256]{2,1,0:T(8,128)(2,1)S(1)}, bf16[37,8,256]{2,1,0:T(8,128)(2,1)S(1)}, u32[]{:S(2)}, u32[]{:S(2)}) collective-permute-start(bf16[37,8,256]{2,1,0:T(8,128)(2,1)S(1)} %get-tuple-element.23.near.i0), channel_id=1, source_target_pairs={{0,17},{1,16},{2,19},{3,18},{4,21},{5,20},{6,23},{7,22},{8,25},{9,... | collective-permute-start | bytes 454664 | tf_op jit(solution)/shard_map/ppermute | solution.py:515
  5.4 1.6 %collective-permute-start.4 = (bf16[37,4,256]{2,1,0:T(4,128)(2,1)S(1)}, bf16[37,4,256]{2,1,0:T(4,128)(2,1)S(1)}, u32[]{:S(2)}, u32[]{:S(2)}) collective-permute-start(bf16[37,4,256]{2,1,0:T(4,128)(2,1)S(1)} %get-tuple-element.28.r0), channel_id=1, source_target_pairs={{0,32},{8,40},{16,48},{24,56},{32,64},{40,72},{48,80},{56,88},{64,... | collective-permute-start | bytes 227336 | tf_op jit(solution)/shard_map/ppermute | solution.py:506
  6.9 2.9 %collective-permute-start.3 = (bf16[37,4,256]{2,1,0:T(4,128)(2,1)S(1)}, bf16[37,4,256]{2,1,0:T(4,128)(2,1)S(1)}, u32[]{:S(2)}, u32[]{:S(2)}) collective-permute-start(bf16[37,4,256]{2,1,0:T(4,128)(2,1)S(1)} %get-tuple-element.28.r0), channel_id=1, source_target_pairs={{0,64},{8,72},{16,80},{24,88},{32,96},{40,104},{48,112},{56,120},{... | collective-permute-start | bytes 227336 | tf_op jit(solution)/shard_map/ppermute | solution.py:506
  9.8 1.3 %collective-permute-start.2 = (bf16[37,4,256]{2,1,0:T(4,128)(2,1)S(1)}, bf16[37,4,256]{2,1,0:T(4,128)(2,1)S(1)}, u32[]{:S(2)}, u32[]{:S(2)}) collective-permute-start(bf16[37,4,256]{2,1,0:T(4,128)(2,1)S(1)} %get-tuple-element.28.r0), channel_id=1, source_target_pairs={{0,96},{8,104},{16,112},{24,120},{32,0},{40,8},{48,16},{56,24},{64... | collective-permute-start | bytes 227336 | tf_op jit(solution)/shard_map/ppermute | solution.py:506
  11.2 0.0 collective-permute-done.far.i2
  11.2 0.1 collective-permute-start.1
  11.3 1.0 %shift.1 = (bf16[2304,256]{1,0:T(8,128)(2,1)S(1)}, bf16[2304,256]{1,0:T(8,128)(2,1)S(1)}) custom-call(bf16[37,8,256]{2,1,0:T(8,128)(2,1)S(1)} %get-tuple-element.23.near.i0, bf16[37,8,256]{2,1,0:T(8,128)(2,1)S(1)} %collective-permute-done.far.i2, f32[16,128]{1,0:T(8,128)S(1)} %get-tuple-element.24.ctf_ref, f32[1,128]{1,0:T(1,128)S(1)} %get-tuple-element.25.noise_ref, ...), custom_call_target="tpu_custom_call" | custom-call | flops 20000000000 | bytes 1000 | tf_op jit(solution)/shard_map/shift/pallas_call | solution.py:255
  12.3 0.0 collective-permute-done.4.r3
  12.3 0.9 %collective-permute-done.3.r2 = bf16[37,4,256]{2,1,0:T(4,128)(2,1)S(1)} collective-permute-done((bf16[37,4,256]{2,1,0:T(4,128)(2,1)S(1)}, bf16[37,4,256]{2,1,0:T(4,128)(2,1)S(1)}, u32[]{:S(2)}, u32[]{:S(2)}) %collective-permute-start.3) | collective-permute-done | bytes 75808 | tf_op jit(solution)/shard_map/ppermute | solution.py:506
  13.2 1.0 %collective-permute-done.2.r1 = bf16[37,4,256]{2,1,0:T(4,128)(2,1)S(1)} collective-permute-done((bf16[37,4,256]{2,1,0:T(4,128)(2,1)S(1)}, bf16[37,4,256]{2,1,0:T(4,128)(2,1)S(1)}, u32[]{:S(2)}, u32[]{:S(2)}) %collective-permute-start.2) | collective-permute-done | bytes 75808 | tf_op jit(solution)/shard_map/ppermute | solution.py:506
  14.2 0.0 collective-permute-done.1.i13
  14.2 2.5 %score.1 = (f32[576,128]{1,0:T(8,128)S(1)}, f32[32,2,128]{2,1,0:T(2,128)S(1)}, bf16[2304,256]{1,0:T(8,128)(2,1)S(1)}, f32[128,256]{1,0:T(8,128)S(1)}) custom-call(s32[1]{0:T(128)} %bitcast.own_ref, bf16[37,8,256]{2,1,0:T(8,128)(2,1)S(1)} %get-tuple-element.23.near.i0, bf16[37,8,256]{2,1,0:T(8,128)(2,1)S(1)} %collective-permute-done.far.i2, ...), custom_call_target="tpu_custom_call" | custom-call | tf_op jit(solution)/shard_map/score/pallas_call | solution.py:359
  16.7 13.2 %all_to_all.5.all_ref = f32[32,2,128]{2,1,0:T(2,128)S(1)} all-to-all(f32[32,2,128]{2,1,0:T(2,128)S(1)} %get-tuple-element.30.pair_ref), channel_id=1, replica_groups={{0,1,2,3,4,5,6,7,8,9,10,11,12,13,14,15,16,17,18,19,20,21,22,23,24,25,26..., dimensions={0} | all-to-all | bytes 65536 | tf_op jit(solution)/shard_map/all_to_all | solution.py:541
  29.9 2.1 %insert.1 = (f32[38,4,256]{2,1,0:T(4,128)S(1)}, bf16[38,4,256]{2,1,0:T(4,128)(2,1)S(1)}, bf16[38,4,256]{2,1,0:T(4,128)(2,1)S(1)}, bf16[38,4,256]{2,1,0:T(4,128)(2,1)S(1)}, f32[8,128]{1,0:T(8,128)S(1)}) custom-call(s32[1]{0:T(128)} %bitcast.own_ref, f32[576,128]{1,0:T(8,128)S(1)} %get-tuple-element.29.exp_ref, f32[32,2,128]{2,1,0:T(2,128)S(1)} %get-tuple-element.30.pair_ref, ...), custom_call_target="tpu_custom_call" | custom-call | tf_op jit(solution)/shard_map/insert/pallas_call | solution.py:438
  32.0 0.6 %collective-permute-start.5 = (bf16[38,4,256]{2,1,0:T(4,128)(2,1)S(1)}, bf16[38,4,256]{2,1,0:T(4,128)(2,1)S(1)}, u32[]{:S(2)}, u32[]{:S(2)}) collective-permute-start(bf16[38,4,256]{2,1,0:T(4,128)(2,1)S(1)} %get-tuple-element.35), channel_id=1, source_target_pairs={{0,32},{8,40},{16,48},{24,56},{32,64},{40,72},{48,80},{56,88},{64,... | collective-permute-start | bytes 233480 | tf_op jit(solution)/shard_map/ppermute | solution.py:506
  32.5 3.5 %collective-permute-start.6 = (bf16[38,4,256]{2,1,0:T(4,128)(2,1)S(1)}, bf16[38,4,256]{2,1,0:T(4,128)(2,1)S(1)}, u32[]{:S(2)}, u32[]{:S(2)}) collective-permute-start(bf16[38,4,256]{2,1,0:T(4,128)(2,1)S(1)} %get-tuple-element.36), channel_id=1, source_target_pairs={{0,64},{8,72},{16,80},{24,88},{32,96},{40,104},{48,112},{56,120},{... | collective-permute-start | bytes 233480 | tf_op jit(solution)/shard_map/ppermute | solution.py:506
  36.1 0.7 %collective-permute-start.7 = (bf16[38,4,256]{2,1,0:T(4,128)(2,1)S(1)}, bf16[38,4,256]{2,1,0:T(4,128)(2,1)S(1)}, u32[]{:S(2)}, u32[]{:S(2)}) collective-permute-start(bf16[38,4,256]{2,1,0:T(4,128)(2,1)S(1)} %get-tuple-element.37), channel_id=1, source_target_pairs={{0,96},{8,104},{16,112},{24,120},{32,0},{40,8},{48,16},{56,24},{64... | collective-permute-start | bytes 233480 | tf_op jit(solution)/shard_map/ppermute | solution.py:506
  36.8 0.9 %collective-permute-done.5.g1 = bf16[38,4,256]{2,1,0:T(4,128)(2,1)S(1)} collective-permute-done((bf16[38,4,256]{2,1,0:T(4,128)(2,1)S(1)}, bf16[38,4,256]{2,1,0:T(4,128)(2,1)S(1)}, u32[]{:S(2)}, u32[]{:S(2)}) %collective-permute-start.5) | collective-permute-done | bytes 77856 | tf_op jit(solution)/shard_map/ppermute | solution.py:506
  37.6 2.4 %collective-permute-done.6.g2 = bf16[38,4,256]{2,1,0:T(4,128)(2,1)S(1)} collective-permute-done((bf16[38,4,256]{2,1,0:T(4,128)(2,1)S(1)}, bf16[38,4,256]{2,1,0:T(4,128)(2,1)S(1)}, u32[]{:S(2)}, u32[]{:S(2)}) %collective-permute-start.6) | collective-permute-done | bytes 77856 | tf_op jit(solution)/shard_map/ppermute | solution.py:506
  40.1 0.4 collective-permute-done.7.g3
  40.4 1.2 %finish.1 = (f32[4,9216]{1,0:T(4,128)}, f32[1,4]{1,0:T(1,128)}, f32[1,8]{1,0:T(1,128)}) custom-call(f32[38,4,256]{2,1,0:T(4,128)S(1)} %get-tuple-element.34.own_ref, bf16[38,4,256]{2,1,0:T(4,128)(2,1)S(1)} %collective-permute-done.5.g1, bf16[38,4,256]{2,1,0:T(4,128)(2,1)S(1)} %collective-permute-done.6.g2, ...), custom_call_target="tpu_custom_call" | custom-call | tf_op jit(solution)/shard_map/finish/pallas_call | solution.py:486
  (1 shorter events, 0.0 us)
Async XLA Ops:
  2.4 8.8 %collective-permute-start = (bf16[37,8,256]{2,1,0:T(8,128)(2,1)S(1)}, bf16[37,8,256]{2,1,0:T(8,128)(2,1)S(1)}, u32[]{:S(2)}, u32[]{:S(2)}) collective-permute-start(bf16[37,8,256]{2,1,0:T(8,128)(2,1)S(1)} %get-tuple-element.23.near.i0), channel_id=1, source_target_pairs={{0,17},{1,16},{2,19},{3,18},{4,21},{5,20},{6,23},{7,22},{8,25},{9,... | collective-permute-start | bytes 454664 | tf_op jit(solution)/shard_map/ppermute | solution.py:515
  5.4 6.9 %collective-permute-start.4 = (bf16[37,4,256]{2,1,0:T(4,128)(2,1)S(1)}, bf16[37,4,256]{2,1,0:T(4,128)(2,1)S(1)}, u32[]{:S(2)}, u32[]{:S(2)}) collective-permute-start(bf16[37,4,256]{2,1,0:T(4,128)(2,1)S(1)} %get-tuple-element.28.r0), channel_id=1, source_target_pairs={{0,32},{8,40},{16,48},{24,56},{32,64},{40,72},{48,80},{56,88},{64,... | collective-permute-start | bytes 227336 | tf_op jit(solution)/shard_map/ppermute | solution.py:506
  6.9 6.3 %collective-permute-start.3 = (bf16[37,4,256]{2,1,0:T(4,128)(2,1)S(1)}, bf16[37,4,256]{2,1,0:T(4,128)(2,1)S(1)}, u32[]{:S(2)}, u32[]{:S(2)}) collective-permute-start(bf16[37,4,256]{2,1,0:T(4,128)(2,1)S(1)} %get-tuple-element.28.r0), channel_id=1, source_target_pairs={{0,64},{8,72},{16,80},{24,88},{32,96},{40,104},{48,112},{56,120},{... | collective-permute-start | bytes 227336 | tf_op jit(solution)/shard_map/ppermute | solution.py:506
  9.8 4.4 %collective-permute-start.2 = (bf16[37,4,256]{2,1,0:T(4,128)(2,1)S(1)}, bf16[37,4,256]{2,1,0:T(4,128)(2,1)S(1)}, u32[]{:S(2)}, u32[]{:S(2)}) collective-permute-start(bf16[37,4,256]{2,1,0:T(4,128)(2,1)S(1)} %get-tuple-element.28.r0), channel_id=1, source_target_pairs={{0,96},{8,104},{16,112},{24,120},{32,0},{40,8},{48,16},{56,24},{64... | collective-permute-start | bytes 227336 | tf_op jit(solution)/shard_map/ppermute | solution.py:506
  11.2 3.0 %collective-permute-start.1 = (bf16[2,37,8,256]{3,2,1,0:T(8,128)(2,1)S(1)}, bf16[2,37,8,256]{3,2,1,0:T(8,128)(2,1)S(1)}, u32[]{:S(2)}, u32[]{:S(2)}) collective-permute-start(bf16[2,37,8,256]{3,2,1,0:T(8,128)(2,1)S(1)} %pad_maximum_fusion), channel_id=1, source_target_pairs={{0,8},{1,9},{2,10},{3,11},{4,12},{5,13},{6,14},{7,15},{8,0},{9,1},... | collective-permute-start | bytes 909320 | tf_op jit(solution)/shard_map/ppermute | solution.py:515
  32.0 5.7 %collective-permute-start.5 = (bf16[38,4,256]{2,1,0:T(4,128)(2,1)S(1)}, bf16[38,4,256]{2,1,0:T(4,128)(2,1)S(1)}, u32[]{:S(2)}, u32[]{:S(2)}) collective-permute-start(bf16[38,4,256]{2,1,0:T(4,128)(2,1)S(1)} %get-tuple-element.35), channel_id=1, source_target_pairs={{0,32},{8,40},{16,48},{24,56},{32,64},{40,72},{48,80},{56,88},{64,... | collective-permute-start | bytes 233480 | tf_op jit(solution)/shard_map/ppermute | solution.py:506
  32.5 7.5 %collective-permute-start.6 = (bf16[38,4,256]{2,1,0:T(4,128)(2,1)S(1)}, bf16[38,4,256]{2,1,0:T(4,128)(2,1)S(1)}, u32[]{:S(2)}, u32[]{:S(2)}) collective-permute-start(bf16[38,4,256]{2,1,0:T(4,128)(2,1)S(1)} %get-tuple-element.36), channel_id=1, source_target_pairs={{0,64},{8,72},{16,80},{24,88},{32,96},{40,104},{48,112},{56,120},{... | collective-permute-start | bytes 233480 | tf_op jit(solution)/shard_map/ppermute | solution.py:506
  36.1 4.4 %collective-permute-start.7 = (bf16[38,4,256]{2,1,0:T(4,128)(2,1)S(1)}, bf16[38,4,256]{2,1,0:T(4,128)(2,1)S(1)}, u32[]{:S(2)}, u32[]{:S(2)}) collective-permute-start(bf16[38,4,256]{2,1,0:T(4,128)(2,1)S(1)} %get-tuple-element.37), channel_id=1, source_target_pairs={{0,96},{8,104},{16,112},{24,120},{32,0},{40,8},{48,16},{56,24},{64... | collective-permute-start | bytes 233480 | tf_op jit(solution)/shard_map/ppermute | solution.py:506

commit v9 on v8

--- a/solution.py
+++ b/solution.py
@@ -144,6 +144,7 @@
     for copy in copies[:-1]:
         copy.wait()
     turn_major(ref_ref, OWN, cut, flat, ref_out)
+    turn_major(img_ref, MINE, cut2, flat2, img_out)
     lane = lax.broadcasted_iota(jnp.int32, (MINE, LANES), 1)
     extra = jnp.where(lane == 8, as_column(def_ref[...].astype(F32), MINE), 0.0)
     for t in range(TRANS):
@@ -155,7 +156,6 @@
     ref_out[ROT] = jnp.broadcast_to(column, (OWN, LANES)).astype(BF16)
     for small, out in ((ctf_ref, ctf_out), (noise_ref, noise_out), (tau_ref, tau_out)):
         out[...] = jnp.concatenate([small[...]] * STEP, axis=1)
-    turn_major(img_ref, MINE, cut2, flat2, img_out)
     copies[-1].wait()
 
 
@@ -286,7 +286,7 @@
 def score_kernel(
     own_ref, i0, i2, i13, w_near, r0, r1, r2, r3, ctf_ref, noise_ref, table,
     exp_out, stat_out, ins_out, sq_out,
-    w_far, back, acc,
+    w_far, back,
 ):
     own = own_ref[0]
     square = jnp.zeros((KS, LANES), F32)
@@ -317,7 +317,7 @@
 
     shift_half(i1, i3, dx1, dy1, far_contrast, noise, table, w_far, ins_out)
     half = US // 2
-    acc[...] = sum(
+    cross = sum(
         nt(
             back[(ROT - 2 * h) * KS : (2 * ROT - 2 * h) * KS, :],
             jnp.concatenate(
@@ -336,7 +336,7 @@
     peak = jnp.full((KS, US), -jnp.inf, F32)
     for r in range(ROT):
         last = (r - 1) % ROT
-        logp = acc[r * KS : (r + 1) * KS, :HALF] + acc[last * KS : (last + 1) * KS, HALF:] + base
+        logp = cross[r * KS : (r + 1) * KS, :HALF] + cross[last * KS : (last + 1) * KS, HALF:] + base
         exp_out[r * KS : (r + 1) * KS, :] = logp
         peak = jnp.maximum(peak, logp)
     peak = jnp.broadcast_to(jnp.max(peak, axis=0, keepdims=True), (8, US))
@@ -369,7 +369,6 @@
         scratch_shapes=[
             pltpu.VMEM((ROT * US // 2, LANES), BF16),
             pltpu.VMEM((2 * ROWS, LANES), BF16),
-            pltpu.VMEM((ROWS, LANES), F32),
         ],
         compiler_params=pltpu.CompilerParams(vmem_limit_bytes=VMEM_LIMIT),
         name="score",
@@ -378,7 +377,7 @@
 
 def insert_kernel(
     own_ref, exp_ref, pair_ref, all_ref, near_ref, far_ref, sq_ref,
-    own_out, s1, s2, s3, like_out, post, acc,
+    own_out, s1, s2, s3, like_out, post,
 ):
     own = own_ref[0]
     peaks = jnp.concatenate([all_ref[j, 0:1, :] for j in range(32)], axis=0)
@@ -401,7 +400,7 @@
                 post[again * KS : (again + 1) * KS, side * HALF : (side + 1) * HALF] = value
 
     half = US // 2
-    acc[...] = sum(
+    numer = sum(
         jnp.dot(
             post[(ROT - 2 * h) * KS : (2 * ROT - 2 * h) * KS, :],
             jnp.concatenate(
@@ -418,7 +417,7 @@
     )
     sums = jnp.dot(count, sq_ref[...], precision=HIGHEST, preferred_element_type=F32)
     for b in range(ROT):
-        block = acc[b * KS : (b + 1) * KS, :]
+        block = numer[b * KS : (b + 1) * KS, :]
         own_out[b] = block[:OWN]
         for d, out in ((1, s1), (2, s2), (3, s3)):
             out[b] = block[d * OWN : (d + 1) * OWN].astype(BF16)
@@ -448,7 +447,6 @@
         out_specs=(vmem,) * 5,
         scratch_shapes=[
             pltpu.VMEM((2 * ROWS, LANES), BF16),
-            pltpu.VMEM((ROWS, LANES), F32),
         ],
         compiler_params=pltpu.CompilerParams(vmem_limit_bytes=VMEM_LIMIT),
         name="insert",

time: 41.9 us -> 41.9 us (level)
  no operation moved by 1% of the time
where the time goes in v9:
time: 41.9 us; the launch traced here: 41.7 us
  starting transfers between devices  13.7 us (33%)
  blocking collectives  13.2 us (32%)
  Pallas kernels  8.57 us (20%)
  waiting for transfers between devices  5.57 us (13%)
  between operations  0.69 us (2%)
    all_to_all x1, blocking collectives, per_device(): lax.all_to_all(stats, ('img', 'cls'), 0, 0, tiled=True, axis_index_groups...  13.2 us
    ppermute x6, starting transfers between devices, along_y(): lax.ppermute(value, 'img', [(i, (i // 4 + distance) % 4 * 4 + i % 4) for...  10.7 us
    ppermute x6, waiting for transfers between devices, along_y(): lax.ppermute(value, 'img', [(i, (i // 4 + distance) % 4 * 4 + i % 4) for...  5.57 us
    ppermute x2, starting transfers between devices, beside(): return lax.ppermute(value, ('img', 'cls'), pairs)  3 us
    pallas_call x1, Pallas kernels, score(): pl.pallas_call(score_kernel, out_shape=(jax.ShapeDtypeStruct((ROWS, US),...  2.49 us
    pallas_call x1, Pallas kernels, insert(): pl.pallas_call(insert_kernel, out_shape=(jax.ShapeDtypeStruct(piece, F32)...  2.06 us
    pallas_call x1, Pallas kernels, arrange(): pl.pallas_call(arrange_kernel, out_shape=(jax.ShapeDtypeStruct((ROT + 1,...  1.81 us
    pallas_call x1, Pallas kernels, finish(): pl.pallas_call(finish_kernel, out_shape=(jax.ShapeDtypeStruct((OWN, 2 * C...  1.25 us
  transfers between devices with their start and end apart: 8, of which 5 were waited for; matrix products, arithmetic and copies ran while one was open for 0% of the time, Pallas kernels for 2%

profile of v9, /device:TPU:0, one launch (start us, length us, event | category | flops | bytes accessed | tf_op | source)
XLA Modules:
  0.0 41.7 jit_solution(16759055728296930749)
XLA Ops:
  0.6 1.8 %arrange.1 = (bf16[37,8,256]{2,1,0:T(8,128)(2,1)S(1)}, bf16[37,4,256]{2,1,0:T(4,128)(2,1)S(1)}, f32[16,128]{1,0:T(8,128)S(1)}, f32[1,128]{1,0:T(1,128)S(1)}, f32...) custom-call(bf16[8,9216]{1,0:T(8,128)(2,1)} %img_hbm.1, bf16[4,9216]{1,0:T(4,128)(2,1)} %ref_hbm.1, ...), custom_call_target="tpu_custom_call" | custom-call | tf_op jit(solution)/shard_map/arrange/pallas_call | solution.py:166
  2.4 2.9 %collective-permute-start = (bf16[37,8,256]{2,1,0:T(8,128)(2,1)S(1)}, bf16[37,8,256]{2,1,0:T(8,128)(2,1)S(1)}, u32[]{:S(2)}, u32[]{:S(2)}) collective-permute-start(bf16[37,8,256]{2,1,0:T(8,128)(2,1)S(1)} %get-tuple-element.23.near.i0), channel_id=1, source_target_pairs={{0,17},{1,16},{2,19},{3,18},{4,21},{5,20},{6,23},{7,22},{8,25},{9,... | collective-permute-start | bytes 454664 | tf_op jit(solution)/shard_map/ppermute | solution.py:513
  5.4 1.6 %collective-permute-start.4 = (bf16[37,4,256]{2,1,0:T(4,128)(2,1)S(1)}, bf16[37,4,256]{2,1,0:T(4,128)(2,1)S(1)}, u32[]{:S(2)}, u32[]{:S(2)}) collective-permute-start(bf16[37,4,256]{2,1,0:T(4,128)(2,1)S(1)} %get-tuple-element.28.r0), channel_id=1, source_target_pairs={{0,32},{8,40},{16,48},{24,56},{32,64},{40,72},{48,80},{56,88},{64,... | collective-permute-start | bytes 227336 | tf_op jit(solution)/shard_map/ppermute | solution.py:504
  6.9 2.9 %collective-permute-start.3 = (bf16[37,4,256]{2,1,0:T(4,128)(2,1)S(1)}, bf16[37,4,256]{2,1,0:T(4,128)(2,1)S(1)}, u32[]{:S(2)}, u32[]{:S(2)}) collective-permute-start(bf16[37,4,256]{2,1,0:T(4,128)(2,1)S(1)} %get-tuple-element.28.r0), channel_id=1, source_target_pairs={{0,64},{8,72},{16,80},{24,88},{32,96},{40,104},{48,112},{56,120},{... | collective-permute-start | bytes 227336 | tf_op jit(solution)/shard_map/ppermute | solution.py:504
  9.8 1.3 %collective-permute-start.2 = (bf16[37,4,256]{2,1,0:T(4,128)(2,1)S(1)}, bf16[37,4,256]{2,1,0:T(4,128)(2,1)S(1)}, u32[]{:S(2)}, u32[]{:S(2)}) collective-permute-start(bf16[37,4,256]{2,1,0:T(4,128)(2,1)S(1)} %get-tuple-element.28.r0), channel_id=1, source_target_pairs={{0,96},{8,104},{16,112},{24,120},{32,0},{40,8},{48,16},{56,24},{64... | collective-permute-start | bytes 227336 | tf_op jit(solution)/shard_map/ppermute | solution.py:504
  11.2 0.0 collective-permute-done.far.i2
  11.2 0.1 collective-permute-start.1
  11.3 1.0 %shift.1 = (bf16[2304,256]{1,0:T(8,128)(2,1)S(1)}, bf16[2304,256]{1,0:T(8,128)(2,1)S(1)}) custom-call(bf16[37,8,256]{2,1,0:T(8,128)(2,1)S(1)} %get-tuple-element.23.near.i0, bf16[37,8,256]{2,1,0:T(8,128)(2,1)S(1)} %collective-permute-done.far.i2, f32[16,128]{1,0:T(8,128)S(1)} %get-tuple-element.24.ctf_ref, f32[1,128]{1,0:T(1,128)S(1)} %get-tuple-element.25.noise_ref, ...), custom_call_target="tpu_custom_call" | custom-call | flops 20000000000 | bytes 1000 | tf_op jit(solution)/shard_map/shift/pallas_call | solution.py:255
  12.3 0.0 collective-permute-done.4.r3
  12.3 0.9 %collective-permute-done.3.r2 = bf16[37,4,256]{2,1,0:T(4,128)(2,1)S(1)} collective-permute-done((bf16[37,4,256]{2,1,0:T(4,128)(2,1)S(1)}, bf16[37,4,256]{2,1,0:T(4,128)(2,1)S(1)}, u32[]{:S(2)}, u32[]{:S(2)}) %collective-permute-start.3) | collective-permute-done | bytes 75808 | tf_op jit(solution)/shard_map/ppermute | solution.py:504
  13.2 1.0 %collective-permute-done.2.r1 = bf16[37,4,256]{2,1,0:T(4,128)(2,1)S(1)} collective-permute-done((bf16[37,4,256]{2,1,0:T(4,128)(2,1)S(1)}, bf16[37,4,256]{2,1,0:T(4,128)(2,1)S(1)}, u32[]{:S(2)}, u32[]{:S(2)}) %collective-permute-start.2) | collective-permute-done | bytes 75808 | tf_op jit(solution)/shard_map/ppermute | solution.py:504
  14.2 0.0 collective-permute-done.1.i13
  14.2 2.5 %score.1 = (f32[576,128]{1,0:T(8,128)S(1)}, f32[32,2,128]{2,1,0:T(2,128)S(1)}, bf16[2304,256]{1,0:T(8,128)(2,1)S(1)}, f32[128,256]{1,0:T(8,128)S(1)}) custom-call(s32[1]{0:T(128)} %bitcast.own_ref, bf16[37,8,256]{2,1,0:T(8,128)(2,1)S(1)} %get-tuple-element.23.near.i0, bf16[37,8,256]{2,1,0:T(8,128)(2,1)S(1)} %collective-permute-done.far.i2, ...), custom_call_target="tpu_custom_call" | custom-call | tf_op jit(solution)/shard_map/score/pallas_call | solution.py:359
  16.7 13.2 %all_to_all.5.all_ref = f32[32,2,128]{2,1,0:T(2,128)S(1)} all-to-all(f32[32,2,128]{2,1,0:T(2,128)S(1)} %get-tuple-element.30.pair_ref), channel_id=1, replica_groups={{0,1,2,3,4,5,6,7,8,9,10,11,12,13,14,15,16,17,18,19,20,21,22,23,24,25,26..., dimensions={0} | all-to-all | bytes 65536 | tf_op jit(solution)/shard_map/all_to_all | solution.py:539
  29.9 2.1 %insert.1 = (f32[38,4,256]{2,1,0:T(4,128)S(1)}, bf16[38,4,256]{2,1,0:T(4,128)(2,1)S(1)}, bf16[38,4,256]{2,1,0:T(4,128)(2,1)S(1)}, bf16[38,4,256]{2,1,0:T(4,128)(2,1)S(1)}, f32[8,128]{1,0:T(8,128)S(1)}) custom-call(s32[1]{0:T(128)} %bitcast.own_ref, f32[576,128]{1,0:T(8,128)S(1)} %get-tuple-element.29.exp_ref, f32[32,2,128]{2,1,0:T(2,128)S(1)} %get-tuple-element.30.pair_ref, ...), custom_call_target="tpu_custom_call" | custom-call | tf_op jit(solution)/shard_map/insert/pallas_call | solution.py:437
  32.0 0.6 %collective-permute-start.5 = (bf16[38,4,256]{2,1,0:T(4,128)(2,1)S(1)}, bf16[38,4,256]{2,1,0:T(4,128)(2,1)S(1)}, u32[]{:S(2)}, u32[]{:S(2)}) collective-permute-start(bf16[38,4,256]{2,1,0:T(4,128)(2,1)S(1)} %get-tuple-element.35), channel_id=1, source_target_pairs={{0,32},{8,40},{16,48},{24,56},{32,64},{40,72},{48,80},{56,88},{64,... | collective-permute-start | bytes 233480 | tf_op jit(solution)/shard_map/ppermute | solution.py:504
  32.5 3.5 %collective-permute-start.6 = (bf16[38,4,256]{2,1,0:T(4,128)(2,1)S(1)}, bf16[38,4,256]{2,1,0:T(4,128)(2,1)S(1)}, u32[]{:S(2)}, u32[]{:S(2)}) collective-permute-start(bf16[38,4,256]{2,1,0:T(4,128)(2,1)S(1)} %get-tuple-element.36), channel_id=1, source_target_pairs={{0,64},{8,72},{16,80},{24,88},{32,96},{40,104},{48,112},{56,120},{... | collective-permute-start | bytes 233480 | tf_op jit(solution)/shard_map/ppermute | solution.py:504
  36.1 0.7 %collective-permute-start.7 = (bf16[38,4,256]{2,1,0:T(4,128)(2,1)S(1)}, bf16[38,4,256]{2,1,0:T(4,128)(2,1)S(1)}, u32[]{:S(2)}, u32[]{:S(2)}) collective-permute-start(bf16[38,4,256]{2,1,0:T(4,128)(2,1)S(1)} %get-tuple-element.37), channel_id=1, source_target_pairs={{0,96},{8,104},{16,112},{24,120},{32,0},{40,8},{48,16},{56,24},{64... | collective-permute-start | bytes 233480 | tf_op jit(solution)/shard_map/ppermute | solution.py:504
  36.8 0.9 %collective-permute-done.5.g1 = bf16[38,4,256]{2,1,0:T(4,128)(2,1)S(1)} collective-permute-done((bf16[38,4,256]{2,1,0:T(4,128)(2,1)S(1)}, bf16[38,4,256]{2,1,0:T(4,128)(2,1)S(1)}, u32[]{:S(2)}, u32[]{:S(2)}) %collective-permute-start.5) | collective-permute-done | bytes 77856 | tf_op jit(solution)/shard_map/ppermute | solution.py:504
  37.6 2.4 %collective-permute-done.6.g2 = bf16[38,4,256]{2,1,0:T(4,128)(2,1)S(1)} collective-permute-done((bf16[38,4,256]{2,1,0:T(4,128)(2,1)S(1)}, bf16[38,4,256]{2,1,0:T(4,128)(2,1)S(1)}, u32[]{:S(2)}, u32[]{:S(2)}) %collective-permute-start.6) | collective-permute-done | bytes 77856 | tf_op jit(solution)/shard_map/ppermute | solution.py:504
  40.1 0.4 collective-permute-done.7.g3
  40.4 1.2 %finish.1 = (f32[4,9216]{1,0:T(4,128)}, f32[1,4]{1,0:T(1,128)}, f32[1,8]{1,0:T(1,128)}) custom-call(f32[38,4,256]{2,1,0:T(4,128)S(1)} %get-tuple-element.34.own_ref, bf16[38,4,256]{2,1,0:T(4,128)(2,1)S(1)} %collective-permute-done.5.g1, bf16[38,4,256]{2,1,0:T(4,128)(2,1)S(1)} %collective-permute-done.6.g2, ...), custom_call_target="tpu_custom_call" | custom-call | tf_op jit(solution)/shard_map/finish/pallas_call | solution.py:484
  (1 shorter events, 0.0 us)
Async XLA Ops:
  2.4 8.8 %collective-permute-start = (bf16[37,8,256]{2,1,0:T(8,128)(2,1)S(1)}, bf16[37,8,256]{2,1,0:T(8,128)(2,1)S(1)}, u32[]{:S(2)}, u32[]{:S(2)}) collective-permute-start(bf16[37,8,256]{2,1,0:T(8,128)(2,1)S(1)} %get-tuple-element.23.near.i0), channel_id=1, source_target_pairs={{0,17},{1,16},{2,19},{3,18},{4,21},{5,20},{6,23},{7,22},{8,25},{9,... | collective-permute-start | bytes 454664 | tf_op jit(solution)/shard_map/ppermute | solution.py:513
  5.4 6.9 %collective-permute-start.4 = (bf16[37,4,256]{2,1,0:T(4,128)(2,1)S(1)}, bf16[37,4,256]{2,1,0:T(4,128)(2,1)S(1)}, u32[]{:S(2)}, u32[]{:S(2)}) collective-permute-start(bf16[37,4,256]{2,1,0:T(4,128)(2,1)S(1)} %get-tuple-element.28.r0), channel_id=1, source_target_pairs={{0,32},{8,40},{16,48},{24,56},{32,64},{40,72},{48,80},{56,88},{64,... | collective-permute-start | bytes 227336 | tf_op jit(solution)/shard_map/ppermute | solution.py:504
  6.9 6.3 %collective-permute-start.3 = (bf16[37,4,256]{2,1,0:T(4,128)(2,1)S(1)}, bf16[37,4,256]{2,1,0:T(4,128)(2,1)S(1)}, u32[]{:S(2)}, u32[]{:S(2)}) collective-permute-start(bf16[37,4,256]{2,1,0:T(4,128)(2,1)S(1)} %get-tuple-element.28.r0), channel_id=1, source_target_pairs={{0,64},{8,72},{16,80},{24,88},{32,96},{40,104},{48,112},{56,120},{... | collective-permute-start | bytes 227336 | tf_op jit(solution)/shard_map/ppermute | solution.py:504
  9.8 4.4 %collective-permute-start.2 = (bf16[37,4,256]{2,1,0:T(4,128)(2,1)S(1)}, bf16[37,4,256]{2,1,0:T(4,128)(2,1)S(1)}, u32[]{:S(2)}, u32[]{:S(2)}) collective-permute-start(bf16[37,4,256]{2,1,0:T(4,128)(2,1)S(1)} %get-tuple-element.28.r0), channel_id=1, source_target_pairs={{0,96},{8,104},{16,112},{24,120},{32,0},{40,8},{48,16},{56,24},{64... | collective-permute-start | bytes 227336 | tf_op jit(solution)/shard_map/ppermute | solution.py:504
  11.2 3.0 %collective-permute-start.1 = (bf16[2,37,8,256]{3,2,1,0:T(8,128)(2,1)S(1)}, bf16[2,37,8,256]{3,2,1,0:T(8,128)(2,1)S(1)}, u32[]{:S(2)}, u32[]{:S(2)}) collective-permute-start(bf16[2,37,8,256]{3,2,1,0:T(8,128)(2,1)S(1)} %pad_maximum_fusion), channel_id=1, source_target_pairs={{0,8},{1,9},{2,10},{3,11},{4,12},{5,13},{6,14},{7,15},{8,0},{9,1},... | collective-permute-start | bytes 909320 | tf_op jit(solution)/shard_map/ppermute | solution.py:513
  32.0 5.7 %collective-permute-start.5 = (bf16[38,4,256]{2,1,0:T(4,128)(2,1)S(1)}, bf16[38,4,256]{2,1,0:T(4,128)(2,1)S(1)}, u32[]{:S(2)}, u32[]{:S(2)}) collective-permute-start(bf16[38,4,256]{2,1,0:T(4,128)(2,1)S(1)} %get-tuple-element.35), channel_id=1, source_target_pairs={{0,32},{8,40},{16,48},{24,56},{32,64},{40,72},{48,80},{56,88},{64,... | collective-permute-start | bytes 233480 | tf_op jit(solution)/shard_map/ppermute | solution.py:504
  32.5 7.5 %collective-permute-start.6 = (bf16[38,4,256]{2,1,0:T(4,128)(2,1)S(1)}, bf16[38,4,256]{2,1,0:T(4,128)(2,1)S(1)}, u32[]{:S(2)}, u32[]{:S(2)}) collective-permute-start(bf16[38,4,256]{2,1,0:T(4,128)(2,1)S(1)} %get-tuple-element.36), channel_id=1, source_target_pairs={{0,64},{8,72},{16,80},{24,88},{32,96},{40,104},{48,112},{56,120},{... | collective-permute-start | bytes 233480 | tf_op jit(solution)/shard_map/ppermute | solution.py:504
  36.1 4.4 %collective-permute-start.7 = (bf16[38,4,256]{2,1,0:T(4,128)(2,1)S(1)}, bf16[38,4,256]{2,1,0:T(4,128)(2,1)S(1)}, u32[]{:S(2)}, u32[]{:S(2)}) collective-permute-start(bf16[38,4,256]{2,1,0:T(4,128)(2,1)S(1)} %get-tuple-element.37), channel_id=1, source_target_pairs={{0,96},{8,104},{16,112},{24,120},{32,0},{40,8},{48,16},{56,24},{64... | collective-permute-start | bytes 233480 | tf_op jit(solution)/shard_map/ppermute | solution.py:504

commit v10 on v8

--- a/solution.py
+++ b/solution.py
@@ -143,7 +143,7 @@
     )
     for copy in copies[:-1]:
         copy.wait()
-    turn_major(ref_ref, OWN, cut, flat, ref_out)
+    turn_major(img_ref, MINE, cut2, flat2, img_out)
     lane = lax.broadcasted_iota(jnp.int32, (MINE, LANES), 1)
     extra = jnp.where(lane == 8, as_column(def_ref[...].astype(F32), MINE), 0.0)
     for t in range(TRANS):
@@ -155,7 +155,7 @@
     ref_out[ROT] = jnp.broadcast_to(column, (OWN, LANES)).astype(BF16)
     for small, out in ((ctf_ref, ctf_out), (noise_ref, noise_out), (tau_ref, tau_out)):
         out[...] = jnp.concatenate([small[...]] * STEP, axis=1)
-    turn_major(img_ref, MINE, cut2, flat2, img_out)
+    turn_major(ref_ref, OWN, cut, flat, ref_out)
     copies[-1].wait()
 
 

time: 41.9 us -> 41.8 us (level)
  no operation moved by 1% of the time
where the time goes in v10:
time: 41.8 us; the launch traced here: 41.7 us
  starting transfers between devices  13.7 us (33%)
  blocking collectives  13.2 us (32%)
  Pallas kernels  8.54 us (20%)
  waiting for transfers between devices  5.58 us (13%)
  between operations  0.69 us (2%)
    all_to_all x1, blocking collectives, per_device(): lax.all_to_all(stats, ('img', 'cls'), 0, 0, tiled=True, axis_index_groups...  13.2 us
    ppermute x6, starting transfers between devices, along_y(): lax.ppermute(value, 'img', [(i, (i // 4 + distance) % 4 * 4 + i % 4) for...  10.7 us
    ppermute x6, waiting for transfers between devices, along_y(): lax.ppermute(value, 'img', [(i, (i // 4 + distance) % 4 * 4 + i % 4) for...  5.57 us
    ppermute x2, starting transfers between devices, beside(): return lax.ppermute(value, ('img', 'cls'), pairs)  3.01 us
    pallas_call x1, Pallas kernels, score(): pl.pallas_call(score_kernel, out_shape=(jax.ShapeDtypeStruct((ROWS, US),...  2.49 us
    pallas_call x1, Pallas kernels, insert(): pl.pallas_call(insert_kernel, out_shape=(jax.ShapeDtypeStruct(piece, F32)...  2.06 us
    pallas_call x1, Pallas kernels, arrange(): pl.pallas_call(arrange_kernel, out_shape=(jax.ShapeDtypeStruct((ROT + 1,...  1.78 us
    pallas_call x1, Pallas kernels, finish(): pl.pallas_call(finish_kernel, out_shape=(jax.ShapeDtypeStruct((OWN, 2 * C...  1.25 us
  transfers between devices with their start and end apart: 8, of which 5 were waited for; matrix products, arithmetic and copies ran while one was open for 0% of the time, Pallas kernels for 2%

profile of v10, /device:TPU:0, one launch (start us, length us, event | category | flops | bytes accessed | tf_op | source)
XLA Modules:
  0.0 41.7 jit_solution(15761087366740687347)
XLA Ops:
  0.6 1.8 %arrange.1 = (bf16[37,8,256]{2,1,0:T(8,128)(2,1)S(1)}, bf16[37,4,256]{2,1,0:T(4,128)(2,1)S(1)}, f32[16,128]{1,0:T(8,128)S(1)}, f32[1,128]{1,0:T(1,128)S(1)}, f32...) custom-call(bf16[8,9216]{1,0:T(8,128)(2,1)} %img_hbm.1, bf16[4,9216]{1,0:T(4,128)(2,1)} %ref_hbm.1, ...), custom_call_target="tpu_custom_call" | custom-call | tf_op jit(solution)/shard_map/arrange/pallas_call | solution.py:166
  2.4 2.9 %collective-permute-start = (bf16[37,8,256]{2,1,0:T(8,128)(2,1)S(1)}, bf16[37,8,256]{2,1,0:T(8,128)(2,1)S(1)}, u32[]{:S(2)}, u32[]{:S(2)}) collective-permute-start(bf16[37,8,256]{2,1,0:T(8,128)(2,1)S(1)} %get-tuple-element.23.near.i0), channel_id=1, source_target_pairs={{0,17},{1,16},{2,19},{3,18},{4,21},{5,20},{6,23},{7,22},{8,25},{9,... | collective-permute-start | bytes 454664 | tf_op jit(solution)/shard_map/ppermute | solution.py:515
  5.3 1.6 %collective-permute-start.4 = (bf16[37,4,256]{2,1,0:T(4,128)(2,1)S(1)}, bf16[37,4,256]{2,1,0:T(4,128)(2,1)S(1)}, u32[]{:S(2)}, u32[]{:S(2)}) collective-permute-start(bf16[37,4,256]{2,1,0:T(4,128)(2,1)S(1)} %get-tuple-element.28.r0), channel_id=1, source_target_pairs={{0,32},{8,40},{16,48},{24,56},{32,64},{40,72},{48,80},{56,88},{64,... | collective-permute-start | bytes 227336 | tf_op jit(solution)/shard_map/ppermute | solution.py:506
  6.9 2.9 %collective-permute-start.3 = (bf16[37,4,256]{2,1,0:T(4,128)(2,1)S(1)}, bf16[37,4,256]{2,1,0:T(4,128)(2,1)S(1)}, u32[]{:S(2)}, u32[]{:S(2)}) collective-permute-start(bf16[37,4,256]{2,1,0:T(4,128)(2,1)S(1)} %get-tuple-element.28.r0), channel_id=1, source_target_pairs={{0,64},{8,72},{16,80},{24,88},{32,96},{40,104},{48,112},{56,120},{... | collective-permute-start | bytes 227336 | tf_op jit(solution)/shard_map/ppermute | solution.py:506
  9.8 1.3 %collective-permute-start.2 = (bf16[37,4,256]{2,1,0:T(4,128)(2,1)S(1)}, bf16[37,4,256]{2,1,0:T(4,128)(2,1)S(1)}, u32[]{:S(2)}, u32[]{:S(2)}) collective-permute-start(bf16[37,4,256]{2,1,0:T(4,128)(2,1)S(1)} %get-tuple-element.28.r0), channel_id=1, source_target_pairs={{0,96},{8,104},{16,112},{24,120},{32,0},{40,8},{48,16},{56,24},{64... | collective-permute-start | bytes 227336 | tf_op jit(solution)/shard_map/ppermute | solution.py:506
  11.2 0.0 collective-permute-done.far.i2
  11.2 0.1 collective-permute-start.1
  11.3 1.0 %shift.1 = (bf16[2304,256]{1,0:T(8,128)(2,1)S(1)}, bf16[2304,256]{1,0:T(8,128)(2,1)S(1)}) custom-call(bf16[37,8,256]{2,1,0:T(8,128)(2,1)S(1)} %get-tuple-element.23.near.i0, bf16[37,8,256]{2,1,0:T(8,128)(2,1)S(1)} %collective-permute-done.far.i2, f32[16,128]{1,0:T(8,128)S(1)} %get-tuple-element.24.ctf_ref, f32[1,128]{1,0:T(1,128)S(1)} %get-tuple-element.25.noise_ref, ...), custom_call_target="tpu_custom_call" | custom-call | flops 20000000000 | bytes 1000 | tf_op jit(solution)/shard_map/shift/pallas_call | solution.py:255
  12.3 0.0 collective-permute-done.4.r3
  12.3 0.9 %collective-permute-done.3.r2 = bf16[37,4,256]{2,1,0:T(4,128)(2,1)S(1)} collective-permute-done((bf16[37,4,256]{2,1,0:T(4,128)(2,1)S(1)}, bf16[37,4,256]{2,1,0:T(4,128)(2,1)S(1)}, u32[]{:S(2)}, u32[]{:S(2)}) %collective-permute-start.3) | collective-permute-done | bytes 75808 | tf_op jit(solution)/shard_map/ppermute | solution.py:506
  13.2 1.0 %collective-permute-done.2.r1 = bf16[37,4,256]{2,1,0:T(4,128)(2,1)S(1)} collective-permute-done((bf16[37,4,256]{2,1,0:T(4,128)(2,1)S(1)}, bf16[37,4,256]{2,1,0:T(4,128)(2,1)S(1)}, u32[]{:S(2)}, u32[]{:S(2)}) %collective-permute-start.2) | collective-permute-done | bytes 75808 | tf_op jit(solution)/shard_map/ppermute | solution.py:506
  14.2 0.0 collective-permute-done.1.i13
  14.2 2.5 %score.1 = (f32[576,128]{1,0:T(8,128)S(1)}, f32[32,2,128]{2,1,0:T(2,128)S(1)}, bf16[2304,256]{1,0:T(8,128)(2,1)S(1)}, f32[128,256]{1,0:T(8,128)S(1)}) custom-call(s32[1]{0:T(128)} %bitcast.own_ref, bf16[37,8,256]{2,1,0:T(8,128)(2,1)S(1)} %get-tuple-element.23.near.i0, bf16[37,8,256]{2,1,0:T(8,128)(2,1)S(1)} %collective-permute-done.far.i2, ...), custom_call_target="tpu_custom_call" | custom-call | tf_op jit(solution)/shard_map/score/pallas_call | solution.py:359
  16.7 13.2 %all_to_all.5.all_ref = f32[32,2,128]{2,1,0:T(2,128)S(1)} all-to-all(f32[32,2,128]{2,1,0:T(2,128)S(1)} %get-tuple-element.30.pair_ref), channel_id=1, replica_groups={{0,1,2,3,4,5,6,7,8,9,10,11,12,13,14,15,16,17,18,19,20,21,22,23,24,25,26..., dimensions={0} | all-to-all | bytes 65536 | tf_op jit(solution)/shard_map/all_to_all | solution.py:541
  29.9 2.1 %insert.1 = (f32[38,4,256]{2,1,0:T(4,128)S(1)}, bf16[38,4,256]{2,1,0:T(4,128)(2,1)S(1)}, bf16[38,4,256]{2,1,0:T(4,128)(2,1)S(1)}, bf16[38,4,256]{2,1,0:T(4,128)(2,1)S(1)}, f32[8,128]{1,0:T(8,128)S(1)}) custom-call(s32[1]{0:T(128)} %bitcast.own_ref, f32[576,128]{1,0:T(8,128)S(1)} %get-tuple-element.29.exp_ref, f32[32,2,128]{2,1,0:T(2,128)S(1)} %get-tuple-element.30.pair_ref, ...), custom_call_target="tpu_custom_call" | custom-call | tf_op jit(solution)/shard_map/insert/pallas_call | solution.py:438
  31.9 0.6 %collective-permute-start.5 = (bf16[38,4,256]{2,1,0:T(4,128)(2,1)S(1)}, bf16[38,4,256]{2,1,0:T(4,128)(2,1)S(1)}, u32[]{:S(2)}, u32[]{:S(2)}) collective-permute-start(bf16[38,4,256]{2,1,0:T(4,128)(2,1)S(1)} %get-tuple-element.35), channel_id=1, source_target_pairs={{0,32},{8,40},{16,48},{24,56},{32,64},{40,72},{48,80},{56,88},{64,... | collective-permute-start | bytes 233480 | tf_op jit(solution)/shard_map/ppermute | solution.py:506
  32.5 3.5 %collective-permute-start.6 = (bf16[38,4,256]{2,1,0:T(4,128)(2,1)S(1)}, bf16[38,4,256]{2,1,0:T(4,128)(2,1)S(1)}, u32[]{:S(2)}, u32[]{:S(2)}) collective-permute-start(bf16[38,4,256]{2,1,0:T(4,128)(2,1)S(1)} %get-tuple-element.36), channel_id=1, source_target_pairs={{0,64},{8,72},{16,80},{24,88},{32,96},{40,104},{48,112},{56,120},{... | collective-permute-start | bytes 233480 | tf_op jit(solution)/shard_map/ppermute | solution.py:506
  36.0 0.7 %collective-permute-start.7 = (bf16[38,4,256]{2,1,0:T(4,128)(2,1)S(1)}, bf16[38,4,256]{2,1,0:T(4,128)(2,1)S(1)}, u32[]{:S(2)}, u32[]{:S(2)}) collective-permute-start(bf16[38,4,256]{2,1,0:T(4,128)(2,1)S(1)} %get-tuple-element.37), channel_id=1, source_target_pairs={{0,96},{8,104},{16,112},{24,120},{32,0},{40,8},{48,16},{56,24},{64... | collective-permute-start | bytes 233480 | tf_op jit(solution)/shard_map/ppermute | solution.py:506
  36.8 0.9 %collective-permute-done.5.g1 = bf16[38,4,256]{2,1,0:T(4,128)(2,1)S(1)} collective-permute-done((bf16[38,4,256]{2,1,0:T(4,128)(2,1)S(1)}, bf16[38,4,256]{2,1,0:T(4,128)(2,1)S(1)}, u32[]{:S(2)}, u32[]{:S(2)}) %collective-permute-start.5) | collective-permute-done | bytes 77856 | tf_op jit(solution)/shard_map/ppermute | solution.py:506
  37.6 2.4 %collective-permute-done.6.g2 = bf16[38,4,256]{2,1,0:T(4,128)(2,1)S(1)} collective-permute-done((bf16[38,4,256]{2,1,0:T(4,128)(2,1)S(1)}, bf16[38,4,256]{2,1,0:T(4,128)(2,1)S(1)}, u32[]{:S(2)}, u32[]{:S(2)}) %collective-permute-start.6) | collective-permute-done | bytes 77856 | tf_op jit(solution)/shard_map/ppermute | solution.py:506
  40.0 0.4 collective-permute-done.7.g3
  40.4 1.2 %finish.1 = (f32[4,9216]{1,0:T(4,128)}, f32[1,4]{1,0:T(1,128)}, f32[1,8]{1,0:T(1,128)}) custom-call(f32[38,4,256]{2,1,0:T(4,128)S(1)} %get-tuple-element.34.own_ref, bf16[38,4,256]{2,1,0:T(4,128)(2,1)S(1)} %collective-permute-done.5.g1, bf16[38,4,256]{2,1,0:T(4,128)(2,1)S(1)} %collective-permute-done.6.g2, ...), custom_call_target="tpu_custom_call" | custom-call | tf_op jit(solution)/shard_map/finish/pallas_call | solution.py:486
  (1 shorter events, 0.0 us)
Async XLA Ops:
  2.4 8.8 %collective-permute-start = (bf16[37,8,256]{2,1,0:T(8,128)(2,1)S(1)}, bf16[37,8,256]{2,1,0:T(8,128)(2,1)S(1)}, u32[]{:S(2)}, u32[]{:S(2)}) collective-permute-start(bf16[37,8,256]{2,1,0:T(8,128)(2,1)S(1)} %get-tuple-element.23.near.i0), channel_id=1, source_target_pairs={{0,17},{1,16},{2,19},{3,18},{4,21},{5,20},{6,23},{7,22},{8,25},{9,... | collective-permute-start | bytes 454664 | tf_op jit(solution)/shard_map/ppermute | solution.py:515
  5.3 6.9 %collective-permute-start.4 = (bf16[37,4,256]{2,1,0:T(4,128)(2,1)S(1)}, bf16[37,4,256]{2,1,0:T(4,128)(2,1)S(1)}, u32[]{:S(2)}, u32[]{:S(2)}) collective-permute-start(bf16[37,4,256]{2,1,0:T(4,128)(2,1)S(1)} %get-tuple-element.28.r0), channel_id=1, source_target_pairs={{0,32},{8,40},{16,48},{24,56},{32,64},{40,72},{48,80},{56,88},{64,... | collective-permute-start | bytes 227336 | tf_op jit(solution)/shard_map/ppermute | solution.py:506
  6.9 6.3 %collective-permute-start.3 = (bf16[37,4,256]{2,1,0:T(4,128)(2,1)S(1)}, bf16[37,4,256]{2,1,0:T(4,128)(2,1)S(1)}, u32[]{:S(2)}, u32[]{:S(2)}) collective-permute-start(bf16[37,4,256]{2,1,0:T(4,128)(2,1)S(1)} %get-tuple-element.28.r0), channel_id=1, source_target_pairs={{0,64},{8,72},{16,80},{24,88},{32,96},{40,104},{48,112},{56,120},{... | collective-permute-start | bytes 227336 | tf_op jit(solution)/shard_map/ppermute | solution.py:506
  9.8 4.4 %collective-permute-start.2 = (bf16[37,4,256]{2,1,0:T(4,128)(2,1)S(1)}, bf16[37,4,256]{2,1,0:T(4,128)(2,1)S(1)}, u32[]{:S(2)}, u32[]{:S(2)}) collective-permute-start(bf16[37,4,256]{2,1,0:T(4,128)(2,1)S(1)} %get-tuple-element.28.r0), channel_id=1, source_target_pairs={{0,96},{8,104},{16,112},{24,120},{32,0},{40,8},{48,16},{56,24},{64... | collective-permute-start | bytes 227336 | tf_op jit(solution)/shard_map/ppermute | solution.py:506
  11.2 3.0 %collective-permute-start.1 = (bf16[2,37,8,256]{3,2,1,0:T(8,128)(2,1)S(1)}, bf16[2,37,8,256]{3,2,1,0:T(8,128)(2,1)S(1)}, u32[]{:S(2)}, u32[]{:S(2)}) collective-permute-start(bf16[2,37,8,256]{3,2,1,0:T(8,128)(2,1)S(1)} %pad_maximum_fusion), channel_id=1, source_target_pairs={{0,8},{1,9},{2,10},{3,11},{4,12},{5,13},{6,14},{7,15},{8,0},{9,1},... | collective-permute-start | bytes 909320 | tf_op jit(solution)/shard_map/ppermute | solution.py:515
  31.9 5.7 %collective-permute-start.5 = (bf16[38,4,256]{2,1,0:T(4,128)(2,1)S(1)}, bf16[38,4,256]{2,1,0:T(4,128)(2,1)S(1)}, u32[]{:S(2)}, u32[]{:S(2)}) collective-permute-start(bf16[38,4,256]{2,1,0:T(4,128)(2,1)S(1)} %get-tuple-element.35), channel_id=1, source_target_pairs={{0,32},{8,40},{16,48},{24,56},{32,64},{40,72},{48,80},{56,88},{64,... | collective-permute-start | bytes 233480 | tf_op jit(solution)/shard_map/ppermute | solution.py:506
  32.5 7.5 %collective-permute-start.6 = (bf16[38,4,256]{2,1,0:T(4,128)(2,1)S(1)}, bf16[38,4,256]{2,1,0:T(4,128)(2,1)S(1)}, u32[]{:S(2)}, u32[]{:S(2)}) collective-permute-start(bf16[38,4,256]{2,1,0:T(4,128)(2,1)S(1)} %get-tuple-element.36), channel_id=1, source_target_pairs={{0,64},{8,72},{16,80},{24,88},{32,96},{40,104},{48,112},{56,120},{... | collective-permute-start | bytes 233480 | tf_op jit(solution)/shard_map/ppermute | solution.py:506
  36.0 4.4 %collective-permute-start.7 = (bf16[38,4,256]{2,1,0:T(4,128)(2,1)S(1)}, bf16[38,4,256]{2,1,0:T(4,128)(2,1)S(1)}, u32[]{:S(2)}, u32[]{:S(2)}) collective-permute-start(bf16[38,4,256]{2,1,0:T(4,128)(2,1)S(1)} %get-tuple-element.37), channel_id=1, source_target_pairs={{0,96},{8,104},{16,112},{24,120},{32,0},{40,8},{48,16},{56,24},{64... | collective-permute-start | bytes 233480 | tf_op jit(solution)/shard_map/ppermute | solution.py:506
